TPU v7x, 512 devices: a whole 4x8x8 slice. The times are simulated.
512 devices in a mesh: dp: 16 (over z, core), tp: 32 (over y, x).
Axes of the slice: x: 4, y: 8, z: 8, core: 2. Of those that a mesh axis runs over, the one named last changes fastest.
Arguments:
- q_new: bfloat16 [512, 1536], P(('dp', 'tp'))
- new_key_value: bfloat16 [512, 512], P(('dp', 'tp')), may hold values from -6 to 6
- resid_dec: bfloat16 [512, 1536], P(('dp', 'tp')), may hold values from -6 to 6
- placing: int32 [512], replicated, may hold values from 0 to 511, as said below
- lengths: int32 [512], P('dp'), may hold values from 5 to 2048, as said below
- write_pos: int32 [512], P('dp'), may hold values from 4 to 2047, as said below
- k_cache: bfloat16 [512, 2, 2048, 128], P('dp', None, 'tp')
- value_cache: bfloat16 [512, 2, 2048, 128], P('dp', None, 'tp'), may hold values from -6 to 6
- w_out: bfloat16 [1536, 1536], P(None, 'tp'), may hold values from -0.15625 to 0.15625
- x_pre: bfloat16 [32256, 1536], P(('dp', 'tp')), may hold values from -6 to 6
- routes: int32 [32768, 4], P(('dp', 'tp')), may hold values from 0 to 31, all different within a row; in each aligned block of 64 rows (0 to 63, 64 to 127, ...) at most 16 rows name the same one
- route_scale: float32 [32768, 4], P(('dp', 'tp')), may hold values from 0.2 to 2
- moe_gain: float32 [1536], replicated, may hold values from 0.5 to 1.5
- w_gate: bfloat16 [32, 768, 1536], P('tp', 'dp'), may hold values from -0.15625 to 0.15625
- w_up: bfloat16 [32, 768, 1536], P('tp', 'dp'), may hold values from -0.15625 to 0.15625
- w_down: bfloat16 [32, 768, 1536], P('tp', 'dp'), may hold values from -0.21875 to 0.21875
Outputs:
- out_pre: bfloat16 [32256, 1536], P(('dp', 'tp'))
- out_dec: bfloat16 [512, 1536], P(('dp', 'tp'))
Inputs may be any that keep to these rules, and one draw needn't show every extreme that they name: Each of 0 to 511 appears once; cache row j belongs to request placing[j]. `lengths`: a cache row is either full (2048 live slots) or filled from slot 0 up; some row is full. `write_pos`: below the row's length; a row that is not full writes at its length - 1, a full row anywhere past the sink slots. `routes`: the 64 rows of one device name any one expert at most 16 times.
All inputs are finite; a program needn't handle non-finite values.
Results may differ from a plain program's by a relative error of at most 0.007.
Values may be sent and summed in bfloat16 or wider, within the bound.
No kernel may reach another device: no remote copies, remote signals or barrier semaphores. Data moves between devices by JAX's collectives and lax.ppermute only.
A program may use at most 64 MiB of HBM per device.

v0:
```python
import jax
import jax.numpy as jnp
from jax import lax
from jax.sharding import PartitionSpec as P

HIGHEST = lax.Precision.HIGHEST


def contract_rows(left_rows, unit_rows):
    return lax.dot_general(
        left_rows, unit_rows, (((1,), (1,)), ((), ())), preferred_element_type=jnp.float32
    )


def on_device(
    q_new,
    new_key_value,
    resid_dec,
    placing,
    lengths,
    write_pos,
    k_cache,
    value_cache,
    w_out,
    x_pre,
    routes,
    route_scale,
    moe_gain,
    w_gate,
    w_up,
    w_down,
):
    tp_size = lax.axis_size("tp")
    dp_group = lax.axis_index("dp")
    tp_lane = lax.axis_index("tp")
    group_reqs = k_cache.shape[0]
    kv_heads = k_cache.shape[1]
    slot_dev = k_cache.shape[2]
    head_size = k_cache.shape[3]
    query_width = q_new.shape[1]
    per_group = query_width // head_size // kv_heads
    fetched = (
        lax.all_gather(w_gate, "dp", axis=1, tiled=True),
        lax.all_gather(w_up, "dp", axis=1, tiled=True),
        lax.all_gather(w_down, "dp", axis=1, tiled=True),
    )
    all_query, all_new = (
        lax.all_gather(q_new, ("dp", "tp"), axis=0, tiled=True),
        lax.all_gather(new_key_value, ("dp", "tp"), axis=0, tiled=True),
    )
    my_rows = lax.dynamic_slice_in_dim(placing, dp_group * group_reqs, group_reqs)
    query_rows = jnp.take(all_query, my_rows, axis=0)
    fresh_rows = jnp.take(all_new, my_rows, axis=0)
    slot_ids = tp_lane * slot_dev + jnp.arange(slot_dev, dtype=jnp.int32)
    incoming_key = fresh_rows[:, : kv_heads * head_size].reshape(group_reqs, kv_heads, 1, head_size)
    incoming_value = fresh_rows[:, kv_heads * head_size :].reshape(
        group_reqs, kv_heads, 1, head_size
    )
    written = (slot_ids[None, :] == write_pos[:, None])[:, None, :, None]
    key_rows = jnp.where(written, incoming_key, k_cache)
    value_rows = jnp.where(written, incoming_value, value_cache).astype(jnp.float32)
    query_head_list = query_rows.reshape(group_reqs, kv_heads, per_group, head_size)
    scores = jnp.einsum(
        "rgqd,rgsd->rgqs", query_head_list, key_rows, preferred_element_type=jnp.float32
    ) * head_size ** (-0.5)
    is_valid = (slot_ids[None, :] < lengths[:, None])[:, None, None, :]
    masked = jnp.where(is_valid, scores, -1e30)
    local_peak = jnp.max(masked, axis=-1)
    peak = lax.pmax(local_peak, "tp")
    weights = jnp.where(is_valid, jnp.exp(masked - peak[..., None]), 0.0)
    local_total = jnp.sum(weights, axis=-1)
    local_mixed = jnp.einsum("rgqs,rgsd->rgqd", weights, value_rows, precision=HIGHEST)
    weight_total, mixed_sum = lax.psum((local_total, local_mixed), "tp")
    attention = (
        (mixed_sum / weight_total[..., None]).reshape(group_reqs, query_width).astype(jnp.bfloat16)
    )
    projected = jnp.dot(attention, w_out, preferred_element_type=jnp.float32).astype(jnp.bfloat16)
    cache_row = lax.all_to_all(projected, "tp", split_axis=0, concat_axis=1, tiled=True)
    all_proj = lax.all_gather(cache_row, ("dp", "tp"), axis=0, tiled=True)
    total_reqs = placing.shape[0]
    my_request = dp_group * tp_size + tp_lane
    where_cached = jnp.sum(
        jnp.where(placing == my_request, jnp.arange(total_reqs, dtype=jnp.int32), 0)
    )
    proj_home = lax.dynamic_slice_in_dim(all_proj, where_cached, 1, 0)
    hidden_dec = (resid_dec.astype(jnp.float32) + proj_home.astype(jnp.float32)).astype(
        jnp.bfloat16
    )
    moe_rows = jnp.concatenate([x_pre, hidden_dec], axis=0)
    rows_dev = moe_rows.shape[0]
    width = moe_rows.shape[1]
    top_count = routes.shape[1]
    experts = tp_size * w_gate.shape[0]
    capacity = min(2 * rows_dev * top_count // experts, rows_dev)
    rows_f32 = moe_rows.astype(jnp.float32)
    mean_square = jnp.mean(rows_f32 * rows_f32, axis=-1, keepdims=True)
    normed = (rows_f32 * lax.rsqrt(mean_square + 1e-06) * moe_gain).astype(jnp.bfloat16)
    route_weight = route_scale / jnp.sum(route_scale, axis=-1, keepdims=True)
    expert_ids = routes.reshape(rows_dev * top_count)
    onehot = (expert_ids[:, None] == jnp.arange(experts, dtype=jnp.int32)[None, :]).astype(
        jnp.int32
    )
    position = jnp.sum(onehot * (jnp.cumsum(onehot, axis=0) - onehot), axis=-1)
    slot_index = expert_ids * capacity + position
    slot_rows = slot_index.reshape(rows_dev, top_count)
    pick_table = jnp.any(
        slot_rows[:, :, None] == jnp.arange(experts * capacity, dtype=jnp.int32)[None, None, :],
        axis=1,
    ).astype(jnp.bfloat16)
    outgoing = jnp.einsum(
        "rc,rd->cd", pick_table, normed, preferred_element_type=jnp.float32
    ).astype(jnp.bfloat16)
    outgoing = outgoing.reshape(experts, capacity, width)
    received = lax.all_to_all(outgoing, "tp", split_axis=0, concat_axis=0, tiled=True)
    flat_rows = received.reshape(-1, received.shape[-1])
    gate = contract_rows(flat_rows, fetched[0][0])
    upper = contract_rows(flat_rows, fetched[1][0])
    active = (jnp.maximum(gate, 0.0) * upper).astype(jnp.bfloat16)
    output = jnp.dot(active, fetched[2][0], preferred_element_type=jnp.float32)
    expert_out = output.astype(jnp.bfloat16).reshape(received.shape)
    returned = lax.all_to_all(expert_out, "tp", split_axis=0, concat_axis=0, tiled=True)
    flat_back = returned.reshape(experts * capacity, width)
    picked = jnp.take(flat_back, slot_index, axis=0).reshape(rows_dev, top_count, width)
    mixture = jnp.sum(route_weight[:, :, None] * picked.astype(jnp.float32), axis=1)
    moe_out = (rows_f32 + mixture).astype(jnp.bfloat16)
    return (moe_out[: rows_dev - 1], moe_out[rows_dev - 1 :])


def solution(mesh):
    placed = (
        P(("dp", "tp"), None),
        P(("dp", "tp"), None),
        P(("dp", "tp"), None),
        P(),
        P("dp"),
        P("dp"),
        P("dp", None, "tp", None),
        P("dp", None, "tp", None),
        P(None, "tp"),
        P(("dp", "tp"), None),
        P(("dp", "tp"), None),
        P(("dp", "tp"), None),
        P(),
        P("tp", "dp", None),
        P("tp", "dp", None),
        P("tp", "dp", None),
    )
    return jax.shard_map(
        on_device,
        mesh=mesh,
        in_specs=placed,
        out_specs=(P(("dp", "tp"), None), P(("dp", "tp"), None)),
        check_vma=False,
    )
```

profile of v0, /device:TPU:4, one launch (start us, length us, event | category | flops | bytes accessed | tf_op | source)
XLA Modules:
  0.0 762.3 jit_solution(4975138523507420202)
XLA Ops:
  7.2 0.7 all-gather.15.cloned.1.call-update
  8.0 132.2 %all-gather.1 = bf16[512,1,512]{2,1,0:T(2,128)(2,1)S(1)} all-gather(bf16[1,1,512]{2,1,0:T(2,128)(2,1)} %bitcast.66), channel_id=1, replica_groups=mesh['dp'=16,'tp'=32] {'dp','tp'}, dimensions={0}, use_global_device_ids=true | all-gather | bytes 525312 | tf_op jit(solution)/shard_map/all_gather | solution.py:49
  140.2 0.1 copy.60
  140.4 0.6 gather_fusion.1
  141.3 2.3 copy.59
  143.6 0.6 gather_fusion
  144.3 0.1 gather.17
  144.4 1.1 fusion.45
  145.6 138.1 %pmax.7 = f32[32,2,6]{2,1,0:T(2,128)S(1)} all-reduce(f32[32,2,6]{2,1,0:T(2,128)S(1)} %get-tuple-element.10), channel_id=1, replica_groups=mesh['dp'=16,'tp'=32] {'tp'}, use_global_device_ids=true, to_apply=%region_1.2 | all-reduce | flops 384 | bytes 3072 | tf_op jit(solution)/shard_map/pmax | solution.py:69
  283.7 1.9 fusion.9
  285.7 0.3 fusion.23
  286.0 137.7 %psum.15 = f32[32,2,6]{2,1,0:T(2,128)S(1)} all-reduce(f32[32,2,6]{2,1,0:T(2,128)S(1)} %fusion.23), channel_id=1, replica_groups=mesh['dp'=16,'tp'=32] {'tp'}, use_global_device_ids=true, to_apply=%region_4.5 | all-reduce | flops 384 | bytes 3072 | tf_op jit(solution)/shard_map/psum | solution.py:73
  423.7 13.1 %all-reduce.2.cloned.1.call-done = f32[32,2,6,128]{3,2,1,0:T(8,128)} async-done(((f32[32,2,6,128]{3,2,1,0:T(8,128)}), f32[32,2,6,128]{3,2,1,0:T(8,128)}) %all-reduce.2.cloned.1.call-update) | async-done | bytes 196624 | tf_op jit(solution)/shard_map/psum | solution.py:73
  436.8 1.1 divide_convert_fusion
  437.9 0.1 convert_element_type.50
  438.0 0.1 fusion.8
  438.2 14.8 %all_to_all.26 = bf16[32,1,48]{2,1,0:T(2,128)(2,1)S(1)} all-to-all(bf16[32,1,48]{2,1,0:T(2,128)(2,1)S(1)} %copy.45), channel_id=1, replica_groups=mesh['dp'=16,'tp'=32] {'tp'}, dimensions={0} | all-to-all | bytes 6144 | tf_op jit(solution)/shard_map/all_to_all | solution.py:78
  453.1 0.7 reshape.210
  453.8 0.5 all-gather.11.cloned.1.call-update
  454.4 0.5 all-gather.13.cloned.1.call-update
  455.0 0.5 all-gather.9.cloned.1.call-update
  455.6 0.1 eq.64
  455.7 0.1 reshape.174
  455.9 0.6 reduce-window.6
  456.5 0.2 slice_reduce_fusion
  456.7 0.1 fusion.35
  456.8 0.1 reduce_sum.62
  457.0 0.1 fusion.18
  457.1 0.6 select_reduce_fusion
  459.7 107.4 %all-gather.17.cloned.1.call-done = bf16[512,1,1536]{2,1,0:T(2,128)(2,1)} async-done(((bf16[1,1,1536]{2,1,0:T(2,128)(2,1)}), bf16[512,1,1536]{2,1,0:T(2,128)(2,1)}) %all-gather.17.cloned.1.call-update) | async-done | bytes 1572880 | tf_op jit(solution)/shard_map/all_gather | solution.py:79
  567.1 0.7 fusion.37
  567.9 0.1 fusion.19
  568.0 1.8 convolution_convert_fusion.1
  569.8 7.1 all-to-all-start.1
  576.9 31.7 %all-gather.11.cloned.1.call-done = bf16[1,768,1536]{2,1,0:T(8,128)(2,1)} async-done(((bf16[1,48,1536]{2,1,0:T(8,128)(2,1)}), bf16[1,768,1536]{2,1,0:T(8,128)(2,1)}) %all-gather.11.cloned.1.call-update) | async-done | bytes 2359312 | tf_op jit(solution)/shard_map/all_gather | solution.py:44
  608.6 8.0 %all-to-all-done.1 = bf16[32,16,1536]{2,1,0:T(8,128)(2,1)S(1)} async-done(((bf16[32,16,1536]{2,1,0:T(8,128)(2,1)}), bf16[32,16,1536]{2,1,0:T(8,128)(2,1)S(1)}, u32[]{:S(2)}, u32[]{:S(2)}) %all-to-all-start.1) | async-done | bytes 1572896 | tf_op jit(solution)/shard_map/all_to_all | solution.py:114
  616.6 3.1 fusion.1
  619.7 32.1 %all-gather.13.cloned.1.call-done = bf16[1,768,1536]{2,1,0:T(8,128)(2,1)} async-done(((bf16[1,48,1536]{2,1,0:T(8,128)(2,1)}), bf16[1,768,1536]{2,1,0:T(8,128)(2,1)}) %all-gather.13.cloned.1.call-update) | async-done | bytes 2359312 | tf_op jit(solution)/shard_map/all_gather | solution.py:45
  651.9 43.5 %all-gather.9.cloned.1.call-done = bf16[1,768,1536]{2,1,0:T(8,128)(2,1)} async-done(((bf16[1,48,1536]{2,1,0:T(8,128)(2,1)}), bf16[1,768,1536]{2,1,0:T(8,128)(2,1)}) %all-gather.9.cloned.1.call-update) | async-done | bytes 2359312 | tf_op jit(solution)/shard_map/all_gather | solution.py:43
  695.4 6.7 convolution_convert_fusion
  702.1 10.0 %all-to-all-start.2 = ((bf16[32,16,1536]{2,1,0:T(8,128)(2,1)}), bf16[32,16,1536]{2,1,0:T(8,128)(2,1)S(1)}, u32[]{:S(2)}, u32[]{:S(2)}) async-start(bf16[32,16,1536]{2,1,0:T(8,128)(2,1)} %bitcast.10), calls=%async_computation.2 | async-start | bytes 3145728 | tf_op jit(solution)/shard_map/all_to_all | solution.py:121
  712.2 0.1 mul.81
  712.3 0.1 copy.51
  712.6 39.2 %all-to-all-done.2 = bf16[32,16,1536]{2,1,0:T(8,128)(2,1)S(1)} async-done(((bf16[32,16,1536]{2,1,0:T(8,128)(2,1)}), bf16[32,16,1536]{2,1,0:T(8,128)(2,1)S(1)}, u32[]{:S(2)}, u32[]{:S(2)}) %all-to-all-start.2) | async-done | bytes 1572896 | tf_op jit(solution)/shard_map/all_to_all | solution.py:121
  751.8 1.3 gather_fusion.2
  753.0 0.2 gather.20
  753.2 1.5 multiply_reduce_fusion
  754.8 0.7 slice.34
  (58 shorter events, 1.3 us)
Async XLA Ops:
  7.2 430.9 %copy-start = (bf16[1536,48]{0,1:T(8,128)(2,1)S(1)}, bf16[1536,48]{0,1:T(8,128)(2,1)}, u32[]{:S(2)}) copy-start(bf16[1536,48]{0,1:T(8,128)(2,1)} %param.24) | copy-start | bytes 442372
  7.2 133.2 %copy-start.7 = (s32[512]{0:T(512)S(1)}, s32[512]{0:T(512)}, u32[]{:S(2)}) copy-start(s32[512]{0:T(512)} %param.19) | copy-start | bytes 6148
  7.2 134.1 %all-gather.15.cloned.1.call-start = ((), (), s32[]{:S(2)}) async-start(), calls=%async_computation.7 | async-start | bytes 3151872 | tf_op jit(solution)/shard_map/all_gather | solution.py:48
  7.9 428.9 %all-reduce.2.cloned.1.call-start = ((), (), s32[]{:S(2)}) async-start(), calls=%async_computation.3 | async-start | bytes 524288 | tf_op jit(solution)/shard_map/psum | solution.py:73
  8.0 133.2 %copy-start.8 = (s32[32]{0:T(128)S(1)}, s32[32]{0:T(128)}, u32[]{:S(2)}) copy-start(s32[32]{0:T(128)} %param.20) | copy-start | bytes 388
  8.0 133.2 %copy-start.9 = (s32[32]{0:T(128)S(1)}, s32[32]{0:T(128)}, u32[]{:S(2)}) copy-start(s32[32]{0:T(128)} %param.21) | copy-start | bytes 388
  141.3 3.1 copy-start.10
  144.3 139.4 %copy-start.11 = (bf16[32,2,64,128]{3,2,1,0:T(8,128)(2,1)S(1)}, bf16[32,2,64,128]{3,2,1,0:T(8,128)(2,1)}, u32[]{:S(2)}) copy-start(bf16[32,2,64,128]{3,2,1,0:T(8,128)(2,1)} %param.23) | copy-start | bytes 3145732
  285.6 169.9 %copy-start.3 = (s32[64,4]{0,1:T(4,128)S(1)}, s32[64,4]{0,1:T(4,128)}, u32[]{:S(2)}) copy-start(s32[64,4]{0,1:T(4,128)} %param.26) | copy-start | bytes 3076
  285.6 281.5 %copy-start.6 = (bf16[1,1536]{1,0:T(2,128)(2,1)S(1)}, bf16[1,1536]{1,0:T(2,128)(2,1)}, u32[]{:S(2)}) copy-start(bf16[1,1536]{1,0:T(2,128)(2,1)} %param.18) | copy-start | bytes 9220
  285.6 282.2 %copy-start.1 = (bf16[63,1536]{1,0:T(8,128)(2,1)S(1)}, bf16[63,1536]{1,0:T(8,128)(2,1)}, u32[]{:S(2)}) copy-start(bf16[63,1536]{1,0:T(8,128)(2,1)} %param.25) | copy-start | bytes 580612
  285.6 282.4 %copy-start.4 = (f32[1536]{0:T(1024)S(1)}, f32[1536]{0:T(1024)}, u32[]{:S(2)}) copy-start(f32[1536]{0:T(1024)} %param.28) | copy-start | bytes 18436
  285.6 281.5 %all-gather.17.cloned.1.call-start = ((), (), s32[]{:S(2)}) async-start(), calls=%async_computation.8 | async-start | bytes 3151872 | tf_op jit(solution)/shard_map/all_gather | solution.py:79
  453.8 154.9 %all-gather.11.cloned.1.call-start = ((), (), s32[]{:S(2)}) async-start(), calls=%async_computation.5 | async-start | bytes 2506752 | tf_op jit(solution)/shard_map/all_gather | solution.py:44
  454.4 197.5 %all-gather.13.cloned.1.call-start = ((), (), s32[]{:S(2)}) async-start(), calls=%async_computation.6 | async-start | bytes 2506752 | tf_op jit(solution)/shard_map/all_gather | solution.py:45
  454.9 240.4 %all-gather.9.cloned.1.call-start = ((), (), s32[]{:S(2)}) async-start(), calls=%async_computation.4 | async-start | bytes 2506752 | tf_op jit(solution)/shard_map/all_gather | solution.py:43
  569.8 46.8 %all-to-all-start.1 = ((bf16[32,16,1536]{2,1,0:T(8,128)(2,1)}), bf16[32,16,1536]{2,1,0:T(8,128)(2,1)S(1)}, u32[]{:S(2)}, u32[]{:S(2)}) async-start(bf16[32,16,1536]{2,1,0:T(8,128)(2,1)} %bitcast.5), calls=%async_computation.1 | async-start | bytes 3145728 | tf_op jit(solution)/shard_map/all_to_all | solution.py:114
  702.1 10.3 %copy-start.5 = (f32[64,4]{0,1:T(4,128)S(1)}, f32[64,4]{0,1:T(4,128)}, u32[]{:S(2)}) copy-start(f32[64,4]{0,1:T(4,128)} %param.27) | copy-start | bytes 3076
  702.1 49.7 %all-to-all-start.2 = ((bf16[32,16,1536]{2,1,0:T(8,128)(2,1)}), bf16[32,16,1536]{2,1,0:T(8,128)(2,1)S(1)}, u32[]{:S(2)}, u32[]{:S(2)}) async-start(bf16[32,16,1536]{2,1,0:T(8,128)(2,1)} %bitcast.10), calls=%async_computation.2 | async-start | bytes 3145728 | tf_op jit(solution)/shard_map/all_to_all | solution.py:121
  754.8 0.7 copy-start.2
Sparse Core Ops, SparseCore 0:
  12.2 121.8 all-gather.14
  285.8 150.9 all-reduce.1
  453.9 113.1 all-gather.16
  569.1 39.4 all-gather.10
  610.6 41.2 all-gather.12
  653.8 41.4 all-gather.8
where the time goes:
time: 763 us; the launch traced here: 762 us
  blocking collectives  423 us (55%)
  waiting for transfers between devices  277 us (36%)
  starting transfers between devices  17.3 us (2%)
  between operations  16.4 us (2%)
  matrix products  14.7 us (2%)
  local copies, waits for them, and re-layouts  7.97 us (1%)
    pmax x1, blocking collectives, on_device(): peak = lax.pmax(local_peak, 'tp')  138 us
    psum x1, blocking collectives, on_device(): weight_total, mixed_sum = lax.psum((local_total, local_mixed), 'tp')  138 us
    all_gather x1, blocking collectives, on_device(): lax.all_gather(new_key_value, ('dp', 'tp'), axis=0, tiled=True)  132 us
    all_gather x1, waiting for transfers between devices, on_device(): all_proj = lax.all_gather(cache_row, ('dp', 'tp'), axis=0, tiled=True)  107 us
    all_gather x1, waiting for transfers between devices, on_device(): lax.all_gather(w_gate, 'dp', axis=1, tiled=True)  43.5 us
    all_to_all x1, waiting for transfers between devices, on_device(): lax.all_to_all(expert_out, 'tp', split_axis=0, concat_axis=0, tiled=True)  39.2 us
    all_gather x1, waiting for transfers between devices, on_device(): lax.all_gather(w_down, 'dp', axis=1, tiled=True)  32.1 us
    all_gather x1, waiting for transfers between devices, on_device(): lax.all_gather(w_up, 'dp', axis=1, tiled=True)  31.7 us
  transfers between devices with their start and end apart: 8, of which 7 were waited for; matrix products, arithmetic and copies ran while one was open for 1% of the time, Pallas kernels for 0%

commit v1 on v0

v1 whole, which is shorter than its diff:
```python
import jax
import jax.numpy as jnp
from jax import lax
from jax.sharding import PartitionSpec as P

HIGHEST = lax.Precision.HIGHEST
F32 = jnp.float32
BF16 = jnp.bfloat16


def contract_rows(left_rows, unit_rows):
    return lax.dot_general(
        left_rows, unit_rows, (((1,), (1,)), ((), ())), preferred_element_type=F32
    )


def swap(blocks, axis_name):
    return lax.all_to_all(blocks, axis_name, split_axis=0, concat_axis=0, tiled=True)


def spread(block, axis_name):
    members = lax.axis_size(axis_name)
    return swap(jnp.broadcast_to(block[None], (members,) + block.shape), axis_name)


def choose_rows(table, rows):
    return jnp.dot(table.astype(BF16), rows, preferred_element_type=F32).astype(BF16)


def pieces_of(x):
    high = lax.reduce_precision(x, 8, 7)
    middle = lax.reduce_precision(x - high, 8, 7)
    low = lax.reduce_precision(x - high - middle, 8, 7)
    return high.astype(BF16), middle.astype(BF16), low.astype(BF16)


def rms(rows_f32, gain):
    mean_square = jnp.mean(rows_f32 * rows_f32, axis=-1, keepdims=True)
    return (rows_f32 * lax.rsqrt(mean_square + 1e-06) * gain).astype(BF16)


def expert_units(rows, units):
    gate = contract_rows(rows, units[0])
    upper = contract_rows(rows, units[1])
    active = (jnp.maximum(gate, 0.0) * upper).astype(BF16)
    return jnp.dot(active, units[2], preferred_element_type=F32).astype(BF16)


def on_device(
    q_new,
    new_key_value,
    resid_dec,
    placing,
    lengths,
    write_pos,
    k_cache,
    value_cache,
    w_out,
    x_pre,
    routes,
    route_scale,
    moe_gain,
    w_gate,
    w_up,
    w_down,
):
    dp_size = lax.axis_size("dp")
    tp_size = lax.axis_size("tp")
    dp_group = lax.axis_index("dp")
    tp_lane = lax.axis_index("tp")
    group_reqs, kv_heads, slot_dev, head_size = k_cache.shape
    width = q_new.shape[1]
    heads = width // head_size
    per_group = heads // kv_heads
    total_reqs = placing.shape[0]
    experts = tp_size * w_gate.shape[0]
    assert group_reqs == tp_size and experts == tp_size

    units = lax.all_gather(
        jnp.concatenate([w_gate, w_up, w_down], axis=0), "dp", axis=1, tiled=True
    )

    columns = heads + 2 * kv_heads
    share = tp_size // columns
    chosen_rows = group_reqs // share
    fresh = jnp.concatenate([q_new, new_key_value], axis=1).reshape(1, columns, 1, head_size)
    by_head = swap(
        jnp.broadcast_to(fresh, (share, columns, 1, head_size)).reshape(tp_size, 1, head_size), "tp"
    )
    all_rows = spread(by_head.reshape(tp_size, head_size), "dp").reshape(total_reqs, head_size)
    first_row = dp_group * group_reqs + (tp_lane // columns) * chosen_rows
    wanted = lax.dynamic_slice_in_dim(placing, first_row, chosen_rows)
    request_ids = jnp.arange(total_reqs, dtype=jnp.int32)
    mine = choose_rows(wanted[:, None] == request_ids[None, :], all_rows)
    heads_here = spread(mine, "tp").reshape(share, columns, chosen_rows, head_size)
    cached = jnp.transpose(heads_here, (0, 2, 1, 3)).reshape(group_reqs, columns, head_size)
    query_head_list = cached[:, :heads].reshape(group_reqs, kv_heads, per_group, head_size)
    incoming_key = cached[:, heads : heads + kv_heads][:, :, None, :]
    incoming_value = cached[:, heads + kv_heads :][:, :, None, :]

    slot_ids = tp_lane * slot_dev + jnp.arange(slot_dev, dtype=jnp.int32)
    written = (slot_ids[None, :] == write_pos[:, None])[:, None, :, None]
    key_rows = jnp.where(written, incoming_key, k_cache)
    value_rows = jnp.where(written, incoming_value, value_cache).astype(F32)
    scores = jnp.einsum(
        "rgqd,rgsd->rgqs", query_head_list, key_rows, preferred_element_type=F32
    ) * head_size ** (-0.5)
    is_valid = (slot_ids[None, :] < lengths[:, None])[:, None, None, :]
    masked = jnp.where(is_valid, scores, -1e30)
    local_peak = jnp.max(masked, axis=-1)
    weights = jnp.where(is_valid, jnp.exp(masked - local_peak[..., None]), 0.0)
    local_total = jnp.sum(weights, axis=-1)
    local_mixed = jnp.einsum("rgqs,rgsd->rgqd", weights, value_rows, precision=HIGHEST)

    def lane_row(values):
        row = jnp.concatenate(pieces_of(values.reshape(group_reqs, heads)), axis=1)
        return jnp.pad(row, ((0, 0), (0, head_size - row.shape[1])))[:, None, :]

    parts = jnp.concatenate(
        [
            local_mixed.reshape(group_reqs, heads, head_size).astype(BF16),
            lane_row(local_peak),
            lane_row(local_total),
            jnp.zeros((group_reqs, 2, head_size), BF16),
        ],
        axis=1,
    )
    gathered = swap(parts, "tp")
    tail = gathered[:, heads : heads + 2, : 3 * heads].astype(F32)
    tail = tail[..., :heads] + tail[..., heads : 2 * heads] + tail[..., 2 * heads :]
    peaks, totals = tail[:, 0], tail[:, 1]
    scale = jnp.exp(peaks - jnp.max(peaks, axis=0, keepdims=True))
    total = jnp.sum(scale * totals, axis=0)
    mixed = jnp.sum(scale[:, :, None] * gathered[:, :heads].astype(F32), axis=0)
    attention_row = (mixed / total[:, None]).astype(BF16)

    attention = spread(attention_row, "tp").reshape(group_reqs, width)
    projected = jnp.dot(attention, w_out, preferred_element_type=F32).astype(BF16)
    all_projected = spread(projected, "dp").reshape(total_reqs, projected.shape[1])
    home_ids = dp_group * group_reqs + jnp.arange(group_reqs, dtype=jnp.int32)
    at_home = choose_rows(home_ids[:, None] == placing[None, :], all_projected)
    proj_home = swap(at_home[:, None, :], "tp").reshape(1, width)
    hidden_dec = (resid_dec.astype(F32) + proj_home.astype(F32)).astype(BF16)

    route_weight = route_scale / jnp.sum(route_scale, axis=-1, keepdims=True)
    expert_ids = jnp.arange(experts, dtype=jnp.int32)
    hits = routes[:, :, None] == expert_ids[None, None, :]
    weight_of = jnp.sum(jnp.where(hits, route_weight[:, :, None], 0.0), axis=1)
    pre_rows = x_pre.shape[0]
    top_count = routes.shape[1]
    capacity = min(2 * (pre_rows + 1) * top_count // experts, pre_rows + 1)

    routed = jnp.any(hits[:pre_rows], axis=1)
    row_ids = jnp.arange(pre_rows, dtype=jnp.int32)
    before = (row_ids[None, :] < row_ids[:, None]).astype(BF16)
    position = jnp.dot(before, routed.astype(BF16), preferred_element_type=F32).astype(jnp.int32)
    slot_ids_e = jnp.arange(capacity, dtype=jnp.int32)
    pick = routed[:, :, None] & (position[:, :, None] == slot_ids_e[None, None, :])
    pick_table = pick.reshape(pre_rows, experts * capacity)
    x_f32 = x_pre.astype(F32)
    normed = rms(x_f32, moe_gain)
    outgoing = lax.dot_general(
        pick_table.astype(BF16), normed, (((0,), (0,)), ((), ())), preferred_element_type=F32
    ).astype(BF16)
    received = swap(outgoing.reshape(experts, capacity, width), "tp")
    expert_out = expert_units(received.reshape(experts * capacity, width), units)
    returned = swap(expert_out.reshape(experts, capacity, width), "tp")
    flat_back = returned.reshape(experts * capacity, width)
    high, middle, low = pieces_of(weight_of[:pre_rows])

    def mix(piece):
        table = jnp.where(pick, piece[:, :, None], jnp.zeros((), BF16))
        return jnp.dot(
            table.reshape(pre_rows, experts * capacity), flat_back, preferred_element_type=F32
        )

    out_pre = (x_f32 + (mix(high) + mix(middle) + mix(low))).astype(BF16)

    hidden_f32 = hidden_dec.astype(F32)
    normed_dec = rms(hidden_f32, moe_gain)
    group_rows = spread(normed_dec, "tp").reshape(group_reqs, width)
    dec_out = expert_units(group_rows, units)
    dec_back = swap(dec_out[:, None, :], "tp").reshape(experts, width)
    dec_weight = weight_of[pre_rows:]
    mixture = jnp.sum(dec_weight.reshape(experts, 1) * dec_back.astype(F32), axis=0, keepdims=True)
    out_dec = (hidden_f32 + mixture).astype(BF16)
    return (out_pre, out_dec)


def solution(mesh):
    placed = (
        P(("dp", "tp"), None),
        P(("dp", "tp"), None),
        P(("dp", "tp"), None),
        P(),
        P("dp"),
        P("dp"),
        P("dp", None, "tp", None),
        P("dp", None, "tp", None),
        P(None, "tp"),
        P(("dp", "tp"), None),
        P(("dp", "tp"), None),
        P(("dp", "tp"), None),
        P(),
        P("tp", "dp", None),
        P("tp", "dp", None),
        P("tp", "dp", None),
    )
    return jax.shard_map(
        on_device,
        mesh=mesh,
        in_specs=placed,
        out_specs=(P(("dp", "tp"), None), P(("dp", "tp"), None)),
        check_vma=False,
    )
```

time: 763 us -> 261 us (0.34)
  the two profiles are of different devices: /device:TPU:4 before, /device:TPU:16 now
where the time goes in v1:
time: 261 us; the launch traced here: 260 us
  waiting for transfers between devices  124 us (48%)
  starting transfers between devices  63.6 us (24%)
  matrix products  24.7 us (9%)
  blocking collectives  17.6 us (7%)
  between operations  15.2 us (6%)
  local copies, waits for them, and re-layouts  7.59 us (3%)
  other arithmetic  7.5 us (3%)
    all_to_all x10, waiting for transfers between devices, swap(): lax.all_to_all(blocks, axis_name, split_axis=0, concat_axis=0, tiled=True)  124 us
    all_to_all x10, starting transfers between devices, swap(): lax.all_to_all(blocks, axis_name, split_axis=0, concat_axis=0, tiled=True)  63.6 us
    all_to_all x1, blocking collectives, swap(): lax.all_to_all(blocks, axis_name, split_axis=0, concat_axis=0, tiled=True)  17.6 us
    dot_general x2, matrix products, expert_units(): return jnp.dot(active, units[2], preferred_element_type=F32).astype(BF16)  11.1 us
    dot_general x2, matrix products, contract_rows(): lax.dot_general(left_rows, unit_rows, (((1,), (1,)), ((), ())), preferred...  6.68 us
  transfers between devices with their start and end apart: 11, of which 9 were waited for; matrix products, arithmetic and copies ran while one was open for 14% of the time, Pallas kernels for 0%

profile of v1, /device:TPU:16, one launch (start us, length us, event | category | flops | bytes accessed | tf_op | source)
XLA Modules:
  0.0 260.3 jit_solution(10199256775622486602)
XLA Ops:
  7.3 2.0 pad_maximum_fusion
  9.3 0.7 maximum_reduce_fusion
  10.0 17.6 %all_to_all.55 = bf16[32,1,128]{2,1,0:T(2,128)(2,1)S(1)} all-to-all(bf16[32,1,128]{2,1,0:T(2,128)(2,1)S(1)} %copy.103), channel_id=1, replica_groups=mesh['dp'=16,'tp'=32] {'tp'}, dimensions={0} | all-to-all | bytes 16384 | tf_op jit(solution)/shard_map/all_to_all | solution.py:18
  27.6 0.7 broadcast_in_dim.183
  28.3 10.4 %all-to-all-start.3 = ((bf16[16,32,128]{2,1,0:T(8,128)(2,1)}), bf16[16,32,128]{2,1,0:T(8,128)(2,1)S(1)}, u32[]{:S(2)}, u32[]{:S(2)}) async-start(bf16[16,32,128]{2,1,0:T(8,128)(2,1)} %broadcast_in_dim.183), calls=%async_computation.3 | async-start | bytes 262144 | tf_op jit(solution)/shard_map/all_to_all | solution.py:18
  38.8 10.5 %all-to-all-done.3 = bf16[16,32,128]{2,1,0:T(8,128)(2,1)S(1)} async-done(((bf16[16,32,128]{2,1,0:T(8,128)(2,1)}), bf16[16,32,128]{2,1,0:T(8,128)(2,1)S(1)}, u32[]{:S(2)}, u32[]{:S(2)}) %all-to-all-start.3) | async-done | bytes 131104 | tf_op jit(solution)/shard_map/all_to_all | solution.py:18
  49.5 0.7 broadcast_in_dim.184
  50.2 5.9 %all-to-all-start.4 = ((bf16[32,16,128]{2,1,0:T(8,128)(2,1)}), bf16[32,16,128]{2,1,0:T(8,128)(2,1)S(1)}, u32[]{:S(2)}, u32[]{:S(2)}) async-start(bf16[32,16,128]{2,1,0:T(8,128)(2,1)} %broadcast_in_dim.184), calls=%async_computation.4 | async-start | bytes 262144 | tf_op jit(solution)/shard_map/all_to_all | solution.py:18
  56.4 9.2 %all-to-all-done.4 = bf16[32,16,128]{2,1,0:T(8,128)(2,1)S(1)} async-done(((bf16[32,16,128]{2,1,0:T(8,128)(2,1)}), bf16[32,16,128]{2,1,0:T(8,128)(2,1)S(1)}, u32[]{:S(2)}, u32[]{:S(2)}) %all-to-all-start.4) | async-done | bytes 131104 | tf_op jit(solution)/shard_map/all_to_all | solution.py:18
  65.7 1.1 fusion.78
  66.9 0.3 fusion.29
  67.5 1.3 convolution_convert_fusion.3
  69.0 0.7 copy.112
  69.7 5.7 %all-to-all-start.5 = ((bf16[32,16,128]{2,1,0:T(8,128)(2,1)}), bf16[32,16,128]{2,1,0:T(8,128)(2,1)S(1)}, u32[]{:S(2)}, u32[]{:S(2)}) async-start(bf16[32,16,128]{2,1,0:T(8,128)(2,1)} %copy.112), calls=%async_computation.5 | async-start | bytes 262144 | tf_op jit(solution)/shard_map/all_to_all | solution.py:18
  75.6 8.8 %all-to-all-done.5 = bf16[32,16,128]{2,1,0:T(8,128)(2,1)S(1)} async-done(((bf16[32,16,128]{2,1,0:T(8,128)(2,1)}), bf16[32,16,128]{2,1,0:T(8,128)(2,1)S(1)}, u32[]{:S(2)}, u32[]{:S(2)}) %all-to-all-start.5) | async-done | bytes 131104 | tf_op jit(solution)/shard_map/all_to_all | solution.py:18
  84.8 0.7 broadcast_in_dim.193
  85.5 5.4 %all-to-all-start.6 = ((bf16[32,12,128]{2,1,0:T(8,128)(2,1)}), bf16[32,12,128]{2,1,0:T(8,128)(2,1)S(1)}, u32[]{:S(2)}, u32[]{:S(2)}) async-start(bf16[32,12,128]{2,1,0:T(8,128)(2,1)} %broadcast_in_dim.193), calls=%async_computation.6 | async-start | bytes 262144 | tf_op jit(solution)/shard_map/all_to_all | solution.py:18
  91.1 8.8 %all-to-all-done.6 = bf16[32,12,128]{2,1,0:T(8,128)(2,1)S(1)} async-done(((bf16[32,12,128]{2,1,0:T(8,128)(2,1)}), bf16[32,12,128]{2,1,0:T(8,128)(2,1)S(1)}, u32[]{:S(2)}, u32[]{:S(2)}) %all-to-all-start.6) | async-done | bytes 98336 | tf_op jit(solution)/shard_map/all_to_all | solution.py:18
  100.1 0.8 reshape.232
  100.9 3.5 %all-to-all-start.7 = ((bf16[16,2,768]{2,1,0:T(2,128)(2,1)}), bf16[16,2,768]{2,1,0:T(2,128)(2,1)S(1)}, u32[]{:S(2)}, u32[]{:S(2)}) async-start(bf16[16,2,768]{2,1,0:T(2,128)(2,1)} %reshape.232), calls=%async_computation.7 | async-start | bytes 98304 | tf_op jit(solution)/shard_map/all_to_all | solution.py:18
  104.4 7.6 %all-to-all-done.7 = bf16[16,2,768]{2,1,0:T(2,128)(2,1)S(1)} async-done(((bf16[16,2,768]{2,1,0:T(2,128)(2,1)}), bf16[16,2,768]{2,1,0:T(2,128)(2,1)S(1)}, u32[]{:S(2)}, u32[]{:S(2)}) %all-to-all-start.7) | async-done | bytes 49184 | tf_op jit(solution)/shard_map/all_to_all | solution.py:18
  112.2 0.2 fusion.13
  112.4 0.6 copy.114
  113.0 5.5 %all-to-all-start.8 = ((bf16[32,1,48]{2,1,0:T(2,128)(2,1)}), bf16[32,1,48]{2,1,0:T(2,128)(2,1)S(1)}, u32[]{:S(2)}, u32[]{:S(2)}) async-start(bf16[32,1,48]{2,1,0:T(2,128)(2,1)} %copy.114), calls=%async_computation.8 | async-start | bytes 32768 | tf_op jit(solution)/shard_map/all_to_all | solution.py:18
  118.8 7.4 %all-to-all-done.8 = bf16[32,1,48]{2,1,0:T(2,128)(2,1)S(1)} async-done(((bf16[32,1,48]{2,1,0:T(2,128)(2,1)}), bf16[32,1,48]{2,1,0:T(2,128)(2,1)S(1)}, u32[]{:S(2)}, u32[]{:S(2)}) %all-to-all-start.8) | async-done | bytes 3104 | tf_op jit(solution)/shard_map/all_to_all | solution.py:18
  126.4 0.6 multiply_reduce_fusion.2
  127.8 0.5 broadcast.106
  128.3 1.2 reduce.12
  129.6 0.7 reshape.234
  130.2 5.8 %all-to-all-start.9 = ((bf16[32,2,768]{2,1,0:T(2,128)(2,1)}), bf16[32,2,768]{2,1,0:T(2,128)(2,1)S(1)}, u32[]{:S(2)}, u32[]{:S(2)}) async-start(bf16[32,2,768]{2,1,0:T(2,128)(2,1)} %reshape.234), calls=%async_computation.9 | async-start | bytes 196608 | tf_op jit(solution)/shard_map/all_to_all | solution.py:18
  136.1 1.8 convolution_convert_fusion.1
  137.9 6.8 %all-to-all-done.9 = bf16[32,2,768]{2,1,0:T(2,128)(2,1)S(1)} async-done(((bf16[32,2,768]{2,1,0:T(2,128)(2,1)}), bf16[32,2,768]{2,1,0:T(2,128)(2,1)S(1)}, u32[]{:S(2)}, u32[]{:S(2)}) %all-to-all-start.9) | async-done | bytes 98336 | tf_op jit(solution)/shard_map/all_to_all | solution.py:18
  144.7 5.6 %all-to-all-start = ((bf16[32,16,1536]{2,1,0:T(8,128)(2,1)}), bf16[32,16,1536]{2,1,0:T(8,128)(2,1)S(1)}, u32[]{:S(2)}, u32[]{:S(2)}) async-start(bf16[32,16,1536]{2,1,0:T(8,128)(2,1)} %bitcast.2), calls=%async_computation | async-start | bytes 3145728 | tf_op jit(solution)/shard_map/all_to_all | solution.py:18
  150.4 2.4 fusion.11
  152.8 3.9 %fusion.4 = bf16[32,1,1536]{2,0,1:T(8,128)(2,1)S(1)} fusion(bf16[3,768,1536]{2,1,0:T(8,128)(2,1)} %all-gather.2.cloned.1.call-done, f32[32,768]{1,0:T(8,128)S(1)} %fusion.11, bf16[32,1,1536]{2,1,0:T(2,128)(2,1)S(1)} %reshape.235), kind=kOutput, calls=%fused_computation.13 | convolution fusion | flops 151093248 | bytes 5013504 | tf_op jit(solution)/shard_map/dot_general | solution.py:46
  156.8 0.7 reduce.13
  157.4 0.7 reshape.236
  158.1 29.7 %all-to-all-done = bf16[32,16,1536]{2,1,0:T(8,128)(2,1)S(1)} async-done(((bf16[32,16,1536]{2,1,0:T(8,128)(2,1)}), bf16[32,16,1536]{2,1,0:T(8,128)(2,1)S(1)}, u32[]{:S(2)}, u32[]{:S(2)}) %all-to-all-start) | async-done | bytes 1572896 | tf_op jit(solution)/shard_map/all_to_all | solution.py:18
  187.8 5.7 %all-to-all-start.10 = ((bf16[32,2,768]{2,1,0:T(2,128)(2,1)}), bf16[32,2,768]{2,1,0:T(2,128)(2,1)S(1)}, u32[]{:S(2)}, u32[]{:S(2)}) async-start(bf16[32,2,768]{2,1,0:T(2,128)(2,1)} %reshape.236), calls=%async_computation.10 | async-start | bytes 196608 | tf_op jit(solution)/shard_map/all_to_all | solution.py:18
  193.6 4.3 %fusion.6 = f32[512,768]{1,0:T(8,128)} fusion(bf16[512,1536]{1,0:T(8,128)(2,1)S(1)} %bitcast.101, bf16[3,768,1536]{2,1,0:T(8,128)(2,1)} %all-gather.2.cloned.1.call-done), kind=kOutput, calls=%fused_computation.15 | convolution fusion | flops 1207959552 | bytes 5505024 | tf_op jit(solution)/shard_map/dot_general | solution.py:12
  197.8 7.2 %convolution_convert_fusion = bf16[512,1536]{1,0:T(8,128)(2,1)} fusion(bf16[3,768,1536]{2,1,0:T(8,128)(2,1)} %all-gather.2.cloned.1.call-done, f32[512,768]{1,0:T(8,128)} %fusion.6, bf16[512,1536]{1,0:T(8,128)(2,1)S(1)} %bitcast.102), kind=kOutput, calls=%fused_computation | convolution fusion | flops 2417885184 | bytes 9437184 | tf_op jit(solution)/shard_map/dot_general | solution.py:46
  205.1 9.9 %all-to-all-start.1 = ((bf16[32,16,1536]{2,1,0:T(8,128)(2,1)}), bf16[32,16,1536]{2,1,0:T(8,128)(2,1)S(1)}, u32[]{:S(2)}, u32[]{:S(2)}) async-start(bf16[32,16,1536]{2,1,0:T(8,128)(2,1)} %bitcast.7), calls=%async_computation.1 | async-start | bytes 3145728 | tf_op jit(solution)/shard_map/all_to_all | solution.py:18
  215.3 0.2 convert_element_type.162
  215.6 0.6 add_convert_fusion
  216.3 35.2 %all-to-all-done.1 = bf16[32,16,1536]{2,1,0:T(8,128)(2,1)S(1)} async-done(((bf16[32,16,1536]{2,1,0:T(8,128)(2,1)}), bf16[32,16,1536]{2,1,0:T(8,128)(2,1)S(1)}, u32[]{:S(2)}, u32[]{:S(2)}) %all-to-all-start.1) | async-done | bytes 1572896 | tf_op jit(solution)/shard_map/all_to_all | solution.py:18
  251.5 0.4 convolution_bitcast_fusion.2
  251.9 0.4 fusion.2
  252.3 1.1 fusion.3
  (82 shorter events, 3.3 us)
Async XLA Ops:
  7.2 92.7 %copy-start = (bf16[1536,48]{0,1:T(8,128)(2,1)S(1)}, bf16[1536,48]{0,1:T(8,128)(2,1)}, u32[]{:S(2)}) copy-start(bf16[1536,48]{0,1:T(8,128)(2,1)} %param.24) | copy-start | bytes 442372
  7.2 31.6 %copy-start.10 = (s32[512]{0:T(512)S(1)}, s32[512]{0:T(512)}, u32[]{:S(2)}) copy-start(s32[512]{0:T(512)} %param.19) | copy-start | bytes 6148
  7.2 49.1 %copy-start.6 = (s32[32]{0:T(128)S(1)}, s32[32]{0:T(128)}, u32[]{:S(2)}) copy-start(s32[32]{0:T(128)} %param.20) | copy-start | bytes 388
  7.2 49.1 %copy-start.7 = (s32[32]{0:T(128)S(1)}, s32[32]{0:T(128)}, u32[]{:S(2)}) copy-start(s32[32]{0:T(128)} %param.21) | copy-start | bytes 388
  7.2 58.5 %copy-start.8 = (bf16[32,2,64,128]{3,2,1,0:T(8,128)(2,1)S(1)}, bf16[32,2,64,128]{3,2,1,0:T(8,128)(2,1)}, u32[]{:S(2)}) copy-start(bf16[32,2,64,128]{3,2,1,0:T(8,128)(2,1)} %param.22) | copy-start | bytes 3145732
  7.2 143.2 %all-gather.2.cloned.1.call-start = ((), (), s32[]{:S(2)}) async-start(), calls=%async_computation.11 | async-start | bytes 7520256 | tf_op jit(solution)/shard_map/all_gather | solution.py:79
  28.3 21.1 %all-to-all-start.3 = ((bf16[16,32,128]{2,1,0:T(8,128)(2,1)}), bf16[16,32,128]{2,1,0:T(8,128)(2,1)S(1)}, u32[]{:S(2)}, u32[]{:S(2)}) async-start(bf16[16,32,128]{2,1,0:T(8,128)(2,1)} %broadcast_in_dim.183), calls=%async_computation.3 | async-start | bytes 262144 | tf_op jit(solution)/shard_map/all_to_all | solution.py:18
  50.2 15.3 %all-to-all-start.4 = ((bf16[32,16,128]{2,1,0:T(8,128)(2,1)}), bf16[32,16,128]{2,1,0:T(8,128)(2,1)S(1)}, u32[]{:S(2)}, u32[]{:S(2)}) async-start(bf16[32,16,128]{2,1,0:T(8,128)(2,1)} %broadcast_in_dim.184), calls=%async_computation.4 | async-start | bytes 262144 | tf_op jit(solution)/shard_map/all_to_all | solution.py:18
  65.6 2.0 copy-start.9
  67.5 7.8 %copy-start.4 = (s32[64,4]{0,1:T(4,128)S(1)}, s32[64,4]{0,1:T(4,128)}, u32[]{:S(2)}) copy-start(s32[64,4]{0,1:T(4,128)} %param.26) | copy-start | bytes 3076
  67.5 7.9 %copy-start.1 = (bf16[63,1536]{1,0:T(8,128)(2,1)S(1)}, bf16[63,1536]{1,0:T(8,128)(2,1)}, u32[]{:S(2)}) copy-start(bf16[63,1536]{1,0:T(8,128)(2,1)} %param.25) | copy-start | bytes 580612
  68.9 57.5 %copy-start.2 = (bf16[1,1536]{1,0:T(2,128)(2,1)S(1)}, bf16[1,1536]{1,0:T(2,128)(2,1)}, u32[]{:S(2)}) copy-start(bf16[1,1536]{1,0:T(2,128)(2,1)} %param.18) | copy-start | bytes 9220
  68.9 58.8 %copy-start.3 = (f32[1536]{0:T(1024)S(1)}, f32[1536]{0:T(1024)}, u32[]{:S(2)}) copy-start(f32[1536]{0:T(1024)} %param.28) | copy-start | bytes 18436
  69.7 14.7 %all-to-all-start.5 = ((bf16[32,16,128]{2,1,0:T(8,128)(2,1)}), bf16[32,16,128]{2,1,0:T(8,128)(2,1)S(1)}, u32[]{:S(2)}, u32[]{:S(2)}) async-start(bf16[32,16,128]{2,1,0:T(8,128)(2,1)} %copy.112), calls=%async_computation.5 | async-start | bytes 262144 | tf_op jit(solution)/shard_map/all_to_all | solution.py:18
  85.5 14.3 %all-to-all-start.6 = ((bf16[32,12,128]{2,1,0:T(8,128)(2,1)}), bf16[32,12,128]{2,1,0:T(8,128)(2,1)S(1)}, u32[]{:S(2)}, u32[]{:S(2)}) async-start(bf16[32,12,128]{2,1,0:T(8,128)(2,1)} %broadcast_in_dim.193), calls=%async_computation.6 | async-start | bytes 262144 | tf_op jit(solution)/shard_map/all_to_all | solution.py:18
  100.9 11.1 %all-to-all-start.7 = ((bf16[16,2,768]{2,1,0:T(2,128)(2,1)}), bf16[16,2,768]{2,1,0:T(2,128)(2,1)S(1)}, u32[]{:S(2)}, u32[]{:S(2)}) async-start(bf16[16,2,768]{2,1,0:T(2,128)(2,1)} %reshape.232), calls=%async_computation.7 | async-start | bytes 98304 | tf_op jit(solution)/shard_map/all_to_all | solution.py:18
  113.0 13.2 %all-to-all-start.8 = ((bf16[32,1,48]{2,1,0:T(2,128)(2,1)}), bf16[32,1,48]{2,1,0:T(2,128)(2,1)S(1)}, u32[]{:S(2)}, u32[]{:S(2)}) async-start(bf16[32,1,48]{2,1,0:T(2,128)(2,1)} %copy.114), calls=%async_computation.8 | async-start | bytes 32768 | tf_op jit(solution)/shard_map/all_to_all | solution.py:18
  130.2 14.5 %all-to-all-start.9 = ((bf16[32,2,768]{2,1,0:T(2,128)(2,1)}), bf16[32,2,768]{2,1,0:T(2,128)(2,1)S(1)}, u32[]{:S(2)}, u32[]{:S(2)}) async-start(bf16[32,2,768]{2,1,0:T(2,128)(2,1)} %reshape.234), calls=%async_computation.9 | async-start | bytes 196608 | tf_op jit(solution)/shard_map/all_to_all | solution.py:18
  144.7 43.1 %all-to-all-start = ((bf16[32,16,1536]{2,1,0:T(8,128)(2,1)}), bf16[32,16,1536]{2,1,0:T(8,128)(2,1)S(1)}, u32[]{:S(2)}, u32[]{:S(2)}) async-start(bf16[32,16,1536]{2,1,0:T(8,128)(2,1)} %bitcast.2), calls=%async_computation | async-start | bytes 3145728 | tf_op jit(solution)/shard_map/all_to_all | solution.py:18
  187.8 17.3 %all-to-all-start.10 = ((bf16[32,2,768]{2,1,0:T(2,128)(2,1)}), bf16[32,2,768]{2,1,0:T(2,128)(2,1)S(1)}, u32[]{:S(2)}, u32[]{:S(2)}) async-start(bf16[32,2,768]{2,1,0:T(2,128)(2,1)} %reshape.236), calls=%async_computation.10 | async-start | bytes 196608 | tf_op jit(solution)/shard_map/all_to_all | solution.py:18
  205.1 9.9 %copy-start.5 = (f32[64,4]{0,1:T(4,128)S(1)}, f32[64,4]{0,1:T(4,128)}, u32[]{:S(2)}) copy-start(f32[64,4]{0,1:T(4,128)} %param.27) | copy-start | bytes 3076
  205.1 46.4 %all-to-all-start.1 = ((bf16[32,16,1536]{2,1,0:T(8,128)(2,1)}), bf16[32,16,1536]{2,1,0:T(8,128)(2,1)S(1)}, u32[]{:S(2)}, u32[]{:S(2)}) async-start(bf16[32,16,1536]{2,1,0:T(8,128)(2,1)} %bitcast.7), calls=%async_computation.1 | async-start | bytes 3145728 | tf_op jit(solution)/shard_map/all_to_all | solution.py:18
Sparse Core Ops, SparseCore 0:
  10.2 60.4 all-gather.1

commit v2 on v1

--- a/solution.py
+++ b/solution.py
@@ -76,9 +76,10 @@
     experts = tp_size * w_gate.shape[0]
     assert group_reqs == tp_size and experts == tp_size
 
-    units = lax.all_gather(
-        jnp.concatenate([w_gate, w_up, w_down], axis=0), "dp", axis=1, tiled=True
-    )
+    out_rows = lax.all_gather(w_out.T, "tp", axis=0, tiled=True)
+    stacked = jnp.concatenate([w_gate, w_up, w_down], axis=0)
+    stacked, _ = lax.optimization_barrier((stacked, out_rows))
+    units = lax.all_gather(stacked, "dp", axis=1, tiled=True)
 
     columns = heads + 2 * kv_heads
     share = tp_size // columns
@@ -134,31 +135,40 @@
     mixed = jnp.sum(scale[:, :, None] * gathered[:, :heads].astype(F32), axis=0)
     attention_row = (mixed / total[:, None]).astype(BF16)
 
-    attention = spread(attention_row, "tp").reshape(group_reqs, width)
-    projected = jnp.dot(attention, w_out, preferred_element_type=F32).astype(BF16)
-    all_projected = spread(projected, "dp").reshape(total_reqs, projected.shape[1])
-    home_ids = dp_group * group_reqs + jnp.arange(group_reqs, dtype=jnp.int32)
-    at_home = choose_rows(home_ids[:, None] == placing[None, :], all_projected)
-    proj_home = swap(at_home[:, None, :], "tp").reshape(1, width)
+    projected = contract_rows(attention_row.reshape(1, width), out_rows).astype(BF16)
+    request = lax.dynamic_slice_in_dim(placing, dp_group * group_reqs + tp_lane, 1)[0]
+    lane_of = jnp.arange(tp_size, dtype=jnp.int32) == request % tp_size
+    no_value = jnp.zeros((), BF16)
+    by_lane = swap(jnp.where(lane_of[:, None], projected, no_value).reshape(tp_size, heads, head_size), "tp")
+    group_rows = lax.dynamic_slice_in_dim(placing, dp_group * group_reqs, group_reqs)
+    here = group_rows % tp_size == tp_lane
+    to_group = (group_rows // tp_size)[None, :] == jnp.arange(dp_size, dtype=jnp.int32)[:, None]
+    outbound = choose_rows(to_group & here[None, :], by_lane.reshape(tp_size, width))
+    inbound = swap(outbound.reshape(dp_size, heads, head_size), "dp").reshape(dp_size, width)
+    home_ids = dp_group * tp_size + tp_lane
+    source = jnp.sum(jnp.where(placing == home_ids, jnp.arange(total_reqs, dtype=jnp.int32), 0))
+    source_group = source // group_reqs
+    from_group = jnp.arange(dp_size, dtype=jnp.int32)[None, :] == source_group
+    proj_home = choose_rows(from_group, inbound)
     hidden_dec = (resid_dec.astype(F32) + proj_home.astype(F32)).astype(BF16)
 
     route_weight = route_scale / jnp.sum(route_scale, axis=-1, keepdims=True)
     expert_ids = jnp.arange(experts, dtype=jnp.int32)
     hits = routes[:, :, None] == expert_ids[None, None, :]
     weight_of = jnp.sum(jnp.where(hits, route_weight[:, :, None], 0.0), axis=1)
-    pre_rows = x_pre.shape[0]
+    moe_rows = jnp.concatenate([x_pre, hidden_dec], axis=0)
+    rows_dev = moe_rows.shape[0]
     top_count = routes.shape[1]
-    capacity = min(2 * (pre_rows + 1) * top_count // experts, pre_rows + 1)
-
-    routed = jnp.any(hits[:pre_rows], axis=1)
-    row_ids = jnp.arange(pre_rows, dtype=jnp.int32)
+    capacity = min(2 * rows_dev * top_count // experts, rows_dev)
+    routed = jnp.any(hits, axis=1)
+    row_ids = jnp.arange(rows_dev, dtype=jnp.int32)
     before = (row_ids[None, :] < row_ids[:, None]).astype(BF16)
     position = jnp.dot(before, routed.astype(BF16), preferred_element_type=F32).astype(jnp.int32)
     slot_ids_e = jnp.arange(capacity, dtype=jnp.int32)
     pick = routed[:, :, None] & (position[:, :, None] == slot_ids_e[None, None, :])
-    pick_table = pick.reshape(pre_rows, experts * capacity)
-    x_f32 = x_pre.astype(F32)
-    normed = rms(x_f32, moe_gain)
+    pick_table = pick.reshape(rows_dev, experts * capacity)
+    rows_f32 = moe_rows.astype(F32)
+    normed = rms(rows_f32, moe_gain)
     outgoing = lax.dot_general(
         pick_table.astype(BF16), normed, (((0,), (0,)), ((), ())), preferred_element_type=F32
     ).astype(BF16)
@@ -166,25 +176,16 @@
     expert_out = expert_units(received.reshape(experts * capacity, width), units)
     returned = swap(expert_out.reshape(experts, capacity, width), "tp")
     flat_back = returned.reshape(experts * capacity, width)
-    high, middle, low = pieces_of(weight_of[:pre_rows])
+    high, middle, low = pieces_of(weight_of)
 
     def mix(piece):
-        table = jnp.where(pick, piece[:, :, None], jnp.zeros((), BF16))
+        table = jnp.where(pick, piece[:, :, None], no_value)
         return jnp.dot(
-            table.reshape(pre_rows, experts * capacity), flat_back, preferred_element_type=F32
+            table.reshape(rows_dev, experts * capacity), flat_back, preferred_element_type=F32
         )
 
-    out_pre = (x_f32 + (mix(high) + mix(middle) + mix(low))).astype(BF16)
-
-    hidden_f32 = hidden_dec.astype(F32)
-    normed_dec = rms(hidden_f32, moe_gain)
-    group_rows = spread(normed_dec, "tp").reshape(group_reqs, width)
-    dec_out = expert_units(group_rows, units)
-    dec_back = swap(dec_out[:, None, :], "tp").reshape(experts, width)
-    dec_weight = weight_of[pre_rows:]
-    mixture = jnp.sum(dec_weight.reshape(experts, 1) * dec_back.astype(F32), axis=0, keepdims=True)
-    out_dec = (hidden_f32 + mixture).astype(BF16)
-    return (out_pre, out_dec)
+    moe_out = (rows_f32 + (mix(high) + mix(middle) + mix(low))).astype(BF16)
+    return (moe_out[: rows_dev - 1], moe_out[rows_dev - 1 :])
 
 
 def solution(mesh):

time: 261 us -> 314 us (1.20)
  the two profiles are of different devices: /device:TPU:16 before, /device:TPU:2 now
where the time goes in v2:
time: 314 us; the launch traced here: 313 us
  waiting for transfers between devices  171 us (54%)
  blocking collectives  60.8 us (19%)
  starting transfers between devices  33 us (11%)
  between operations  19 us (6%)
  matrix products  18.5 us (6%)
  other arithmetic  5.56 us (2%)
  local copies, waits for them, and re-layouts  4.87 us (2%)
    all_gather x1, waiting for transfers between devices, on_device(): out_rows = lax.all_gather(w_out.T, 'tp', axis=0, tiled=True)  93.1 us
    all_to_all x6, waiting for transfers between devices, swap(): lax.all_to_all(blocks, axis_name, split_axis=0, concat_axis=0, tiled=True)  77.6 us
    all_to_all x2, blocking collectives, swap(): lax.all_to_all(blocks, axis_name, split_axis=0, concat_axis=0, tiled=True)  60.8 us
    all_to_all x6, starting transfers between devices, swap(): lax.all_to_all(blocks, axis_name, split_axis=0, concat_axis=0, tiled=True)  33 us
    dot_general x2, matrix products, contract_rows(): lax.dot_general(left_rows, unit_rows, (((1,), (1,)), ((), ())), preferred...  6.79 us
    dot_general x1, matrix products, expert_units(): return jnp.dot(active, units[2], preferred_element_type=F32).astype(BF16)  6.77 us
  transfers between devices with their start and end apart: 8, of which 7 were waited for; matrix products, arithmetic and copies ran while one was open for 5% of the time, Pallas kernels for 0%

profile of v2, /device:TPU:2, one launch (start us, length us, event | category | flops | bytes accessed | tf_op | source)
XLA Modules:
  0.0 313.3 jit_solution(5747145062844890888)
XLA Ops:
  7.3 0.7 all-gather.3.cloned.1.call-update
  8.0 2.0 pad_maximum_fusion
  10.0 93.1 %all-gather.3.cloned.1.call-done = bf16[1536,1536]{1,0:T(8,128)(2,1)} async-done(((bf16[48,1536]{1,0:T(8,128)(2,1)}), bf16[1536,1536]{1,0:T(8,128)(2,1)}) %all-gather.3.cloned.1.call-update) | async-done | bytes 4718608 | tf_op jit(solution)/shard_map/all_gather | solution.py:79
  103.1 0.7 maximum_reduce_fusion
  103.9 16.0 %all_to_all.40 = bf16[32,1,128]{2,1,0:T(2,128)(2,1)S(1)} all-to-all(bf16[32,1,128]{2,1,0:T(2,128)(2,1)S(1)} %copy.71), channel_id=1, replica_groups=mesh['dp'=16,'tp'=32] {'tp'}, dimensions={0} | all-to-all | bytes 16384 | tf_op jit(solution)/shard_map/all_to_all | solution.py:18
  119.9 0.7 broadcast_in_dim.175
  120.6 7.5 %all-to-all-start.1 = ((bf16[16,32,128]{2,1,0:T(8,128)(2,1)}), bf16[16,32,128]{2,1,0:T(8,128)(2,1)S(1)}, u32[]{:S(2)}, u32[]{:S(2)}) async-start(bf16[16,32,128]{2,1,0:T(8,128)(2,1)} %broadcast_in_dim.175), calls=%async_computation.1 | async-start | bytes 262144 | tf_op jit(solution)/shard_map/all_to_all | solution.py:18
  128.3 10.4 %all-to-all-done.1 = bf16[16,32,128]{2,1,0:T(8,128)(2,1)S(1)} async-done(((bf16[16,32,128]{2,1,0:T(8,128)(2,1)}), bf16[16,32,128]{2,1,0:T(8,128)(2,1)S(1)}, u32[]{:S(2)}, u32[]{:S(2)}) %all-to-all-start.1) | async-done | bytes 131104 | tf_op jit(solution)/shard_map/all_to_all | solution.py:18
  138.7 0.2 convolution_convert_fusion.5
  138.9 0.7 broadcast_in_dim.176
  139.6 5.1 %all-to-all-start.2 = ((bf16[32,16,128]{2,1,0:T(8,128)(2,1)}), bf16[32,16,128]{2,1,0:T(8,128)(2,1)S(1)}, u32[]{:S(2)}, u32[]{:S(2)}) async-start(bf16[32,16,128]{2,1,0:T(8,128)(2,1)} %broadcast_in_dim.176), calls=%async_computation.2 | async-start | bytes 262144 | tf_op jit(solution)/shard_map/all_to_all | solution.py:18
  144.7 0.6 dynamic_slice.10
  147.4 6.6 %all-to-all-done.2 = bf16[32,16,128]{2,1,0:T(8,128)(2,1)S(1)} async-done(((bf16[32,16,128]{2,1,0:T(8,128)(2,1)}), bf16[32,16,128]{2,1,0:T(8,128)(2,1)S(1)}, u32[]{:S(2)}, u32[]{:S(2)}) %all-to-all-start.2) | async-done | bytes 131104 | tf_op jit(solution)/shard_map/all_to_all | solution.py:18
  154.2 1.1 fusion.76
  155.3 0.1 copy.76
  155.4 1.3 convolution_convert_fusion.3
  156.7 0.1 copy.84
  156.8 0.3 fusion.22
  157.1 0.1 copy.78
  157.2 0.1 copy.85
  157.4 0.7 copy.80
  158.1 5.7 %all-to-all-start.3 = ((bf16[32,16,128]{2,1,0:T(8,128)(2,1)}), bf16[32,16,128]{2,1,0:T(8,128)(2,1)S(1)}, u32[]{:S(2)}, u32[]{:S(2)}) async-start(bf16[32,16,128]{2,1,0:T(8,128)(2,1)} %copy.80), calls=%async_computation.3 | async-start | bytes 262144 | tf_op jit(solution)/shard_map/all_to_all | solution.py:18
  163.9 0.1 convolution_convert_fusion.4
  164.0 8.8 %all-to-all-done.3 = bf16[32,16,128]{2,1,0:T(8,128)(2,1)S(1)} async-done(((bf16[32,16,128]{2,1,0:T(8,128)(2,1)}), bf16[32,16,128]{2,1,0:T(8,128)(2,1)S(1)}, u32[]{:S(2)}, u32[]{:S(2)}) %all-to-all-start.3) | async-done | bytes 131104 | tf_op jit(solution)/shard_map/all_to_all | solution.py:18
  172.9 0.1 slice_add_fusion
  173.1 0.1 multiply_reduce_fusion
  173.4 3.7 %convolution_reduce_fusion.1 = bf16[1536]{0:T(1024)(128)(2,1)S(1)} fusion(bf16[1536,1]{0,1:T(2,128)(2,1)S(1)} %reshape.225, bf16[1536,1536]{1,0:T(8,128)(2,1)} %all-gather.3.cloned.1.call-done), kind=kOutput, calls=%fused_computation.21 | convolution fusion | flops 4718592 | bytes 4724736 | tf_op jit(solution)/shard_map/dot_general | solution.py:12
  177.1 0.8 broadcast_select_fusion
  177.9 5.4 %all-to-all-start.4 = ((bf16[32,12,128]{2,1,0:T(8,128)(2,1)}), bf16[32,12,128]{2,1,0:T(8,128)(2,1)S(1)}, u32[]{:S(2)}, u32[]{:S(2)}) async-start(bf16[32,12,128]{2,1,0:T(8,128)(2,1)} %broadcast_select_fusion), calls=%async_computation.4 | async-start | bytes 262144 | tf_op jit(solution)/shard_map/all_to_all | solution.py:18
  183.4 8.9 %all-to-all-done.4 = bf16[32,12,128]{2,1,0:T(8,128)(2,1)S(1)} async-done(((bf16[32,12,128]{2,1,0:T(8,128)(2,1)}), bf16[32,12,128]{2,1,0:T(8,128)(2,1)S(1)}, u32[]{:S(2)}, u32[]{:S(2)}) %all-to-all-start.4) | async-done | bytes 98336 | tf_op jit(solution)/shard_map/all_to_all | solution.py:18
  192.3 0.1 convolution_convert_fusion.2
  192.4 0.7 reshape.219
  193.1 3.5 %all-to-all-start.5 = ((bf16[16,12,128]{2,1,0:T(8,128)(2,1)}), bf16[16,12,128]{2,1,0:T(8,128)(2,1)S(1)}, u32[]{:S(2)}, u32[]{:S(2)}) async-start(bf16[16,12,128]{2,1,0:T(8,128)(2,1)} %reshape.219), calls=%async_computation.5 | async-start | bytes 131072 | tf_op jit(solution)/shard_map/all_to_all | solution.py:18
  196.6 0.6 select_reduce_fusion.1
  199.9 0.1 fusion.21
  200.1 4.3 %all-to-all-done.5 = bf16[16,12,128]{2,1,0:T(8,128)(2,1)S(1)} async-done(((bf16[16,12,128]{2,1,0:T(8,128)(2,1)}), bf16[16,12,128]{2,1,0:T(8,128)(2,1)S(1)}, u32[]{:S(2)}, u32[]{:S(2)}) %all-to-all-start.5) | async-done | bytes 49184 | tf_op jit(solution)/shard_map/all_to_all | solution.py:18
  204.4 0.1 convolution_reduce_fusion
  204.6 0.1 fusion.14
  204.7 0.6 convolution_convert_fusion.1
  205.4 44.8 %all_to_all.41 = bf16[32,16,1536]{2,1,0:T(8,128)(2,1)S(1)} all-to-all(bf16[32,16,1536]{2,1,0:T(8,128)(2,1)S(1)} %bitcast.91), channel_id=1, replica_groups=mesh['dp'=16,'tp'=32] {'tp'}, dimensions={0} | all-to-all | bytes 3145728 | tf_op jit(solution)/shard_map/all_to_all | solution.py:18
  250.2 3.1 fusion
  253.3 6.8 %convolution_convert_fusion = bf16[512,1536]{1,0:T(8,128)(2,1)} fusion(bf16[3,768,1536]{2,1,0:T(8,128)(2,1)} %all-gather.5.cloned.1.call-done, f32[512,768]{1,0:T(8,128)S(1)} %fusion, bf16[512,1536]{1,0:T(8,128)(2,1)S(1)} %bitcast.93), kind=kOutput, calls=%fused_computation | convolution fusion | flops 2417885184 | bytes 9437184 | tf_op jit(solution)/shard_map/dot_general | solution.py:46
  260.0 5.7 %all-to-all-start.7 = ((bf16[32,16,1536]{2,1,0:T(8,128)(2,1)}), bf16[32,16,1536]{2,1,0:T(8,128)(2,1)S(1)}, u32[]{:S(2)}, u32[]{:S(2)}) async-start(bf16[32,16,1536]{2,1,0:T(8,128)(2,1)} %bitcast.24), calls=%async_computation.7 | async-start | bytes 3145728 | tf_op jit(solution)/shard_map/all_to_all | solution.py:18
  265.8 38.6 %all-to-all-done.7 = bf16[32,16,1536]{2,1,0:T(8,128)(2,1)S(1)} async-done(((bf16[32,16,1536]{2,1,0:T(8,128)(2,1)}), bf16[32,16,1536]{2,1,0:T(8,128)(2,1)S(1)}, u32[]{:S(2)}, u32[]{:S(2)}) %all-to-all-start.7) | async-done | bytes 1572896 | tf_op jit(solution)/shard_map/all_to_all | solution.py:18
  304.4 0.4 convolution_bitcast_fusion.2
  304.9 0.4 fusion.4
  305.3 0.4 fusion.5
  305.7 0.7 slice.74
  (65 shorter events, 1.2 us)
Async XLA Ops:
  7.2 121.0 %copy-start.6 = (s32[512]{0:T(512)S(1)}, s32[512]{0:T(512)}, u32[]{:S(2)}) copy-start(s32[512]{0:T(512)} %param.19) | copy-start | bytes 6148
  7.2 121.1 %copy-start.3 = (s32[64,4]{0,1:T(4,128)S(1)}, s32[64,4]{0,1:T(4,128)}, u32[]{:S(2)}) copy-start(s32[64,4]{0,1:T(4,128)} %param.26) | copy-start | bytes 3076
  7.2 140.2 %copy-start.7 = (s32[32]{0:T(128)S(1)}, s32[32]{0:T(128)}, u32[]{:S(2)}) copy-start(s32[32]{0:T(128)} %param.20) | copy-start | bytes 388
  7.2 140.2 %copy-start.8 = (s32[32]{0:T(128)S(1)}, s32[32]{0:T(128)}, u32[]{:S(2)}) copy-start(s32[32]{0:T(128)} %param.21) | copy-start | bytes 388
  7.2 95.9 %all-gather.3.cloned.1.call-start = ((), (), s32[]{:S(2)}) async-start(), calls=%async_computation.8 | async-start | bytes 4866048 | tf_op jit(solution)/shard_map/all_gather | solution.py:79
  7.9 146.2 %copy-start.9 = (bf16[32,2,64,128]{3,2,1,0:T(8,128)(2,1)S(1)}, bf16[32,2,64,128]{3,2,1,0:T(8,128)(2,1)}, u32[]{:S(2)}) copy-start(bf16[32,2,64,128]{3,2,1,0:T(8,128)(2,1)} %param.22) | copy-start | bytes 3145732
  8.0 242.2 %all-gather.5.cloned.1.call-start = ((), (), s32[]{:S(2)}) async-start(), calls=%async_computation.9 | async-start | bytes 7520256 | tf_op jit(solution)/shard_map/all_gather | solution.py:82
  120.6 18.1 %all-to-all-start.1 = ((bf16[16,32,128]{2,1,0:T(8,128)(2,1)}), bf16[16,32,128]{2,1,0:T(8,128)(2,1)S(1)}, u32[]{:S(2)}, u32[]{:S(2)}) async-start(bf16[16,32,128]{2,1,0:T(8,128)(2,1)} %broadcast_in_dim.175), calls=%async_computation.1 | async-start | bytes 262144 | tf_op jit(solution)/shard_map/all_to_all | solution.py:18
  138.9 16.5 %copy-start.10 = (bf16[32,2,64,128]{3,2,1,0:T(8,128)(2,1)S(1)}, bf16[32,2,64,128]{3,2,1,0:T(8,128)(2,1)}, u32[]{:S(2)}) copy-start(bf16[32,2,64,128]{3,2,1,0:T(8,128)(2,1)} %param.23) | copy-start | bytes 3145732
  139.6 14.5 %all-to-all-start.2 = ((bf16[32,16,128]{2,1,0:T(8,128)(2,1)}), bf16[32,16,128]{2,1,0:T(8,128)(2,1)S(1)}, u32[]{:S(2)}, u32[]{:S(2)}) async-start(bf16[32,16,128]{2,1,0:T(8,128)(2,1)} %broadcast_in_dim.176), calls=%async_computation.2 | async-start | bytes 262144 | tf_op jit(solution)/shard_map/all_to_all | solution.py:18
  158.1 14.7 %all-to-all-start.3 = ((bf16[32,16,128]{2,1,0:T(8,128)(2,1)}), bf16[32,16,128]{2,1,0:T(8,128)(2,1)S(1)}, u32[]{:S(2)}, u32[]{:S(2)}) async-start(bf16[32,16,128]{2,1,0:T(8,128)(2,1)} %copy.80), calls=%async_computation.3 | async-start | bytes 262144 | tf_op jit(solution)/shard_map/all_to_all | solution.py:18
  173.3 31.2 %copy-start.5 = (bf16[1,1536]{1,0:T(2,128)(2,1)S(1)}, bf16[1,1536]{1,0:T(2,128)(2,1)}, u32[]{:S(2)}) copy-start(bf16[1,1536]{1,0:T(2,128)(2,1)} %param.18) | copy-start | bytes 9220
  173.3 31.2 %copy-start = (bf16[63,1536]{1,0:T(8,128)(2,1)S(1)}, bf16[63,1536]{1,0:T(8,128)(2,1)}, u32[]{:S(2)}) copy-start(bf16[63,1536]{1,0:T(8,128)(2,1)} %param.25) | copy-start | bytes 580612
  173.4 31.4 %copy-start.2 = (f32[1536]{0:T(1024)S(1)}, f32[1536]{0:T(1024)}, u32[]{:S(2)}) copy-start(f32[1536]{0:T(1024)} %param.28) | copy-start | bytes 18436
  177.9 14.4 %all-to-all-start.4 = ((bf16[32,12,128]{2,1,0:T(8,128)(2,1)}), bf16[32,12,128]{2,1,0:T(8,128)(2,1)S(1)}, u32[]{:S(2)}, u32[]{:S(2)}) async-start(bf16[32,12,128]{2,1,0:T(8,128)(2,1)} %broadcast_select_fusion), calls=%async_computation.4 | async-start | bytes 262144 | tf_op jit(solution)/shard_map/all_to_all | solution.py:18
  193.1 11.3 %all-to-all-start.5 = ((bf16[16,12,128]{2,1,0:T(8,128)(2,1)}), bf16[16,12,128]{2,1,0:T(8,128)(2,1)S(1)}, u32[]{:S(2)}, u32[]{:S(2)}) async-start(bf16[16,12,128]{2,1,0:T(8,128)(2,1)} %reshape.219), calls=%async_computation.5 | async-start | bytes 131072 | tf_op jit(solution)/shard_map/all_to_all | solution.py:18
  260.0 5.7 %copy-start.4 = (f32[64,4]{0,1:T(4,128)S(1)}, f32[64,4]{0,1:T(4,128)}, u32[]{:S(2)}) copy-start(f32[64,4]{0,1:T(4,128)} %param.27) | copy-start | bytes 3076
  260.0 44.4 %all-to-all-start.7 = ((bf16[32,16,1536]{2,1,0:T(8,128)(2,1)}), bf16[32,16,1536]{2,1,0:T(8,128)(2,1)S(1)}, u32[]{:S(2)}, u32[]{:S(2)}) async-start(bf16[32,16,1536]{2,1,0:T(8,128)(2,1)} %bitcast.24), calls=%async_computation.7 | async-start | bytes 3145728 | tf_op jit(solution)/shard_map/all_to_all | solution.py:18
  305.7 0.7 copy-start.1
Sparse Core Ops, SparseCore 0:
  11.2 91.8 all-gather.2
  105.2 55.1 all-gather.4

commit v3 on v1

v3 whole, which is shorter than its diff:
```python
import jax
import jax.numpy as jnp
from jax import lax
from jax.sharding import Mesh
from jax.sharding import PartitionSpec as P

TP = ("y", "x")
HIGHEST = lax.Precision.HIGHEST
F32 = jnp.float32
BF16 = jnp.bfloat16


def contract_rows(left_rows, unit_rows):
    return lax.dot_general(
        left_rows, unit_rows, (((1,), (1,)), ((), ())), preferred_element_type=F32
    )


def swap(blocks, axis_name):
    return lax.all_to_all(blocks, axis_name, split_axis=0, concat_axis=0, tiled=True)


def spread(block, axis_name):
    members = lax.axis_size(axis_name) if isinstance(axis_name, str) else lax.psum(1, axis_name)
    return swap(jnp.broadcast_to(block[None], (members,) + block.shape), axis_name)


def choose_rows(table, rows):
    return jnp.dot(table.astype(BF16), rows, preferred_element_type=F32).astype(BF16)


def pieces_of(x):
    high = lax.reduce_precision(x, 8, 7)
    middle = lax.reduce_precision(x - high, 8, 7)
    low = lax.reduce_precision(x - high - middle, 8, 7)
    return high.astype(BF16), middle.astype(BF16), low.astype(BF16)


def rms(rows_f32, gain):
    mean_square = jnp.mean(rows_f32 * rows_f32, axis=-1, keepdims=True)
    return (rows_f32 * lax.rsqrt(mean_square + 1e-06) * gain).astype(BF16)


def expert_units(rows, units):
    gate = contract_rows(rows, units[0])
    upper = contract_rows(rows, units[1])
    active = (jnp.maximum(gate, 0.0) * upper).astype(BF16)
    return jnp.dot(active, units[2], preferred_element_type=F32).astype(BF16)


def on_device(
    q_new,
    new_key_value,
    resid_dec,
    placing,
    lengths,
    write_pos,
    k_cache,
    value_cache,
    w_out,
    x_pre,
    routes,
    route_scale,
    moe_gain,
    w_gate,
    w_up,
    w_down,
):
    dp_size = lax.axis_size("dp")
    lines, posts = lax.axis_size("y"), lax.axis_size("x")
    tp_size = lines * posts
    dp_group = lax.axis_index("dp")
    line = lax.axis_index("y")
    tp_lane = line * posts + lax.axis_index("x")
    group_reqs, kv_heads, slot_dev, head_size = k_cache.shape
    width = q_new.shape[1]
    heads = width // head_size
    per_group = heads // kv_heads
    total_reqs = placing.shape[0]
    experts = tp_size * w_gate.shape[0]
    assert group_reqs == tp_size and experts == tp_size

    out_rows = lax.all_gather(w_out.T, "y", axis=0, tiled=True)
    units = lax.all_gather(
        jnp.concatenate([w_gate, w_up, w_down], axis=0), "dp", axis=1, tiled=True
    )

    no_value = jnp.zeros((), BF16)
    rows_dev, top_count = routes.shape
    pre_rows = rows_dev - 1
    capacity = min(2 * rows_dev * top_count // experts, rows_dev)
    route_weight = route_scale / jnp.sum(route_scale, axis=-1, keepdims=True)
    expert_ids = jnp.arange(experts, dtype=jnp.int32)
    hits = routes[:, :, None] == expert_ids[None, None, :]
    weight_of = jnp.sum(jnp.where(hits, route_weight[:, :, None], 0.0), axis=1)
    routed = jnp.any(hits, axis=1)

    row_ids = jnp.arange(rows_dev, dtype=jnp.int32)
    before = (row_ids[None, :] < row_ids[:, None]).astype(BF16)
    position = jnp.dot(before, routed.astype(BF16), preferred_element_type=F32).astype(jnp.int32)
    position = jnp.where(row_ids[:, None] == pre_rows, capacity - 1, position)
    slots = jnp.arange(capacity, dtype=jnp.int32)
    pick = routed[:, :, None] & (position[:, :, None] == slots[None, None, :])
    pick_table = pick.reshape(rows_dev, experts * capacity)
    x_f32 = x_pre.astype(F32)
    outgoing = lax.dot_general(
        pick_table[:pre_rows].astype(BF16),
        rms(x_f32, moe_gain),
        (((0,), (0,)), ((), ())),
        preferred_element_type=F32,
    ).astype(BF16)

    columns = heads + 2 * kv_heads
    share = tp_size // columns
    chosen_rows = group_reqs // share
    fresh = jnp.concatenate([q_new, new_key_value], axis=1).reshape(1, columns, 1, head_size)
    by_head = swap(
        jnp.broadcast_to(fresh, (share, columns, 1, head_size)).reshape(tp_size, 1, head_size), TP
    )
    by_head, outgoing = lax.optimization_barrier((by_head, outgoing))
    received = swap(outgoing.reshape(experts, capacity, width), TP)
    all_rows = lax.all_gather(by_head.reshape(tp_size, head_size), "dp", axis=0, tiled=True)
    first_row = dp_group * group_reqs + (tp_lane // columns) * chosen_rows
    wanted = lax.dynamic_slice_in_dim(placing, first_row, chosen_rows)
    request_ids = jnp.arange(total_reqs, dtype=jnp.int32)
    mine = choose_rows(wanted[:, None] == request_ids[None, :], all_rows)
    mine, received = lax.optimization_barrier((mine, received))
    heads_here = spread(mine, TP).reshape(share, columns, chosen_rows, head_size)
    cached = jnp.transpose(heads_here, (0, 2, 1, 3)).reshape(group_reqs, columns, head_size)
    query_head_list = cached[:, :heads].reshape(group_reqs, kv_heads, per_group, head_size)
    incoming_key = cached[:, heads : heads + kv_heads][:, :, None, :]
    incoming_value = cached[:, heads + kv_heads :][:, :, None, :]

    slot_ids = tp_lane * slot_dev + jnp.arange(slot_dev, dtype=jnp.int32)
    written = (slot_ids[None, :] == write_pos[:, None])[:, None, :, None]
    key_rows = jnp.where(written, incoming_key, k_cache)
    value_rows = jnp.where(written, incoming_value, value_cache).astype(F32)
    scores = jnp.einsum(
        "rgqd,rgsd->rgqs", query_head_list, key_rows, preferred_element_type=F32
    ) * head_size ** (-0.5)
    is_valid = (slot_ids[None, :] < lengths[:, None])[:, None, None, :]
    masked = jnp.where(is_valid, scores, -1e30)
    local_peak = jnp.max(masked, axis=-1)
    weights = jnp.where(is_valid, jnp.exp(masked - local_peak[..., None]), 0.0)
    local_total = jnp.sum(weights, axis=-1)
    local_mixed = jnp.einsum("rgqs,rgsd->rgqd", weights, value_rows, precision=HIGHEST)

    def lane_row(values):
        row = jnp.concatenate(pieces_of(values.reshape(group_reqs, heads)), axis=1)
        return jnp.pad(row, ((0, 0), (0, head_size - row.shape[1])))[:, None, :]

    parts = jnp.concatenate(
        [
            local_mixed.reshape(group_reqs, heads, head_size).astype(BF16),
            lane_row(local_peak),
            lane_row(local_total),
            jnp.zeros((group_reqs, 2, head_size), BF16),
        ],
        axis=1,
    )
    gathered = swap(parts, TP)
    tail = gathered[:, heads : heads + 2, : 3 * heads].astype(F32)
    tail = tail[..., :heads] + tail[..., heads : 2 * heads] + tail[..., 2 * heads :]
    peaks, totals = tail[:, 0], tail[:, 1]
    scale = jnp.exp(peaks - jnp.max(peaks, axis=0, keepdims=True))
    total = jnp.sum(scale * totals, axis=0)
    mixed = jnp.sum(scale[:, :, None] * gathered[:, :heads].astype(F32), axis=0)
    attention_row = (mixed / total[:, None]).astype(BF16)

    attention = spread(attention_row, "x").reshape(posts, width)
    projected = contract_rows(attention, out_rows).astype(BF16)
    post_columns = projected.shape[1]
    all_projected = spread(projected, "dp").reshape(dp_size * posts, post_columns)
    line_rows = placing.reshape(dp_size, lines, posts)
    line_rows = lax.dynamic_slice_in_dim(line_rows, line, 1, axis=1).reshape(1, dp_size * posts)
    home_ids = dp_group * group_reqs + jnp.arange(group_reqs, dtype=jnp.int32)
    at_home = choose_rows(home_ids[:, None] == line_rows, all_projected)
    from_lanes = swap(at_home.reshape(tp_size, post_columns // head_size, head_size), TP)
    from_lanes = from_lanes.reshape(lines, posts, post_columns).astype(F32)
    proj_home = jnp.sum(from_lanes, axis=0).reshape(posts, lines, post_columns // lines)
    proj_home = jnp.transpose(proj_home, (1, 0, 2)).reshape(1, width)
    hidden_f32 = (resid_dec.astype(F32) + proj_home).astype(BF16).astype(F32)

    pre_out = expert_units(received.reshape(experts * capacity, width), units)
    normed_dec = rms(hidden_f32, moe_gain)
    dec_rows = jnp.where(routed[pre_rows][:, None], normed_dec, no_value)
    group_rows = swap(dec_rows.reshape(experts, heads, head_size), TP).reshape(group_reqs, width)
    dec_out = expert_units(group_rows, units)
    last = (slots == capacity - 1)[None, :, None]
    pre_out = pre_out.reshape(experts, capacity, width)
    outbound = jnp.where(last, pre_out + dec_out[:, None, :], pre_out)
    returned = swap(outbound, TP)
    flat_back = returned.reshape(experts * capacity, width)
    high, middle, low = pieces_of(weight_of)

    def mix(piece):
        table = jnp.where(pick, piece[:, :, None], no_value)
        return jnp.dot(
            table.reshape(rows_dev, experts * capacity), flat_back, preferred_element_type=F32
        )

    mixture = mix(high) + mix(middle) + mix(low)
    out_pre = (x_f32 + mixture[:pre_rows]).astype(BF16)
    out_dec = (hidden_f32 + mixture[pre_rows:]).astype(BF16)
    return (out_pre, out_dec)


def solution(mesh):
    groups, lanes = mesh.devices.shape
    fine = Mesh(mesh.devices.reshape(groups, 8, lanes // 8), ("dp", "y", "x"))
    rows = P(("dp", "y", "x"), None)
    units = P(TP, "dp", None)
    cache = P("dp", None, TP, None)
    placed = (rows, rows, rows, P(), P("dp"), P("dp"), cache, cache, P(None, TP))
    placed = placed + (rows, rows, rows, P(), units, units, units)
    return jax.shard_map(
        on_device, mesh=fine, in_specs=placed, out_specs=(rows, rows), check_vma=False
    )
```

time: 261 us -> 243 us (0.931)
  the two profiles are of different devices: /device:TPU:16 before, /device:TPU:2 now
where the time goes in v3:
time: 243 us; the launch traced here: 242 us
  waiting for transfers between devices  95.9 us (39%)
  starting transfers between devices  55.3 us (23%)
  blocking collectives  37.3 us (15%)
  matrix products  25.3 us (10%)
  between operations  15.2 us (6%)
  other arithmetic  8.01 us (3%)
  local copies, waits for them, and re-layouts  4.64 us (2%)
    all_to_all x8, waiting for transfers between devices, swap(): lax.all_to_all(blocks, axis_name, split_axis=0, concat_axis=0, tiled=True)  95.1 us
    all_to_all x8, starting transfers between devices, swap(): lax.all_to_all(blocks, axis_name, split_axis=0, concat_axis=0, tiled=True)  55.2 us
    all_gather x1, blocking collectives, on_device(): lax.all_gather(by_head.reshape(tp_size, head_size), 'dp', axis=0, tiled=T...  23.5 us
    all_to_all x1, blocking collectives, swap(): lax.all_to_all(blocks, axis_name, split_axis=0, concat_axis=0, tiled=True)  13.8 us
    dot_general x2, matrix products, expert_units(): return jnp.dot(active, units[2], preferred_element_type=F32).astype(BF16)  9.92 us
    dot_general x3, matrix products, contract_rows(): lax.dot_general(left_rows, unit_rows, (((1,), (1,)), ((), ())), preferred...  8.37 us
  transfers between devices with their start and end apart: 10, of which 7 were waited for; matrix products, arithmetic and copies ran while one was open for 11% of the time, Pallas kernels for 0%

profile of v3, /device:TPU:2, one launch (start us, length us, event | category | flops | bytes accessed | tf_op | source)
XLA Modules:
  0.0 241.5 jit_solution(16130079277603761448)
XLA Ops:
  7.2 0.7 all-gather.6.cloned.1.call-update
  8.0 1.9 pad_maximum_fusion
  9.9 0.7 maximum_reduce_fusion
  10.6 0.6 copy.96
  11.3 10.2 %all-to-all-start = ((bf16[32,1,128]{2,1,0:T(2,128)(2,1)}), bf16[32,1,128]{2,1,0:T(2,128)(2,1)S(1)}, u32[]{:S(2)}, u32[]{:S(2)}) async-start(bf16[32,1,128]{2,1,0:T(2,128)(2,1)} %copy.96), calls=%async_computation | async-start | bytes 32768 | tf_op jit(solution)/shard_map/all_to_all | solution.py:20
  21.6 0.1 fusion.18
  21.7 0.1 fusion.10
  21.9 1.8 convolution_convert_fusion.1
  23.8 6.2 %all-to-all-done = bf16[32,1,128]{2,1,0:T(2,128)(2,1)S(1)} async-done(((bf16[32,1,128]{2,1,0:T(2,128)(2,1)}), bf16[32,1,128]{2,1,0:T(2,128)(2,1)S(1)}, u32[]{:S(2)}, u32[]{:S(2)}) %all-to-all-start) | async-done | bytes 8224 | tf_op jit(solution)/shard_map/all_to_all | solution.py:20
  30.0 5.2 %all-to-all-start.1 = ((bf16[32,16,1536]{2,1,0:T(8,128)(2,1)}), bf16[32,16,1536]{2,1,0:T(8,128)(2,1)S(1)}, u32[]{:S(2)}, u32[]{:S(2)}) async-start(bf16[32,16,1536]{2,1,0:T(8,128)(2,1)} %bitcast.3), calls=%async_computation.1 | async-start | bytes 3145728 | tf_op jit(solution)/shard_map/all_to_all | solution.py:20
  35.3 23.5 %all-gather = bf16[512,1,128]{2,0,1:T(8,128)(2,1)S(1)} all-gather(bf16[32,1,128]{2,0,1:T(8,128)(2,1)S(1)} %copy.97), channel_id=2, replica_groups=mesh['dp'=16,'y'=8,'x'=4] {'dp'}, dimensions={0}, use_global_device_ids=true | all-gather | bytes 139264 | tf_op jit(solution)/shard_map/all_gather | solution.py:122
  58.8 0.2 convolution_convert_fusion.6
  59.0 22.2 %all-to-all-done.1 = bf16[32,16,1536]{2,1,0:T(8,128)(2,1)S(1)} async-done(((bf16[32,16,1536]{2,1,0:T(8,128)(2,1)}), bf16[32,16,1536]{2,1,0:T(8,128)(2,1)S(1)}, u32[]{:S(2)}, u32[]{:S(2)}) %all-to-all-start.1) | async-done | bytes 1572896 | tf_op jit(solution)/shard_map/all_to_all | solution.py:20
  81.1 0.7 broadcast_in_dim.207
  81.8 6.4 %all-to-all-start.2 = ((bf16[32,16,128]{2,1,0:T(8,128)(2,1)}), bf16[32,16,128]{2,1,0:T(8,128)(2,1)S(1)}, u32[]{:S(2)}, u32[]{:S(2)}) async-start(bf16[32,16,128]{2,1,0:T(8,128)(2,1)} %broadcast_in_dim.207), calls=%async_computation.2 | async-start | bytes 262144 | tf_op jit(solution)/shard_map/all_to_all | solution.py:20
  88.4 8.7 %all-to-all-done.2 = bf16[32,16,128]{2,1,0:T(8,128)(2,1)S(1)} async-done(((bf16[32,16,128]{2,1,0:T(8,128)(2,1)}), bf16[32,16,128]{2,1,0:T(8,128)(2,1)S(1)}, u32[]{:S(2)}, u32[]{:S(2)}) %all-to-all-start.2) | async-done | bytes 131104 | tf_op jit(solution)/shard_map/all_to_all | solution.py:20
  97.3 1.1 fusion.71
  98.5 0.3 fusion.23
  99.1 2.3 convolution_convert_fusion.3
  101.6 13.8 %all_to_all.45 = bf16[32,16,128]{2,1,0:T(8,128)(2,1)S(1)} all-to-all(bf16[32,16,128]{2,1,0:T(8,128)(2,1)S(1)} %copy.106), channel_id=1, replica_groups=mesh['dp'=16,'y'=8,'x'=4] {'y','x'}, dimensions={0} | all-to-all | bytes 262144 | tf_op jit(solution)/shard_map/all_to_all | solution.py:20
  115.6 0.1 multiply_reduce_fusion
  115.9 0.6 broadcast_in_dim.216
  116.5 5.1 %all-to-all-start.4 = ((bf16[4,12,128]{2,1,0:T(8,128)(2,1)}), bf16[4,12,128]{2,1,0:T(8,128)(2,1)S(1)}, u32[]{:S(2)}, u32[]{:S(2)}) async-start(bf16[4,12,128]{2,1,0:T(8,128)(2,1)} %broadcast_in_dim.216), calls=%async_computation.4 | async-start | bytes 32768 | tf_op jit(solution)/shard_map/all_to_all | solution.py:20
  121.6 0.2 slice_reduce_fusion
  122.1 3.5 %all-to-all-done.4 = bf16[4,12,128]{2,1,0:T(8,128)(2,1)S(1)} async-done(((bf16[4,12,128]{2,1,0:T(8,128)(2,1)}), bf16[4,12,128]{2,1,0:T(8,128)(2,1)S(1)}, u32[]{:S(2)}, u32[]{:S(2)}) %all-to-all-start.4) | async-done | bytes 12320 | tf_op jit(solution)/shard_map/all_to_all | solution.py:20
  125.5 1.7 convolution_convert_fusion.7
  127.2 0.7 broadcast_in_dim.217
  127.9 8.3 %all-to-all-start.5 = ((bf16[16,4,384]{2,1,0:T(4,128)(2,1)}), bf16[16,4,384]{2,1,0:T(4,128)(2,1)S(1)}, u32[]{:S(2)}, u32[]{:S(2)}) async-start(bf16[16,4,384]{2,1,0:T(4,128)(2,1)} %broadcast_in_dim.217), calls=%async_computation.5 | async-start | bytes 98304 | tf_op jit(solution)/shard_map/all_to_all | solution.py:20
  136.2 7.7 %all-to-all-done.5 = bf16[16,4,384]{2,1,0:T(4,128)(2,1)S(1)} async-done(((bf16[16,4,384]{2,1,0:T(4,128)(2,1)}), bf16[16,4,384]{2,1,0:T(4,128)(2,1)S(1)}, u32[]{:S(2)}, u32[]{:S(2)}) %all-to-all-start.5) | async-done | bytes 49184 | tf_op jit(solution)/shard_map/all_to_all | solution.py:20
  143.9 0.2 convolution_convert_fusion.4
  144.1 0.6 reshape.240
  144.7 5.0 %all-to-all-start.6 = ((bf16[32,3,128]{2,1,0:T(4,128)(2,1)}), bf16[32,3,128]{2,1,0:T(4,128)(2,1)S(1)}, u32[]{:S(2)}, u32[]{:S(2)}) async-start(bf16[32,3,128]{2,1,0:T(4,128)(2,1)} %reshape.240), calls=%async_computation.6 | async-start | bytes 65536 | tf_op jit(solution)/shard_map/all_to_all | solution.py:20
  149.7 8.7 %all-to-all-done.6 = bf16[32,3,128]{2,1,0:T(4,128)(2,1)S(1)} async-done(((bf16[32,3,128]{2,1,0:T(4,128)(2,1)}), bf16[32,3,128]{2,1,0:T(4,128)(2,1)S(1)}, u32[]{:S(2)}, u32[]{:S(2)}) %all-to-all-start.6) | async-done | bytes 24608 | tf_op jit(solution)/shard_map/all_to_all | solution.py:20
  158.7 0.6 multiply_reduce_fusion.2
  160.1 0.8 broadcast_select_fusion
  160.8 4.9 %all-to-all-start.7 = ((bf16[32,12,128]{2,1,0:T(8,128)(2,1)}), bf16[32,12,128]{2,1,0:T(8,128)(2,1)S(1)}, u32[]{:S(2)}, u32[]{:S(2)}) async-start(bf16[32,12,128]{2,1,0:T(8,128)(2,1)} %broadcast_select_fusion), calls=%async_computation.7 | async-start | bytes 262144 | tf_op jit(solution)/shard_map/all_to_all | solution.py:20
  165.8 4.3 %fusion.3 = f32[512,768]{1,0:T(8,128)} fusion(bf16[512,1536]{1,0:T(8,128)(2,1)S(1)} %bitcast.86, bf16[3,768,1536]{2,1,0:T(8,128)(2,1)} %all-gather.4.cloned.1.call-done), kind=kOutput, calls=%fused_computation.13 | convolution fusion | flops 1207959552 | bytes 5505024 | tf_op jit(solution)/shard_map/dot_general | solution.py:14
  170.0 6.0 %convolution_convert_fusion = bf16[512,1536]{1,0:T(8,128)(2,1)S(1)} fusion(bf16[3,768,1536]{2,1,0:T(8,128)(2,1)} %all-gather.4.cloned.1.call-done, f32[512,768]{1,0:T(8,128)} %fusion.3, bf16[512,1536]{1,0:T(8,128)(2,1)S(1)} %bitcast.87), kind=kOutput, calls=%fused_computation | convolution fusion | flops 2417885184 | bytes 9437184 | tf_op jit(solution)/shard_map/dot_general | solution.py:48
  176.1 2.4 fusion.8
  178.5 3.9 %convolution_convert_fusion.2 = bf16[32,1536]{1,0:T(8,128)(2,1)S(1)} fusion(bf16[3,768,1536]{2,1,0:T(8,128)(2,1)} %all-gather.4.cloned.1.call-done, f32[32,768]{1,0:T(8,128)S(1)} %fusion.8, bf16[4,8,12,128]{3,2,1,0:T(8,128)(2,1)S(1)} %bitcast.98), kind=kOutput, calls=%fused_computation.11 | convolution fusion | flops 151093248 | bytes 5013504 | tf_op jit(solution)/shard_map/dot_general | solution.py:48
  182.4 1.4 add_select_fusion
  183.8 10.0 %all-to-all-start.8 = ((bf16[32,16,1536]{2,1,0:T(8,128)(2,1)}), bf16[32,16,1536]{2,1,0:T(8,128)(2,1)S(1)}, u32[]{:S(2)}, u32[]{:S(2)}) async-start(bf16[32,16,1536]{2,1,0:T(8,128)(2,1)} %add_select_fusion), calls=%async_computation.8 | async-start | bytes 3145728 | tf_op jit(solution)/shard_map/all_to_all | solution.py:20
  193.9 38.2 %all-to-all-done.8 = bf16[32,16,1536]{2,1,0:T(8,128)(2,1)S(1)} async-done(((bf16[32,16,1536]{2,1,0:T(8,128)(2,1)}), bf16[32,16,1536]{2,1,0:T(8,128)(2,1)S(1)}, u32[]{:S(2)}, u32[]{:S(2)}) %all-to-all-start.8) | async-done | bytes 1572896 | tf_op jit(solution)/shard_map/all_to_all | solution.py:20
  232.1 0.4 convolution_bitcast_fusion.2
  232.5 0.4 fusion.1
  233.0 0.4 fusion
  233.4 0.7 fusion.21
  234.1 0.6 fusion.60
  (74 shorter events, 2.1 us)
Async XLA Ops:
  7.2 14.4 %copy-start.3 = (s32[64,4]{0,1:T(4,128)S(1)}, s32[64,4]{0,1:T(4,128)}, u32[]{:S(2)}) copy-start(s32[64,4]{0,1:T(4,128)} %param.26) | copy-start | bytes 3076
  7.2 14.4 %copy-start = (bf16[63,1536]{1,0:T(8,128)(2,1)S(1)}, bf16[63,1536]{1,0:T(8,128)(2,1)}, u32[]{:S(2)}) copy-start(bf16[63,1536]{1,0:T(8,128)(2,1)} %param.25) | copy-start | bytes 580612
  7.2 14.7 %copy-start.2 = (f32[1536]{0:T(1024)S(1)}, f32[1536]{0:T(1024)}, u32[]{:S(2)}) copy-start(f32[1536]{0:T(1024)} %param.28) | copy-start | bytes 18436
  7.2 114.9 %all-gather.6.cloned.1.call-start = ((), (), s32[]{:S(2)}) async-start(), calls=%async_computation.10 | async-start | bytes 1327104 | tf_op jit(solution)/shard_map/all_gather | solution.py:83
  7.9 157.8 %all-gather.4.cloned.1.call-start = ((), (), s32[]{:S(2)}) async-start(), calls=%async_computation.9 | async-start | bytes 7520256 | tf_op jit(solution)/shard_map/all_gather | solution.py:84
  11.3 18.7 %all-to-all-start = ((bf16[32,1,128]{2,1,0:T(2,128)(2,1)}), bf16[32,1,128]{2,1,0:T(2,128)(2,1)S(1)}, u32[]{:S(2)}, u32[]{:S(2)}) async-start(bf16[32,1,128]{2,1,0:T(2,128)(2,1)} %copy.96), calls=%async_computation | async-start | bytes 32768 | tf_op jit(solution)/shard_map/all_to_all | solution.py:20
  30.0 5.3 %copy-start.5 = (s32[512]{0:T(512)S(1)}, s32[512]{0:T(512)}, u32[]{:S(2)}) copy-start(s32[512]{0:T(512)} %param.19) | copy-start | bytes 6148
  30.0 58.4 %copy-start.6 = (s32[32]{0:T(128)S(1)}, s32[32]{0:T(128)}, u32[]{:S(2)}) copy-start(s32[32]{0:T(128)} %param.20) | copy-start | bytes 388
  30.0 58.4 %copy-start.7 = (s32[32]{0:T(128)S(1)}, s32[32]{0:T(128)}, u32[]{:S(2)}) copy-start(s32[32]{0:T(128)} %param.21) | copy-start | bytes 388
  30.0 67.3 %copy-start.8 = (bf16[32,2,64,128]{3,2,1,0:T(8,128)(2,1)S(1)}, bf16[32,2,64,128]{3,2,1,0:T(8,128)(2,1)}, u32[]{:S(2)}) copy-start(bf16[32,2,64,128]{3,2,1,0:T(8,128)(2,1)} %param.22) | copy-start | bytes 3145732
  30.0 51.2 %all-to-all-start.1 = ((bf16[32,16,1536]{2,1,0:T(8,128)(2,1)}), bf16[32,16,1536]{2,1,0:T(8,128)(2,1)S(1)}, u32[]{:S(2)}, u32[]{:S(2)}) async-start(bf16[32,16,1536]{2,1,0:T(8,128)(2,1)} %bitcast.3), calls=%async_computation.1 | async-start | bytes 3145728 | tf_op jit(solution)/shard_map/all_to_all | solution.py:20
  81.8 15.3 %all-to-all-start.2 = ((bf16[32,16,128]{2,1,0:T(8,128)(2,1)}), bf16[32,16,128]{2,1,0:T(8,128)(2,1)S(1)}, u32[]{:S(2)}, u32[]{:S(2)}) async-start(bf16[32,16,128]{2,1,0:T(8,128)(2,1)} %broadcast_in_dim.207), calls=%async_computation.2 | async-start | bytes 262144 | tf_op jit(solution)/shard_map/all_to_all | solution.py:20
  101.5 57.2 %copy-start.1 = (bf16[1,1536]{1,0:T(2,128)(2,1)S(1)}, bf16[1,1536]{1,0:T(2,128)(2,1)}, u32[]{:S(2)}) copy-start(bf16[1,1536]{1,0:T(2,128)(2,1)} %param.18) | copy-start | bytes 9220
  116.5 9.0 %all-to-all-start.4 = ((bf16[4,12,128]{2,1,0:T(8,128)(2,1)}), bf16[4,12,128]{2,1,0:T(8,128)(2,1)S(1)}, u32[]{:S(2)}, u32[]{:S(2)}) async-start(bf16[4,12,128]{2,1,0:T(8,128)(2,1)} %broadcast_in_dim.216), calls=%async_computation.4 | async-start | bytes 32768 | tf_op jit(solution)/shard_map/all_to_all | solution.py:20
  127.9 16.0 %all-to-all-start.5 = ((bf16[16,4,384]{2,1,0:T(4,128)(2,1)}), bf16[16,4,384]{2,1,0:T(4,128)(2,1)S(1)}, u32[]{:S(2)}, u32[]{:S(2)}) async-start(bf16[16,4,384]{2,1,0:T(4,128)(2,1)} %broadcast_in_dim.217), calls=%async_computation.5 | async-start | bytes 98304 | tf_op jit(solution)/shard_map/all_to_all | solution.py:20
  144.7 13.7 %all-to-all-start.6 = ((bf16[32,3,128]{2,1,0:T(4,128)(2,1)}), bf16[32,3,128]{2,1,0:T(4,128)(2,1)S(1)}, u32[]{:S(2)}, u32[]{:S(2)}) async-start(bf16[32,3,128]{2,1,0:T(4,128)(2,1)} %reshape.240), calls=%async_computation.6 | async-start | bytes 65536 | tf_op jit(solution)/shard_map/all_to_all | solution.py:20
  160.8 15.2 %all-to-all-start.7 = ((bf16[32,12,128]{2,1,0:T(8,128)(2,1)}), bf16[32,12,128]{2,1,0:T(8,128)(2,1)S(1)}, u32[]{:S(2)}, u32[]{:S(2)}) async-start(bf16[32,12,128]{2,1,0:T(8,128)(2,1)} %broadcast_select_fusion), calls=%async_computation.7 | async-start | bytes 262144 | tf_op jit(solution)/shard_map/all_to_all | solution.py:20
  183.8 10.0 %copy-start.4 = (f32[64,4]{0,1:T(4,128)S(1)}, f32[64,4]{0,1:T(4,128)}, u32[]{:S(2)}) copy-start(f32[64,4]{0,1:T(4,128)} %param.27) | copy-start | bytes 3076
  183.8 48.3 %all-to-all-start.8 = ((bf16[32,16,1536]{2,1,0:T(8,128)(2,1)}), bf16[32,16,1536]{2,1,0:T(8,128)(2,1)S(1)}, u32[]{:S(2)}, u32[]{:S(2)}) async-start(bf16[32,16,1536]{2,1,0:T(8,128)(2,1)} %add_select_fusion), calls=%async_computation.8 | async-start | bytes 3145728 | tf_op jit(solution)/shard_map/all_to_all | solution.py:20
Sparse Core Ops, SparseCore 0:
  10.1 56.8 all-gather.5
  69.1 51.4 all-gather.3

commit v4 on v3

--- a/solution.py
+++ b/solution.py
@@ -1,3 +1,5 @@
+import math
+
 import jax
 import jax.numpy as jnp
 from jax import lax
@@ -80,10 +82,12 @@
     experts = tp_size * w_gate.shape[0]
     assert group_reqs == tp_size and experts == tp_size
 
-    out_rows = lax.all_gather(w_out.T, "y", axis=0, tiled=True)
-    units = lax.all_gather(
-        jnp.concatenate([w_gate, w_up, w_down], axis=0), "dp", axis=1, tiled=True
-    )
+    turned = [
+        (group * lines + other, (other + group // lines * lines) * lines + group % lines)
+        for group in range(dp_size)
+        for other in range(lines)
+    ]
+    line_columns = lax.ppermute(w_out.T, ("dp", "y"), turned)
 
     no_value = jnp.zeros((), BF16)
     rows_dev, top_count = routes.shape
@@ -93,40 +97,48 @@
     expert_ids = jnp.arange(experts, dtype=jnp.int32)
     hits = routes[:, :, None] == expert_ids[None, None, :]
     weight_of = jnp.sum(jnp.where(hits, route_weight[:, :, None], 0.0), axis=1)
-    routed = jnp.any(hits, axis=1)
-
-    row_ids = jnp.arange(rows_dev, dtype=jnp.int32)
+
+    routed = jnp.any(hits[:pre_rows], axis=1)
+    row_ids = jnp.arange(pre_rows, dtype=jnp.int32)
     before = (row_ids[None, :] < row_ids[:, None]).astype(BF16)
     position = jnp.dot(before, routed.astype(BF16), preferred_element_type=F32).astype(jnp.int32)
-    position = jnp.where(row_ids[:, None] == pre_rows, capacity - 1, position)
     slots = jnp.arange(capacity, dtype=jnp.int32)
     pick = routed[:, :, None] & (position[:, :, None] == slots[None, None, :])
-    pick_table = pick.reshape(rows_dev, experts * capacity)
+    pick_table = pick.reshape(pre_rows, experts * capacity)
     x_f32 = x_pre.astype(F32)
     outgoing = lax.dot_general(
-        pick_table[:pre_rows].astype(BF16),
+        pick_table.astype(BF16),
         rms(x_f32, moe_gain),
         (((0,), (0,)), ((), ())),
         preferred_element_type=F32,
     ).astype(BF16)
 
+    line_columns, outgoing = lax.optimization_barrier((line_columns, outgoing))
+    units = lax.all_gather(
+        jnp.concatenate([w_gate, w_up, w_down, line_columns[None]], axis=0),
+        "dp",
+        axis=1,
+        tiled=True,
+    )
+    out_rows = units[3, : lines * w_out.shape[1]]
+
     columns = heads + 2 * kv_heads
-    share = tp_size // columns
-    chosen_rows = group_reqs // share
-    fresh = jnp.concatenate([q_new, new_key_value], axis=1).reshape(1, columns, 1, head_size)
-    by_head = swap(
-        jnp.broadcast_to(fresh, (share, columns, 1, head_size)).reshape(tp_size, 1, head_size), TP
-    )
-    by_head, outgoing = lax.optimization_barrier((by_head, outgoing))
+    share = columns * head_size // posts
+    post = lax.axis_index("x")
+    fresh = jnp.concatenate([q_new, new_key_value], axis=1)
+    fresh, outgoing = lax.optimization_barrier((fresh, outgoing))
     received = swap(outgoing.reshape(experts, capacity, width), TP)
-    all_rows = lax.all_gather(by_head.reshape(tp_size, head_size), "dp", axis=0, tiled=True)
-    first_row = dp_group * group_reqs + (tp_lane // columns) * chosen_rows
-    wanted = lax.dynamic_slice_in_dim(placing, first_row, chosen_rows)
-    request_ids = jnp.arange(total_reqs, dtype=jnp.int32)
-    mine = choose_rows(wanted[:, None] == request_ids[None, :], all_rows)
+    line_fresh = lax.all_gather(fresh, "x", axis=0, tiled=True)
+    line_share = lax.dynamic_slice_in_dim(line_fresh, post * share, share, axis=1)
+    all_rows = lax.all_gather(line_share, "dp", axis=0, tiled=True)
+    wanted = lax.dynamic_slice_in_dim(placing, dp_group * group_reqs, group_reqs)
+    held = jnp.arange(dp_size, dtype=jnp.int32)[:, None] * tp_size + line * posts
+    held = (held + jnp.arange(posts, dtype=jnp.int32)[None, :]).reshape(1, dp_size * posts)
+    mine = choose_rows(wanted[:, None] == held, all_rows)
     mine, received = lax.optimization_barrier((mine, received))
-    heads_here = spread(mine, TP).reshape(share, columns, chosen_rows, head_size)
-    cached = jnp.transpose(heads_here, (0, 2, 1, 3)).reshape(group_reqs, columns, head_size)
+    chosen = jnp.sum(spread(mine, "y").astype(F32), axis=0).astype(BF16)
+    cached = spread(chosen, "x").reshape(posts, group_reqs, columns // posts, head_size)
+    cached = jnp.transpose(cached, (1, 0, 2, 3)).reshape(group_reqs, columns, head_size)
     query_head_list = cached[:, :heads].reshape(group_reqs, kv_heads, per_group, head_size)
     incoming_key = cached[:, heads : heads + kv_heads][:, :, None, :]
     incoming_value = cached[:, heads + kv_heads :][:, :, None, :]
@@ -159,6 +171,11 @@
         axis=1,
     )
     gathered = swap(parts, TP)
+
+    pre_out = expert_units(received.reshape(experts * capacity, width), units)
+    gathered, pre_out = lax.optimization_barrier((gathered, pre_out))
+    returned = swap(pre_out.reshape(experts, capacity, width), TP)
+
     tail = gathered[:, heads : heads + 2, : 3 * heads].astype(F32)
     tail = tail[..., :heads] + tail[..., heads : 2 * heads] + tail[..., 2 * heads :]
     peaks, totals = tail[:, 0], tail[:, 1]
@@ -167,47 +184,46 @@
     mixed = jnp.sum(scale[:, :, None] * gathered[:, :heads].astype(F32), axis=0)
     attention_row = (mixed / total[:, None]).astype(BF16)
 
-    attention = spread(attention_row, "x").reshape(posts, width)
+    attention = lax.all_gather(attention_row.reshape(1, width), "x", axis=0, tiled=True)
     projected = contract_rows(attention, out_rows).astype(BF16)
     post_columns = projected.shape[1]
-    all_projected = spread(projected, "dp").reshape(dp_size * posts, post_columns)
+    all_projected = lax.all_gather(projected, "dp", axis=0, tiled=True)
     line_rows = placing.reshape(dp_size, lines, posts)
     line_rows = lax.dynamic_slice_in_dim(line_rows, line, 1, axis=1).reshape(1, dp_size * posts)
     home_ids = dp_group * group_reqs + jnp.arange(group_reqs, dtype=jnp.int32)
     at_home = choose_rows(home_ids[:, None] == line_rows, all_projected)
-    from_lanes = swap(at_home.reshape(tp_size, post_columns // head_size, head_size), TP)
+    at_home, returned = lax.optimization_barrier((at_home, returned))
+    from_lanes = swap(at_home.reshape(tp_size, -1, math.gcd(post_columns, head_size)), TP)
     from_lanes = from_lanes.reshape(lines, posts, post_columns).astype(F32)
     proj_home = jnp.sum(from_lanes, axis=0).reshape(posts, lines, post_columns // lines)
     proj_home = jnp.transpose(proj_home, (1, 0, 2)).reshape(1, width)
     hidden_f32 = (resid_dec.astype(F32) + proj_home).astype(BF16).astype(F32)
 
-    pre_out = expert_units(received.reshape(experts * capacity, width), units)
     normed_dec = rms(hidden_f32, moe_gain)
-    dec_rows = jnp.where(routed[pre_rows][:, None], normed_dec, no_value)
-    group_rows = swap(dec_rows.reshape(experts, heads, head_size), TP).reshape(group_reqs, width)
+    group_rows = spread(normed_dec.reshape(heads, head_size), TP).reshape(group_reqs, width)
     dec_out = expert_units(group_rows, units)
-    last = (slots == capacity - 1)[None, :, None]
-    pre_out = pre_out.reshape(experts, capacity, width)
-    outbound = jnp.where(last, pre_out + dec_out[:, None, :], pre_out)
-    returned = swap(outbound, TP)
+    dec_back = swap(dec_out.reshape(group_reqs, heads, head_size), TP).astype(F32)
+    dec_weight = weight_of[pre_rows:].reshape(experts, 1, 1)
+    dec_mixture = jnp.sum(dec_weight * dec_back, axis=0).reshape(1, width)
+    out_dec = (hidden_f32 + dec_mixture).astype(BF16)
+
     flat_back = returned.reshape(experts * capacity, width)
-    high, middle, low = pieces_of(weight_of)
+    high, middle, low = pieces_of(weight_of[:pre_rows])
 
     def mix(piece):
         table = jnp.where(pick, piece[:, :, None], no_value)
         return jnp.dot(
-            table.reshape(rows_dev, experts * capacity), flat_back, preferred_element_type=F32
+            table.reshape(pre_rows, experts * capacity), flat_back, preferred_element_type=F32
         )
 
-    mixture = mix(high) + mix(middle) + mix(low)
-    out_pre = (x_f32 + mixture[:pre_rows]).astype(BF16)
-    out_dec = (hidden_f32 + mixture[pre_rows:]).astype(BF16)
+    out_pre = (x_f32 + (mix(high) + mix(middle) + mix(low))).astype(BF16)
     return (out_pre, out_dec)
 
 
 def solution(mesh):
     groups, lanes = mesh.devices.shape
-    fine = Mesh(mesh.devices.reshape(groups, 8, lanes // 8), ("dp", "y", "x"))
+    lines = min(8, groups)
+    fine = Mesh(mesh.devices.reshape(groups, lines, lanes // lines), ("dp", "y", "x"))
     rows = P(("dp", "y", "x"), None)
     units = P(TP, "dp", None)
     cache = P("dp", None, TP, None)

time: 243 us -> 234 us (0.963)
  the two profiles are of different devices: /device:TPU:2 before, /device:TPU:8 now
where the time goes in v4:
time: 234 us; the launch traced here: 232 us
  starting transfers between devices  68 us (29%)
  blocking collectives  66.4 us (28%)
  waiting for transfers between devices  45.2 us (19%)
  matrix products  26.4 us (11%)
  between operations  15.3 us (7%)
  local copies, waits for them, and re-layouts  5.79 us (2%)
  other arithmetic  5.31 us (2%)
    all_to_all x8, starting transfers between devices, swap(): lax.all_to_all(blocks, axis_name, split_axis=0, concat_axis=0, tiled=True)  65.9 us
    all_to_all x8, waiting for transfers between devices, swap(): lax.all_to_all(blocks, axis_name, split_axis=0, concat_axis=0, tiled=True)  45.2 us
    all_gather x1, blocking collectives, on_device(): all_projected = lax.all_gather(projected, 'dp', axis=0, tiled=True)  21.5 us
    all_gather x1, blocking collectives, on_device(): all_rows = lax.all_gather(line_share, 'dp', axis=0, tiled=True)  20.3 us
    all_gather x1, blocking collectives, on_device(): line_fresh = lax.all_gather(fresh, 'x', axis=0, tiled=True)  12.4 us
    all_gather x1, blocking collectives, on_device(): lax.all_gather(attention_row.reshape(1, width), 'x', axis=0, tiled=True)  12.2 us
    dot_general x2, matrix products, expert_units(): return jnp.dot(active, units[2], preferred_element_type=F32).astype(BF16)  10.6 us
    dot_general x3, matrix products, contract_rows(): lax.dot_general(left_rows, unit_rows, (((1,), (1,)), ((), ())), preferred...  7.18 us
  transfers between devices with their start and end apart: 10, of which 7 were waited for; matrix products, arithmetic and copies ran while one was open for 11% of the time, Pallas kernels for 0%

profile of v4, /device:TPU:8, one launch (start us, length us, event | category | flops | bytes accessed | tf_op | source)
XLA Modules:
  0.0 232.4 jit_solution(8475087615504868340)
XLA Ops:
  7.2 2.1 collective-permute-start
  9.3 0.7 iota_compare_fusion.1
  10.2 1.1 fusion.22
  11.3 0.1 fusion.29
  11.5 2.7 %convolution_convert_fusion.1 = bf16[512,1536]{1,0:T(8,128)(2,1)} fusion(pred[63,512]{0,1:T(32,128)(4,1)S(1)} %fusion.29, bf16[63,1536]{1,0:T(8,128)(2,1)} %param.25, f32[1536]{0:T(1024)} %param.28, f32[63]{0:T(128)S(1)} %add_rsqrt_fusion), kind=kOutput, calls=%fused_computation.1 | convolution fusion | flops 100263936 | bytes 1805052 | tf_op jit(solution)/shard_map/dot_general | solution.py:109
  14.3 0.9 pad_maximum_fusion
  15.3 22.3 %all-to-all-start = ((bf16[32,16,1536]{2,1,0:T(8,128)(2,1)}), bf16[32,16,1536]{2,1,0:T(8,128)(2,1)S(1)}, u32[]{:S(2)}, u32[]{:S(2)}) async-start(bf16[32,16,1536]{2,1,0:T(8,128)(2,1)} %bitcast.4), calls=%async_computation | async-start | bytes 3145728 | tf_op jit(solution)/shard_map/all_to_all | solution.py:22
  37.8 12.4 %all-gather = bf16[4,1,2048]{2,1,0:T(2,128)(2,1)S(1)} all-gather(bf16[1,1,2048]{2,1,0:T(2,128)(2,1)S(1)} %bitcast.119), channel_id=1, replica_groups=mesh['dp'=16,'y'=8,'x'=4] {'x'}, dimensions={0}, use_global_device_ids=true | all-gather | bytes 20480 | tf_op jit(solution)/shard_map/all_gather | solution.py:131
  50.2 20.3 %all-gather.1 = bf16[16,4,512]{2,1,0:T(4,128)(2,1)S(1)} all-gather(bf16[1,4,512]{2,1,0:T(4,128)(2,1)S(1)} %bitcast.121), channel_id=1, replica_groups=mesh['dp'=16,'y'=8,'x'=4] {'dp'}, dimensions={0}, use_global_device_ids=true | all-gather | bytes 69632 | tf_op jit(solution)/shard_map/all_gather | solution.py:133
  70.6 0.2 convolution_convert_fusion.4
  70.8 2.0 all-to-all-done
  72.7 0.7 broadcast_in_dim.148
  73.5 5.9 %all-to-all-start.1 = ((bf16[8,32,512]{2,1,0:T(8,128)(2,1)}), bf16[8,32,512]{2,1,0:T(8,128)(2,1)S(1)}, u32[]{:S(2)}, u32[]{:S(2)}) async-start(bf16[8,32,512]{2,1,0:T(8,128)(2,1)} %broadcast_in_dim.148), calls=%async_computation.1 | async-start | bytes 524288 | tf_op jit(solution)/shard_map/all_to_all | solution.py:22
  79.3 10.9 %all-to-all-done.1 = bf16[8,32,512]{2,1,0:T(8,128)(2,1)S(1)} async-done(((bf16[8,32,512]{2,1,0:T(8,128)(2,1)}), bf16[8,32,512]{2,1,0:T(8,128)(2,1)S(1)}, u32[]{:S(2)}, u32[]{:S(2)}) %all-to-all-start.1) | async-done | bytes 262176 | tf_op jit(solution)/shard_map/all_to_all | solution.py:22
  90.3 0.7 broadcast_in_dim.149
  91.0 3.3 %all-to-all-start.2 = ((bf16[4,32,512]{2,1,0:T(8,128)(2,1)}), bf16[4,32,512]{2,1,0:T(8,128)(2,1)S(1)}, u32[]{:S(2)}, u32[]{:S(2)}) async-start(bf16[4,32,512]{2,1,0:T(8,128)(2,1)} %broadcast_in_dim.149), calls=%async_computation.2 | async-start | bytes 262144 | tf_op jit(solution)/shard_map/all_to_all | solution.py:22
  94.5 5.8 %all-to-all-done.2 = bf16[4,32,512]{2,1,0:T(8,128)(2,1)S(1)} async-done(((bf16[4,32,512]{2,1,0:T(8,128)(2,1)}), bf16[4,32,512]{2,1,0:T(8,128)(2,1)S(1)}, u32[]{:S(2)}, u32[]{:S(2)}) %all-to-all-start.2) | async-done | bytes 131104 | tf_op jit(solution)/shard_map/all_to_all | solution.py:22
  100.4 1.1 fusion.81
  101.7 2.3 convolution_convert_fusion.3
  104.1 0.3 fusion.30
  104.7 0.7 copy.109
  105.5 5.0 %all-to-all-start.3 = ((bf16[32,16,128]{2,1,0:T(8,128)(2,1)}), bf16[32,16,128]{2,1,0:T(8,128)(2,1)S(1)}, u32[]{:S(2)}, u32[]{:S(2)}) async-start(bf16[32,16,128]{2,1,0:T(8,128)(2,1)} %copy.109), calls=%async_computation.3 | async-start | bytes 262144 | tf_op jit(solution)/shard_map/all_to_all | solution.py:22
  110.5 3.1 %fusion.5 = f32[512,768]{1,0:T(8,128)S(1)} fusion(bf16[512,1536]{1,0:T(8,128)(2,1)S(1)} %bitcast.105, bf16[4,768,1536]{2,1,0:T(8,128)(2,1)} %all-gather.6.cloned.1.call-done), kind=kOutput, calls=%fused_computation.14 | convolution fusion | flops 1207959552 | bytes 5505024 | tf_op jit(solution)/shard_map/dot_general | solution.py:16
  113.6 6.7 %convolution_convert_fusion = bf16[512,1536]{1,0:T(8,128)(2,1)} fusion(bf16[4,768,1536]{2,1,0:T(8,128)(2,1)} %all-gather.6.cloned.1.call-done, f32[512,768]{1,0:T(8,128)S(1)} %fusion.5, bf16[512,1536]{1,0:T(8,128)(2,1)S(1)} %bitcast.106), kind=kOutput, calls=%fused_computation | convolution fusion | flops 2417885184 | bytes 9437184 | tf_op jit(solution)/shard_map/dot_general | solution.py:50
  120.3 10.0 %all-to-all-start.4 = ((bf16[32,16,1536]{2,1,0:T(8,128)(2,1)}), bf16[32,16,1536]{2,1,0:T(8,128)(2,1)S(1)}, u32[]{:S(2)}, u32[]{:S(2)}) async-start(bf16[32,16,1536]{2,1,0:T(8,128)(2,1)} %bitcast.20), calls=%async_computation.4 | async-start | bytes 3145728 | tf_op jit(solution)/shard_map/all_to_all | solution.py:22
  130.6 0.2 slice_reduce_fusion.1
  131.1 0.1 multiply_reduce_fusion.1
  131.3 12.2 %all-gather.2 = bf16[4,1,1536]{2,1,0:T(2,128)(2,1)S(1)} all-gather(bf16[1,1,1536]{2,1,0:T(2,128)(2,1)S(1)} %reshape.242), channel_id=1, replica_groups=mesh['dp'=16,'y'=8,'x'=4] {'x'}, dimensions={0}, use_global_device_ids=true | all-gather | bytes 15360 | tf_op jit(solution)/shard_map/all_gather | solution.py:187
  143.5 1.7 fusion.14
  145.2 21.5 %all-gather.3 = bf16[16,4,384]{2,1,0:T(4,128)(2,1)S(1)} all-gather(bf16[1,4,384]{2,1,0:T(4,128)(2,1)S(1)} %fusion.14), channel_id=1, replica_groups=mesh['dp'=16,'y'=8,'x'=4] {'dp'}, dimensions={0}, use_global_device_ids=true | all-gather | bytes 52224 | tf_op jit(solution)/shard_map/all_gather | solution.py:190
  166.7 0.2 convolution_convert_fusion.5
  166.9 0.4 all-to-all-done.4
  167.4 0.6 reshape.231
  168.0 9.8 %all-to-all-start.5 = ((bf16[32,3,128]{2,1,0:T(4,128)(2,1)}), bf16[32,3,128]{2,1,0:T(4,128)(2,1)S(1)}, u32[]{:S(2)}, u32[]{:S(2)}) async-start(bf16[32,3,128]{2,1,0:T(4,128)(2,1)} %reshape.231), calls=%async_computation.5 | async-start | bytes 65536 | tf_op jit(solution)/shard_map/all_to_all | solution.py:22
  177.8 0.4 convolution_bitcast_fusion.2
  178.2 8.3 %all-to-all-done.5 = bf16[32,3,128]{2,1,0:T(4,128)(2,1)S(1)} async-done(((bf16[32,3,128]{2,1,0:T(4,128)(2,1)}), bf16[32,3,128]{2,1,0:T(4,128)(2,1)S(1)}, u32[]{:S(2)}, u32[]{:S(2)}) %all-to-all-start.5) | async-done | bytes 24608 | tf_op jit(solution)/shard_map/all_to_all | solution.py:22
  186.8 0.6 multiply_reduce_fusion.3
  188.2 0.7 broadcast_in_dim.163
  188.8 4.8 %all-to-all-start.6 = ((bf16[32,12,128]{2,1,0:T(8,128)(2,1)}), bf16[32,12,128]{2,1,0:T(8,128)(2,1)S(1)}, u32[]{:S(2)}, u32[]{:S(2)}) async-start(bf16[32,12,128]{2,1,0:T(8,128)(2,1)} %broadcast_in_dim.163), calls=%async_computation.6 | async-start | bytes 262144 | tf_op jit(solution)/shard_map/all_to_all | solution.py:22
  193.7 0.4 fusion.2
  194.1 9.2 %all-to-all-done.6 = bf16[32,12,128]{2,1,0:T(8,128)(2,1)S(1)} async-done(((bf16[32,12,128]{2,1,0:T(8,128)(2,1)}), bf16[32,12,128]{2,1,0:T(8,128)(2,1)S(1)}, u32[]{:S(2)}, u32[]{:S(2)}) %all-to-all-start.6) | async-done | bytes 98336 | tf_op jit(solution)/shard_map/all_to_all | solution.py:22
  203.3 2.4 %fusion.11 = f32[32,768]{1,0:T(8,128)S(1)} fusion(bf16[4,768,1536]{2,1,0:T(8,128)(2,1)} %all-gather.6.cloned.1.call-done, bf16[4,8,12,128]{3,2,1,0:T(8,128)(2,1)S(1)} %bitcast.114), kind=kOutput, calls=%fused_computation.24 | convolution fusion | flops 75522048 | bytes 2555904 | tf_op jit(solution)/shard_map/dot_general | solution.py:16
  205.7 3.9 %convolution_convert_fusion.2 = bf16[32,1536]{1,0:T(8,128)(2,1)S(1)} fusion(bf16[4,768,1536]{2,1,0:T(8,128)(2,1)} %all-gather.6.cloned.1.call-done, f32[32,768]{1,0:T(8,128)S(1)} %fusion.11, bf16[4,8,12,128]{3,2,1,0:T(8,128)(2,1)S(1)} %bitcast.115), kind=kOutput, calls=%fused_computation.12 | convolution fusion | flops 151093248 | bytes 5013504 | tf_op jit(solution)/shard_map/dot_general | solution.py:50
  209.6 0.7 reshape.235
  210.4 4.8 %all-to-all-start.7 = ((bf16[32,12,128]{2,1,0:T(8,128)(2,1)}), bf16[32,12,128]{2,1,0:T(8,128)(2,1)S(1)}, u32[]{:S(2)}, u32[]{:S(2)}) async-start(bf16[32,12,128]{2,1,0:T(8,128)(2,1)} %reshape.235), calls=%async_computation.7 | async-start | bytes 262144 | tf_op jit(solution)/shard_map/all_to_all | solution.py:22
  215.2 1.1 fusion.3
  216.3 8.5 %all-to-all-done.7 = bf16[32,12,128]{2,1,0:T(8,128)(2,1)S(1)} async-done(((bf16[32,12,128]{2,1,0:T(8,128)(2,1)}), bf16[32,12,128]{2,1,0:T(8,128)(2,1)S(1)}, u32[]{:S(2)}, u32[]{:S(2)}) %all-to-all-start.7) | async-done | bytes 98336 | tf_op jit(solution)/shard_map/all_to_all | solution.py:22
  225.0 0.6 fusion.73
  (93 shorter events, 2.5 us)
Async XLA Ops:
  7.2 7.1 %copy-start.3 = (bf16[1,48,1536]{2,1,0:T(8,128)(2,1)S(1)}, bf16[1,48,1536]{2,1,0:T(8,128)(2,1)}, u32[]{:S(2)}) copy-start(bf16[1,48,1536]{2,1,0:T(8,128)(2,1)} %param.29) | copy-start | bytes 442372
  7.2 7.1 %copy-start.2 = (bf16[1,48,1536]{2,1,0:T(8,128)(2,1)S(1)}, bf16[1,48,1536]{2,1,0:T(8,128)(2,1)}, u32[]{:S(2)}) copy-start(bf16[1,48,1536]{2,1,0:T(8,128)(2,1)} %param.30) | copy-start | bytes 442372
  7.2 7.1 %copy-start.1 = (bf16[1,48,1536]{2,1,0:T(8,128)(2,1)S(1)}, bf16[1,48,1536]{2,1,0:T(8,128)(2,1)}, u32[]{:S(2)}) copy-start(bf16[1,48,1536]{2,1,0:T(8,128)(2,1)} %param.31) | copy-start | bytes 442372
  7.2 103.3 %all-gather.6.cloned.1.call-start = ((), (), s32[]{:S(2)}) async-start(), calls=%async_computation.8 | async-start | bytes 10027008 | tf_op jit(solution)/shard_map/all_gather | solution.py:117
  7.2 7.0 %collective-permute-start = (bf16[48,1536]{1,0:T(8,128)(2,1)}, bf16[48,1536]{1,0:T(8,128)(2,1)S(1)}, u32[]{:S(2)}, u32[]{:S(2)}) collective-permute-start(bf16[48,1536]{1,0:T(8,128)(2,1)} %bitcast.123), channel_id=1, source_target_pairs={{0,0},{4,32},{8,64},{12,96},{16,128},{20,160},{24,192},{28,224},{3... | collective-permute-start | bytes 442376 | tf_op jit(solution)/shard_map/ppermute | solution.py:90
  11.5 3.7 %copy-start.8 = (bf16[1,1536]{1,0:T(2,128)(2,1)S(1)}, bf16[1,1536]{1,0:T(2,128)(2,1)}, u32[]{:S(2)}) copy-start(bf16[1,1536]{1,0:T(2,128)(2,1)} %param.16) | copy-start | bytes 9220
  11.5 3.7 %copy-start.10 = (bf16[1,512]{1,0:T(2,128)(2,1)S(1)}, bf16[1,512]{1,0:T(2,128)(2,1)}, u32[]{:S(2)}) copy-start(bf16[1,512]{1,0:T(2,128)(2,1)} %param.17) | copy-start | bytes 3076
  15.2 22.5 %copy-start.9 = (s32[512]{0:T(512)S(1)}, s32[512]{0:T(512)}, u32[]{:S(2)}) copy-start(s32[512]{0:T(512)} %param.19) | copy-start | bytes 6148
  15.3 57.5 %all-to-all-start = ((bf16[32,16,1536]{2,1,0:T(8,128)(2,1)}), bf16[32,16,1536]{2,1,0:T(8,128)(2,1)S(1)}, u32[]{:S(2)}, u32[]{:S(2)}) async-start(bf16[32,16,1536]{2,1,0:T(8,128)(2,1)} %bitcast.4), calls=%async_computation | async-start | bytes 3145728 | tf_op jit(solution)/shard_map/all_to_all | solution.py:22
  37.5 56.8 %copy-start.11 = (s32[32]{0:T(128)S(1)}, s32[32]{0:T(128)}, u32[]{:S(2)}) copy-start(s32[32]{0:T(128)} %param.20) | copy-start | bytes 388
  37.5 56.8 %copy-start.12 = (s32[32]{0:T(128)S(1)}, s32[32]{0:T(128)}, u32[]{:S(2)}) copy-start(s32[32]{0:T(128)} %param.21) | copy-start | bytes 388
  37.6 62.9 %copy-start.13 = (bf16[32,2,64,128]{3,2,1,0:T(8,128)(2,1)S(1)}, bf16[32,2,64,128]{3,2,1,0:T(8,128)(2,1)}, u32[]{:S(2)}) copy-start(bf16[32,2,64,128]{3,2,1,0:T(8,128)(2,1)} %param.22) | copy-start | bytes 3145732
  73.5 16.8 %all-to-all-start.1 = ((bf16[8,32,512]{2,1,0:T(8,128)(2,1)}), bf16[8,32,512]{2,1,0:T(8,128)(2,1)S(1)}, u32[]{:S(2)}, u32[]{:S(2)}) async-start(bf16[8,32,512]{2,1,0:T(8,128)(2,1)} %broadcast_in_dim.148), calls=%async_computation.1 | async-start | bytes 524288 | tf_op jit(solution)/shard_map/all_to_all | solution.py:22
  91.0 9.3 %all-to-all-start.2 = ((bf16[4,32,512]{2,1,0:T(8,128)(2,1)}), bf16[4,32,512]{2,1,0:T(8,128)(2,1)S(1)}, u32[]{:S(2)}, u32[]{:S(2)}) async-start(bf16[4,32,512]{2,1,0:T(8,128)(2,1)} %broadcast_in_dim.149), calls=%async_computation.2 | async-start | bytes 262144 | tf_op jit(solution)/shard_map/all_to_all | solution.py:22
  105.5 14.8 %all-to-all-start.3 = ((bf16[32,16,128]{2,1,0:T(8,128)(2,1)}), bf16[32,16,128]{2,1,0:T(8,128)(2,1)S(1)}, u32[]{:S(2)}, u32[]{:S(2)}) async-start(bf16[32,16,128]{2,1,0:T(8,128)(2,1)} %copy.109), calls=%async_computation.3 | async-start | bytes 262144 | tf_op jit(solution)/shard_map/all_to_all | solution.py:22
  120.3 10.3 %copy-start.7 = (f32[64,4]{0,1:T(4,128)S(1)}, f32[64,4]{0,1:T(4,128)}, u32[]{:S(2)}) copy-start(f32[64,4]{0,1:T(4,128)} %param.27) | copy-start | bytes 3076
  120.3 10.3 %copy-start.6 = (s32[64,4]{0,1:T(4,128)S(1)}, s32[64,4]{0,1:T(4,128)}, u32[]{:S(2)}) copy-start(s32[64,4]{0,1:T(4,128)} %param.26) | copy-start | bytes 3076
  120.3 47.1 %all-to-all-start.4 = ((bf16[32,16,1536]{2,1,0:T(8,128)(2,1)}), bf16[32,16,1536]{2,1,0:T(8,128)(2,1)S(1)}, u32[]{:S(2)}, u32[]{:S(2)}) async-start(bf16[32,16,1536]{2,1,0:T(8,128)(2,1)} %bitcast.20), calls=%async_computation.4 | async-start | bytes 3145728 | tf_op jit(solution)/shard_map/all_to_all | solution.py:22
  145.2 41.6 %copy-start.4 = (bf16[1,1536]{1,0:T(2,128)(2,1)S(1)}, bf16[1,1536]{1,0:T(2,128)(2,1)}, u32[]{:S(2)}) copy-start(bf16[1,1536]{1,0:T(2,128)(2,1)} %param.18) | copy-start | bytes 9220
  145.2 42.9 %copy-start.5 = (f32[1536]{0:T(1024)S(1)}, f32[1536]{0:T(1024)}, u32[]{:S(2)}) copy-start(f32[1536]{0:T(1024)} %param.28) | copy-start | bytes 18436
  168.0 18.6 %all-to-all-start.5 = ((bf16[32,3,128]{2,1,0:T(4,128)(2,1)}), bf16[32,3,128]{2,1,0:T(4,128)(2,1)S(1)}, u32[]{:S(2)}, u32[]{:S(2)}) async-start(bf16[32,3,128]{2,1,0:T(4,128)(2,1)} %reshape.231), calls=%async_computation.5 | async-start | bytes 65536 | tf_op jit(solution)/shard_map/all_to_all | solution.py:22
  188.8 14.4 %all-to-all-start.6 = ((bf16[32,12,128]{2,1,0:T(8,128)(2,1)}), bf16[32,12,128]{2,1,0:T(8,128)(2,1)S(1)}, u32[]{:S(2)}, u32[]{:S(2)}) async-start(bf16[32,12,128]{2,1,0:T(8,128)(2,1)} %broadcast_in_dim.163), calls=%async_computation.6 | async-start | bytes 262144 | tf_op jit(solution)/shard_map/all_to_all | solution.py:22
  205.7 9.5 %copy-start = (bf16[63,1536]{1,0:T(8,128)(2,1)S(1)}, bf16[63,1536]{1,0:T(8,128)(2,1)}, u32[]{:S(2)}) copy-start(bf16[63,1536]{1,0:T(8,128)(2,1)} %param.25) | copy-start | bytes 580612
  210.4 14.5 %all-to-all-start.7 = ((bf16[32,12,128]{2,1,0:T(8,128)(2,1)}), bf16[32,12,128]{2,1,0:T(8,128)(2,1)S(1)}, u32[]{:S(2)}, u32[]{:S(2)}) async-start(bf16[32,12,128]{2,1,0:T(8,128)(2,1)} %reshape.235), calls=%async_computation.7 | async-start | bytes 262144 | tf_op jit(solution)/shard_map/all_to_all | solution.py:22
Sparse Core Ops, SparseCore 0:
  15.3 80.7 all-gather.5

commit v5 on v4

--- a/solution.py
+++ b/solution.py
@@ -1,5 +1,3 @@
-import math
-
 import jax
 import jax.numpy as jnp
 from jax import lax
@@ -82,12 +80,13 @@
     experts = tp_size * w_gate.shape[0]
     assert group_reqs == tp_size and experts == tp_size
 
-    turned = [
-        (group * lines + other, (other + group // lines * lines) * lines + group % lines)
-        for group in range(dp_size)
-        for other in range(lines)
-    ]
-    line_columns = lax.ppermute(w_out.T, ("dp", "y"), turned)
+    turned = []
+    for group in range(dp_size):
+        for lane in range(tp_size):
+            taker = lane % lines + group // lines * lines
+            place = (taker * lines + group % lines) * posts + lane // lines
+            turned.append((group * tp_size + lane, place))
+    post_part = lax.ppermute(w_out.T, ("dp", "y", "x"), turned)
 
     no_value = jnp.zeros((), BF16)
     rows_dev, top_count = routes.shape
@@ -113,9 +112,9 @@
         preferred_element_type=F32,
     ).astype(BF16)
 
-    line_columns, outgoing = lax.optimization_barrier((line_columns, outgoing))
+    post_part, outgoing = lax.optimization_barrier((post_part, outgoing))
     units = lax.all_gather(
-        jnp.concatenate([w_gate, w_up, w_down, line_columns[None]], axis=0),
+        jnp.concatenate([w_gate, w_up, w_down, post_part[None]], axis=0),
         "dp",
         axis=1,
         tiled=True,
@@ -125,11 +124,15 @@
     columns = heads + 2 * kv_heads
     share = columns * head_size // posts
     post = lax.axis_index("x")
-    fresh = jnp.concatenate([q_new, new_key_value], axis=1)
+    fresh = jnp.concatenate([q_new, new_key_value, resid_dec], axis=1)
     fresh, outgoing = lax.optimization_barrier((fresh, outgoing))
     received = swap(outgoing.reshape(experts, capacity, width), TP)
     line_fresh = lax.all_gather(fresh, "x", axis=0, tiled=True)
     line_share = lax.dynamic_slice_in_dim(line_fresh, post * share, share, axis=1)
+    post_columns = width // posts
+    line_resid = lax.dynamic_slice_in_dim(
+        line_fresh, columns * head_size + post * post_columns, post_columns, axis=1
+    )
     all_rows = lax.all_gather(line_share, "dp", axis=0, tiled=True)
     wanted = lax.dynamic_slice_in_dim(placing, dp_group * group_reqs, group_reqs)
     held = jnp.arange(dp_size, dtype=jnp.int32)[:, None] * tp_size + line * posts
@@ -186,22 +189,21 @@
 
     attention = lax.all_gather(attention_row.reshape(1, width), "x", axis=0, tiled=True)
     projected = contract_rows(attention, out_rows).astype(BF16)
-    post_columns = projected.shape[1]
     all_projected = lax.all_gather(projected, "dp", axis=0, tiled=True)
     line_rows = placing.reshape(dp_size, lines, posts)
     line_rows = lax.dynamic_slice_in_dim(line_rows, line, 1, axis=1).reshape(1, dp_size * posts)
-    home_ids = dp_group * group_reqs + jnp.arange(group_reqs, dtype=jnp.int32)
-    at_home = choose_rows(home_ids[:, None] == line_rows, all_projected)
+    lane_ids = jnp.arange(group_reqs, dtype=jnp.int32)[:, None]
+    from_cache = (dp_group * group_reqs + lane_ids == line_rows).astype(BF16)
+    from_line = lane_ids == line * posts + jnp.arange(posts, dtype=jnp.int32)[None, :]
+    at_home = jnp.dot(from_cache, all_projected, preferred_element_type=F32)
+    at_home = at_home + jnp.dot(from_line.astype(BF16), line_resid, preferred_element_type=F32)
+    at_home = at_home.astype(BF16)
     at_home, returned = lax.optimization_barrier((at_home, returned))
-    from_lanes = swap(at_home.reshape(tp_size, -1, math.gcd(post_columns, head_size)), TP)
-    from_lanes = from_lanes.reshape(lines, posts, post_columns).astype(F32)
-    proj_home = jnp.sum(from_lanes, axis=0).reshape(posts, lines, post_columns // lines)
-    proj_home = jnp.transpose(proj_home, (1, 0, 2)).reshape(1, width)
-    hidden_f32 = (resid_dec.astype(F32) + proj_home).astype(BF16).astype(F32)
-
-    normed_dec = rms(hidden_f32, moe_gain)
-    group_rows = spread(normed_dec.reshape(heads, head_size), TP).reshape(group_reqs, width)
-    dec_out = expert_units(group_rows, units)
+    hidden_share = jnp.sum(spread(at_home, "y").astype(F32), axis=0).astype(BF16)
+    hidden_all = jnp.transpose(spread(hidden_share, "x"), (1, 0, 2)).reshape(group_reqs, width)
+    hidden_f32 = lax.dynamic_slice_in_dim(hidden_all, tp_lane, 1).astype(F32)
+
+    dec_out = expert_units(rms(hidden_all.astype(F32), moe_gain), units)
     dec_back = swap(dec_out.reshape(group_reqs, heads, head_size), TP).astype(F32)
     dec_weight = weight_of[pre_rows:].reshape(experts, 1, 1)
     dec_mixture = jnp.sum(dec_weight * dec_back, axis=0).reshape(1, width)

time: 234 us -> 227 us (0.970)
  blocking collectives: 66.4 us -> 63.1 us
  starting transfers between devices: 68 us -> 64.9 us
    all_to_all x8, starting transfers between devices: 65.9 us -> 58.8 us  [swap(): lax.all_to_all(blocks, axis_name, split_axis=0, concat_axis=0, tiled=True)]
    ppermute x1, starting transfers between devices: 2.05 us -> 6.11 us  [on_device(): post_part = lax.ppermute(w_out.T, ('dp', 'y', 'x'), turned)]
    all_gather x1, blocking collectives: 21.5 us -> 19 us  [on_device(): all_projected = lax.all_gather(projected, 'dp', axis=0, tiled=True)]
  transfers between devices with their start and end apart: 10 -> 10, of which waited for: 7 -> 7; matrix products, arithmetic and copies ran while one was open for 11% -> 12% of each run, Pallas kernels for 0% -> 0%
where the time goes in v5:
time: 227 us; the launch traced here: 226 us
  starting transfers between devices  64.9 us (29%)
  blocking collectives  63.1 us (28%)
  waiting for transfers between devices  46.5 us (20%)
  matrix products  26.6 us (12%)
  between operations  14.6 us (6%)
  local copies, waits for them, and re-layouts  5.67 us (2%)
  other arithmetic  4.91 us (2%)
    all_to_all x8, starting transfers between devices, swap(): lax.all_to_all(blocks, axis_name, split_axis=0, concat_axis=0, tiled=True)  58.8 us
    all_to_all x8, waiting for transfers between devices, swap(): lax.all_to_all(blocks, axis_name, split_axis=0, concat_axis=0, tiled=True)  46.5 us
    all_gather x1, blocking collectives, on_device(): all_rows = lax.all_gather(line_share, 'dp', axis=0, tiled=True)  19.3 us
    all_gather x1, blocking collectives, on_device(): all_projected = lax.all_gather(projected, 'dp', axis=0, tiled=True)  19 us
    all_gather x1, blocking collectives, on_device(): line_fresh = lax.all_gather(fresh, 'x', axis=0, tiled=True)  12.4 us
    all_gather x1, blocking collectives, on_device(): lax.all_gather(attention_row.reshape(1, width), 'x', axis=0, tiled=True)  12.3 us
    dot_general x2, matrix products, expert_units(): return jnp.dot(active, units[2], preferred_element_type=F32).astype(BF16)  10.6 us
    dot_general x3, matrix products, contract_rows(): lax.dot_general(left_rows, unit_rows, (((1,), (1,)), ((), ())), preferred...  7.18 us
  transfers between devices with their start and end apart: 10, of which 7 were waited for; matrix products, arithmetic and copies ran while one was open for 12% of the time, Pallas kernels for 0%

profile of v5, /device:TPU:8, one launch (start us, length us, event | category | flops | bytes accessed | tf_op | source)
XLA Modules:
  0.0 226.3 jit_solution(16450521314963162766)
XLA Ops:
  7.2 6.1 %collective-permute-start = (bf16[48,1536]{1,0:T(8,128)(2,1)}, bf16[48,1536]{1,0:T(8,128)(2,1)S(1)}, u32[]{:S(2)}, u32[]{:S(2)}) collective-permute-start(bf16[48,1536]{1,0:T(8,128)(2,1)} %bitcast.127), channel_id=1, source_target_pairs={{0,0},{1,32},{2,64},{3,96},{4,128},{5,160},{6,192},{7,224},{8,1},{... | collective-permute-start | bytes 442376 | tf_op jit(solution)/shard_map/ppermute | solution.py:89
  13.4 0.7 iota_compare_fusion.1
  14.3 1.1 fusion.23
  15.4 0.1 fusion.30
  15.6 2.8 %convolution_convert_fusion.1 = bf16[512,1536]{1,0:T(8,128)(2,1)} fusion(pred[63,512]{0,1:T(32,128)(4,1)S(1)} %fusion.30, bf16[63,1536]{1,0:T(8,128)(2,1)} %param.25, f32[1536]{0:T(1024)} %param.28, f32[63]{0:T(128)S(1)} %add_rsqrt_fusion.1), kind=kOutput, calls=%fused_computation.1 | convolution fusion | flops 100263936 | bytes 1805052 | tf_op jit(solution)/shard_map/dot_general | solution.py:108
  18.4 0.9 pad_maximum_fusion
  19.3 19.6 %all-to-all-start = ((bf16[32,16,1536]{2,1,0:T(8,128)(2,1)}), bf16[32,16,1536]{2,1,0:T(8,128)(2,1)S(1)}, u32[]{:S(2)}, u32[]{:S(2)}) async-start(bf16[32,16,1536]{2,1,0:T(8,128)(2,1)} %bitcast.4), calls=%async_computation | async-start | bytes 3145728 | tf_op jit(solution)/shard_map/all_to_all | solution.py:20
  39.3 12.4 %all-gather = bf16[4,1,3584]{2,1,0:T(2,128)(2,1)S(1)} all-gather(bf16[1,1,3584]{2,1,0:T(2,128)(2,1)S(1)} %bitcast.124), channel_id=1, replica_groups=mesh['dp'=16,'y'=8,'x'=4] {'x'}, dimensions={0}, use_global_device_ids=true | all-gather | bytes 35840 | tf_op jit(solution)/shard_map/all_gather | solution.py:130
  51.7 19.3 %all-gather.1 = bf16[16,4,512]{2,1,0:T(4,128)(2,1)S(1)} all-gather(bf16[1,4,512]{2,1,0:T(4,128)(2,1)S(1)} %bitcast.126), channel_id=1, replica_groups=mesh['dp'=16,'y'=8,'x'=4] {'dp'}, dimensions={0}, use_global_device_ids=true | all-gather | bytes 69632 | tf_op jit(solution)/shard_map/all_gather | solution.py:136
  71.1 0.2 convolution_convert_fusion.4
  71.3 7.0 %all-to-all-done = bf16[32,16,1536]{2,1,0:T(8,128)(2,1)S(1)} async-done(((bf16[32,16,1536]{2,1,0:T(8,128)(2,1)}), bf16[32,16,1536]{2,1,0:T(8,128)(2,1)S(1)}, u32[]{:S(2)}, u32[]{:S(2)}) %all-to-all-start) | async-done | bytes 1572896 | tf_op jit(solution)/shard_map/all_to_all | solution.py:20
  78.2 0.7 broadcast_in_dim.152
  79.0 5.3 %all-to-all-start.1 = ((bf16[8,32,512]{2,1,0:T(8,128)(2,1)}), bf16[8,32,512]{2,1,0:T(8,128)(2,1)S(1)}, u32[]{:S(2)}, u32[]{:S(2)}) async-start(bf16[8,32,512]{2,1,0:T(8,128)(2,1)} %broadcast_in_dim.152), calls=%async_computation.1 | async-start | bytes 524288 | tf_op jit(solution)/shard_map/all_to_all | solution.py:20
  84.2 8.7 %all-to-all-done.1 = bf16[8,32,512]{2,1,0:T(8,128)(2,1)S(1)} async-done(((bf16[8,32,512]{2,1,0:T(8,128)(2,1)}), bf16[8,32,512]{2,1,0:T(8,128)(2,1)S(1)}, u32[]{:S(2)}, u32[]{:S(2)}) %all-to-all-start.1) | async-done | bytes 262176 | tf_op jit(solution)/shard_map/all_to_all | solution.py:20
  92.9 0.7 broadcast_in_dim.153
  93.6 5.0 %all-to-all-start.2 = ((bf16[4,32,512]{2,1,0:T(8,128)(2,1)}), bf16[4,32,512]{2,1,0:T(8,128)(2,1)S(1)}, u32[]{:S(2)}, u32[]{:S(2)}) async-start(bf16[4,32,512]{2,1,0:T(8,128)(2,1)} %broadcast_in_dim.153), calls=%async_computation.2 | async-start | bytes 262144 | tf_op jit(solution)/shard_map/all_to_all | solution.py:20
  98.8 5.8 %all-to-all-done.2 = bf16[4,32,512]{2,1,0:T(8,128)(2,1)S(1)} async-done(((bf16[4,32,512]{2,1,0:T(8,128)(2,1)}), bf16[4,32,512]{2,1,0:T(8,128)(2,1)S(1)}, u32[]{:S(2)}, u32[]{:S(2)}) %all-to-all-start.2) | async-done | bytes 131104 | tf_op jit(solution)/shard_map/all_to_all | solution.py:20
  104.7 1.1 fusion.84
  105.9 0.3 fusion.31
  106.6 2.3 %convolution_convert_fusion.3 = bf16[32,2,6,128]{3,2,1,0:T(8,128)(2,1)S(1)} fusion(bf16[32,2,64,128]{3,2,1,0:T(8,128)(2,1)} %param.23, pred[32,64]{1,0:T(8,128)(4,1)S(1)} %get-tuple-element.38, bf16[32,2,128]{2,1,0:T(2,128)(2,1)S(1)} %copy.119, f32[32,2,6,64]{3,2,1,0:T(8,128)S(1)} %get-tuple-element.40, f32[32,2,6]{2,1,0:T(2,128)S(1)} %get-tuple-element.39, ...), kind=kOutput, calls=%fused_computation.22 | convolution fusion | flops 38371328 | bytes 1267200 | tf_op jit(solution)/shard_map/rgqs,rgsd->rgqd/dot_general | solution.py:161
  109.0 0.7 copy.125
  109.7 5.0 %all-to-all-start.3 = ((bf16[32,16,128]{2,1,0:T(8,128)(2,1)}), bf16[32,16,128]{2,1,0:T(8,128)(2,1)S(1)}, u32[]{:S(2)}, u32[]{:S(2)}) async-start(bf16[32,16,128]{2,1,0:T(8,128)(2,1)} %copy.125), calls=%async_computation.3 | async-start | bytes 262144 | tf_op jit(solution)/shard_map/all_to_all | solution.py:20
  114.7 3.1 %fusion.5 = f32[512,768]{1,0:T(8,128)S(1)} fusion(bf16[512,1536]{1,0:T(8,128)(2,1)S(1)} %bitcast.109, bf16[4,768,1536]{2,1,0:T(8,128)(2,1)} %all-gather.6.cloned.1.call-done), kind=kOutput, calls=%fused_computation.14 | convolution fusion | flops 1207959552 | bytes 5505024 | tf_op jit(solution)/shard_map/dot_general | solution.py:14
  117.8 6.7 %convolution_convert_fusion = bf16[512,1536]{1,0:T(8,128)(2,1)} fusion(bf16[4,768,1536]{2,1,0:T(8,128)(2,1)} %all-gather.6.cloned.1.call-done, f32[512,768]{1,0:T(8,128)S(1)} %fusion.5, bf16[512,1536]{1,0:T(8,128)(2,1)S(1)} %bitcast.110), kind=kOutput, calls=%fused_computation | convolution fusion | flops 2417885184 | bytes 9437184 | tf_op jit(solution)/shard_map/dot_general | solution.py:48
  124.5 10.0 %all-to-all-start.4 = ((bf16[32,16,1536]{2,1,0:T(8,128)(2,1)}), bf16[32,16,1536]{2,1,0:T(8,128)(2,1)S(1)}, u32[]{:S(2)}, u32[]{:S(2)}) async-start(bf16[32,16,1536]{2,1,0:T(8,128)(2,1)} %bitcast.20), calls=%async_computation.4 | async-start | bytes 3145728 | tf_op jit(solution)/shard_map/all_to_all | solution.py:20
  135.1 0.1 slice_add_fusion
  135.3 0.1 multiply_reduce_fusion.1
  135.5 12.3 %all-gather.2 = bf16[4,1,1536]{2,1,0:T(2,128)(2,1)S(1)} all-gather(bf16[1,1,1536]{2,1,0:T(2,128)(2,1)S(1)} %reshape.251), channel_id=1, replica_groups=mesh['dp'=16,'y'=8,'x'=4] {'x'}, dimensions={0}, use_global_device_ids=true | all-gather | bytes 15360 | tf_op jit(solution)/shard_map/all_gather | solution.py:190
  147.9 1.7 fusion.15
  149.6 19.0 %all-gather.3 = bf16[16,4,384]{2,1,0:T(4,128)(2,1)S(1)} all-gather(bf16[1,4,384]{2,1,0:T(4,128)(2,1)S(1)} %fusion.15), channel_id=1, replica_groups=mesh['dp'=16,'y'=8,'x'=4] {'dp'}, dimensions={0}, use_global_device_ids=true | all-gather | bytes 52224 | tf_op jit(solution)/shard_map/all_gather | solution.py:192
  168.6 0.2 fusion.13
  168.8 2.3 %all-to-all-done.4 = bf16[32,16,1536]{2,1,0:T(8,128)(2,1)S(1)} async-done(((bf16[32,16,1536]{2,1,0:T(8,128)(2,1)}), bf16[32,16,1536]{2,1,0:T(8,128)(2,1)S(1)}, u32[]{:S(2)}, u32[]{:S(2)}) %all-to-all-start.4) | async-done | bytes 1572896 | tf_op jit(solution)/shard_map/all_to_all | solution.py:20
  171.1 0.7 broadcast_in_dim.165
  171.8 4.9 %all-to-all-start.5 = ((bf16[8,32,384]{2,1,0:T(8,128)(2,1)}), bf16[8,32,384]{2,1,0:T(8,128)(2,1)S(1)}, u32[]{:S(2)}, u32[]{:S(2)}) async-start(bf16[8,32,384]{2,1,0:T(8,128)(2,1)} %broadcast_in_dim.165), calls=%async_computation.5 | async-start | bytes 393216 | tf_op jit(solution)/shard_map/all_to_all | solution.py:20
  176.7 0.2 slice_reduce_fusion.1
  176.9 0.4 convolution_bitcast_fusion.2
  177.4 8.9 %all-to-all-done.5 = bf16[8,32,384]{2,1,0:T(8,128)(2,1)S(1)} async-done(((bf16[8,32,384]{2,1,0:T(8,128)(2,1)}), bf16[8,32,384]{2,1,0:T(8,128)(2,1)S(1)}, u32[]{:S(2)}, u32[]{:S(2)}) %all-to-all-start.5) | async-done | bytes 196640 | tf_op jit(solution)/shard_map/all_to_all | solution.py:20
  186.3 0.7 broadcast_in_dim.166
  186.9 4.1 %all-to-all-start.6 = ((bf16[4,32,384]{2,1,0:T(8,128)(2,1)}), bf16[4,32,384]{2,1,0:T(8,128)(2,1)S(1)}, u32[]{:S(2)}, u32[]{:S(2)}) async-start(bf16[4,32,384]{2,1,0:T(8,128)(2,1)} %broadcast_in_dim.166), calls=%async_computation.6 | async-start | bytes 196608 | tf_op jit(solution)/shard_map/all_to_all | solution.py:20
  191.0 0.4 fusion.2
  191.4 5.4 %all-to-all-done.6 = bf16[4,32,384]{2,1,0:T(8,128)(2,1)S(1)} async-done(((bf16[4,32,384]{2,1,0:T(8,128)(2,1)}), bf16[4,32,384]{2,1,0:T(8,128)(2,1)S(1)}, u32[]{:S(2)}, u32[]{:S(2)}) %all-to-all-start.6) | async-done | bytes 98336 | tf_op jit(solution)/shard_map/all_to_all | solution.py:20
  197.0 2.4 %fusion.11 = f32[32,768]{1,0:T(8,128)S(1)} fusion(bf16[32,1536]{1,0:T(8,128)(2,1)S(1)} %bitcast.121, bf16[4,768,1536]{2,1,0:T(8,128)(2,1)} %all-gather.6.cloned.1.call-done), kind=kOutput, calls=%fused_computation.24 | convolution fusion | flops 75522048 | bytes 2555904 | tf_op jit(solution)/shard_map/dot_general | solution.py:14
  199.5 3.9 %convolution_convert_fusion.2 = bf16[32,1536]{1,0:T(8,128)(2,1)S(1)} fusion(bf16[4,768,1536]{2,1,0:T(8,128)(2,1)} %all-gather.6.cloned.1.call-done, f32[32,768]{1,0:T(8,128)S(1)} %fusion.11, bf16[32,1536]{1,0:T(8,128)(2,1)S(1)} %bitcast.122), kind=kOutput, calls=%fused_computation.12 | convolution fusion | flops 151093248 | bytes 5013504 | tf_op jit(solution)/shard_map/dot_general | solution.py:48
  203.4 0.7 reshape.245
  204.1 5.0 %all-to-all-start.7 = ((bf16[32,12,128]{2,1,0:T(8,128)(2,1)}), bf16[32,12,128]{2,1,0:T(8,128)(2,1)S(1)}, u32[]{:S(2)}, u32[]{:S(2)}) async-start(bf16[32,12,128]{2,1,0:T(8,128)(2,1)} %reshape.245), calls=%async_computation.7 | async-start | bytes 262144 | tf_op jit(solution)/shard_map/all_to_all | solution.py:20
  209.2 1.1 fusion.3
  210.3 8.5 %all-to-all-done.7 = bf16[32,12,128]{2,1,0:T(8,128)(2,1)S(1)} async-done(((bf16[32,12,128]{2,1,0:T(8,128)(2,1)}), bf16[32,12,128]{2,1,0:T(8,128)(2,1)S(1)}, u32[]{:S(2)}, u32[]{:S(2)}) %all-to-all-start.7) | async-done | bytes 98336 | tf_op jit(solution)/shard_map/all_to_all | solution.py:20
  218.9 0.6 fusion.74
  (96 shorter events, 2.6 us)
Async XLA Ops:
  7.2 11.2 %copy-start.1 = (bf16[1,48,1536]{2,1,0:T(8,128)(2,1)S(1)}, bf16[1,48,1536]{2,1,0:T(8,128)(2,1)}, u32[]{:S(2)}) copy-start(bf16[1,48,1536]{2,1,0:T(8,128)(2,1)} %param.31) | copy-start | bytes 442372
  7.2 11.2 %copy-start.2 = (bf16[1,48,1536]{2,1,0:T(8,128)(2,1)S(1)}, bf16[1,48,1536]{2,1,0:T(8,128)(2,1)}, u32[]{:S(2)}) copy-start(bf16[1,48,1536]{2,1,0:T(8,128)(2,1)} %param.30) | copy-start | bytes 442372
  7.2 11.2 %copy-start.3 = (bf16[1,48,1536]{2,1,0:T(8,128)(2,1)S(1)}, bf16[1,48,1536]{2,1,0:T(8,128)(2,1)}, u32[]{:S(2)}) copy-start(bf16[1,48,1536]{2,1,0:T(8,128)(2,1)} %param.29) | copy-start | bytes 442372
  7.2 107.5 %all-gather.6.cloned.1.call-start = ((), (), s32[]{:S(2)}) async-start(), calls=%async_computation.8 | async-start | bytes 10027008 | tf_op jit(solution)/shard_map/all_gather | solution.py:116
  7.2 11.1 %collective-permute-start = (bf16[48,1536]{1,0:T(8,128)(2,1)}, bf16[48,1536]{1,0:T(8,128)(2,1)S(1)}, u32[]{:S(2)}, u32[]{:S(2)}) collective-permute-start(bf16[48,1536]{1,0:T(8,128)(2,1)} %bitcast.127), channel_id=1, source_target_pairs={{0,0},{1,32},{2,64},{3,96},{4,128},{5,160},{6,192},{7,224},{8,1},{... | collective-permute-start | bytes 442376 | tf_op jit(solution)/shard_map/ppermute | solution.py:89
  15.5 3.7 %copy-start.7 = (bf16[1,1536]{1,0:T(2,128)(2,1)S(1)}, bf16[1,1536]{1,0:T(2,128)(2,1)}, u32[]{:S(2)}) copy-start(bf16[1,1536]{1,0:T(2,128)(2,1)} %param.18) | copy-start | bytes 9220
  15.6 3.7 %copy-start.8 = (bf16[1,1536]{1,0:T(2,128)(2,1)S(1)}, bf16[1,1536]{1,0:T(2,128)(2,1)}, u32[]{:S(2)}) copy-start(bf16[1,1536]{1,0:T(2,128)(2,1)} %param.16) | copy-start | bytes 9220
  15.6 3.7 %copy-start.9 = (bf16[1,512]{1,0:T(2,128)(2,1)S(1)}, bf16[1,512]{1,0:T(2,128)(2,1)}, u32[]{:S(2)}) copy-start(bf16[1,512]{1,0:T(2,128)(2,1)} %param.17) | copy-start | bytes 3076
  19.3 19.8 %copy-start.10 = (s32[512]{0:T(512)S(1)}, s32[512]{0:T(512)}, u32[]{:S(2)}) copy-start(s32[512]{0:T(512)} %param.19) | copy-start | bytes 6148
  19.3 58.9 %all-to-all-start = ((bf16[32,16,1536]{2,1,0:T(8,128)(2,1)}), bf16[32,16,1536]{2,1,0:T(8,128)(2,1)S(1)}, u32[]{:S(2)}, u32[]{:S(2)}) async-start(bf16[32,16,1536]{2,1,0:T(8,128)(2,1)} %bitcast.4), calls=%async_computation | async-start | bytes 3145728 | tf_op jit(solution)/shard_map/all_to_all | solution.py:20
  38.9 59.6 %copy-start.11 = (s32[32]{0:T(128)S(1)}, s32[32]{0:T(128)}, u32[]{:S(2)}) copy-start(s32[32]{0:T(128)} %param.20) | copy-start | bytes 388
  39.0 59.6 %copy-start.12 = (s32[32]{0:T(128)S(1)}, s32[32]{0:T(128)}, u32[]{:S(2)}) copy-start(s32[32]{0:T(128)} %param.21) | copy-start | bytes 388
  39.0 65.7 %copy-start.13 = (bf16[32,2,64,128]{3,2,1,0:T(8,128)(2,1)S(1)}, bf16[32,2,64,128]{3,2,1,0:T(8,128)(2,1)}, u32[]{:S(2)}) copy-start(bf16[32,2,64,128]{3,2,1,0:T(8,128)(2,1)} %param.22) | copy-start | bytes 3145732
  79.0 13.9 %all-to-all-start.1 = ((bf16[8,32,512]{2,1,0:T(8,128)(2,1)}), bf16[8,32,512]{2,1,0:T(8,128)(2,1)S(1)}, u32[]{:S(2)}, u32[]{:S(2)}) async-start(bf16[8,32,512]{2,1,0:T(8,128)(2,1)} %broadcast_in_dim.152), calls=%async_computation.1 | async-start | bytes 524288 | tf_op jit(solution)/shard_map/all_to_all | solution.py:20
  93.6 11.0 %all-to-all-start.2 = ((bf16[4,32,512]{2,1,0:T(8,128)(2,1)}), bf16[4,32,512]{2,1,0:T(8,128)(2,1)S(1)}, u32[]{:S(2)}, u32[]{:S(2)}) async-start(bf16[4,32,512]{2,1,0:T(8,128)(2,1)} %broadcast_in_dim.153), calls=%async_computation.2 | async-start | bytes 262144 | tf_op jit(solution)/shard_map/all_to_all | solution.py:20
  109.7 14.8 %all-to-all-start.3 = ((bf16[32,16,128]{2,1,0:T(8,128)(2,1)}), bf16[32,16,128]{2,1,0:T(8,128)(2,1)S(1)}, u32[]{:S(2)}, u32[]{:S(2)}) async-start(bf16[32,16,128]{2,1,0:T(8,128)(2,1)} %copy.125), calls=%async_computation.3 | async-start | bytes 262144 | tf_op jit(solution)/shard_map/all_to_all | solution.py:20
  124.5 10.3 %copy-start.6 = (f32[64,4]{0,1:T(4,128)S(1)}, f32[64,4]{0,1:T(4,128)}, u32[]{:S(2)}) copy-start(f32[64,4]{0,1:T(4,128)} %param.27) | copy-start | bytes 3076
  124.5 10.3 %copy-start.5 = (s32[64,4]{0,1:T(4,128)S(1)}, s32[64,4]{0,1:T(4,128)}, u32[]{:S(2)}) copy-start(s32[64,4]{0,1:T(4,128)} %param.26) | copy-start | bytes 3076
  124.5 46.5 %all-to-all-start.4 = ((bf16[32,16,1536]{2,1,0:T(8,128)(2,1)}), bf16[32,16,1536]{2,1,0:T(8,128)(2,1)S(1)}, u32[]{:S(2)}, u32[]{:S(2)}) async-start(bf16[32,16,1536]{2,1,0:T(8,128)(2,1)} %bitcast.20), calls=%async_computation.4 | async-start | bytes 3145728 | tf_op jit(solution)/shard_map/all_to_all | solution.py:20
  134.6 42.2 %copy-start.4 = (f32[1536]{0:T(1024)S(1)}, f32[1536]{0:T(1024)}, u32[]{:S(2)}) copy-start(f32[1536]{0:T(1024)} %param.28) | copy-start | bytes 18436
  171.8 14.5 %all-to-all-start.5 = ((bf16[8,32,384]{2,1,0:T(8,128)(2,1)}), bf16[8,32,384]{2,1,0:T(8,128)(2,1)S(1)}, u32[]{:S(2)}, u32[]{:S(2)}) async-start(bf16[8,32,384]{2,1,0:T(8,128)(2,1)} %broadcast_in_dim.165), calls=%async_computation.5 | async-start | bytes 393216 | tf_op jit(solution)/shard_map/all_to_all | solution.py:20
  186.9 9.9 %all-to-all-start.6 = ((bf16[4,32,384]{2,1,0:T(8,128)(2,1)}), bf16[4,32,384]{2,1,0:T(8,128)(2,1)S(1)}, u32[]{:S(2)}, u32[]{:S(2)}) async-start(bf16[4,32,384]{2,1,0:T(8,128)(2,1)} %broadcast_in_dim.166), calls=%async_computation.6 | async-start | bytes 196608 | tf_op jit(solution)/shard_map/all_to_all | solution.py:20
  199.5 9.7 %copy-start = (bf16[63,1536]{1,0:T(8,128)(2,1)S(1)}, bf16[63,1536]{1,0:T(8,128)(2,1)}, u32[]{:S(2)}) copy-start(bf16[63,1536]{1,0:T(8,128)(2,1)} %param.25) | copy-start | bytes 580612
  204.1 14.6 %all-to-all-start.7 = ((bf16[32,12,128]{2,1,0:T(8,128)(2,1)}), bf16[32,12,128]{2,1,0:T(8,128)(2,1)S(1)}, u32[]{:S(2)}, u32[]{:S(2)}) async-start(bf16[32,12,128]{2,1,0:T(8,128)(2,1)} %reshape.245), calls=%async_computation.7 | async-start | bytes 262144 | tf_op jit(solution)/shard_map/all_to_all | solution.py:20
Sparse Core Ops, SparseCore 0:
  19.4 78.8 all-gather.5

commit v6 on v5

--- a/solution.py
+++ b/solution.py
@@ -5,7 +5,6 @@
 from jax.sharding import PartitionSpec as P
 
 TP = ("y", "x")
-HIGHEST = lax.Precision.HIGHEST
 F32 = jnp.float32
 BF16 = jnp.bfloat16
 
@@ -41,9 +40,13 @@
     return (rows_f32 * lax.rsqrt(mean_square + 1e-06) * gain).astype(BF16)
 
 
-def expert_units(rows, units):
-    gate = contract_rows(rows, units[0])
-    upper = contract_rows(rows, units[1])
+def expert_units(rows, units, joined=False):
+    if joined:
+        both = contract_rows(rows, units[:2].reshape(-1, units.shape[2]))
+        gate, upper = both[:, : units.shape[1]], both[:, units.shape[1] :]
+    else:
+        gate = contract_rows(rows, units[0])
+        upper = contract_rows(rows, units[1])
     active = (jnp.maximum(gate, 0.0) * upper).astype(BF16)
     return jnp.dot(active, units[2], preferred_element_type=F32).astype(BF16)
 
@@ -137,9 +140,9 @@
     wanted = lax.dynamic_slice_in_dim(placing, dp_group * group_reqs, group_reqs)
     held = jnp.arange(dp_size, dtype=jnp.int32)[:, None] * tp_size + line * posts
     held = (held + jnp.arange(posts, dtype=jnp.int32)[None, :]).reshape(1, dp_size * posts)
-    mine = choose_rows(wanted[:, None] == held, all_rows)
+    mine = choose_rows(jnp.tile(wanted, lines)[:, None] == held, all_rows)
     mine, received = lax.optimization_barrier((mine, received))
-    chosen = jnp.sum(spread(mine, "y").astype(F32), axis=0).astype(BF16)
+    chosen = jnp.sum(swap(mine.reshape(lines, group_reqs, share), "y").astype(F32), axis=0).astype(BF16)
     cached = spread(chosen, "x").reshape(posts, group_reqs, columns // posts, head_size)
     cached = jnp.transpose(cached, (1, 0, 2, 3)).reshape(group_reqs, columns, head_size)
     query_head_list = cached[:, :heads].reshape(group_reqs, kv_heads, per_group, head_size)
@@ -149,7 +152,7 @@
     slot_ids = tp_lane * slot_dev + jnp.arange(slot_dev, dtype=jnp.int32)
     written = (slot_ids[None, :] == write_pos[:, None])[:, None, :, None]
     key_rows = jnp.where(written, incoming_key, k_cache)
-    value_rows = jnp.where(written, incoming_value, value_cache).astype(F32)
+    value_rows = jnp.where(written, incoming_value, value_cache)
     scores = jnp.einsum(
         "rgqd,rgsd->rgqs", query_head_list, key_rows, preferred_element_type=F32
     ) * head_size ** (-0.5)
@@ -158,7 +161,12 @@
     local_peak = jnp.max(masked, axis=-1)
     weights = jnp.where(is_valid, jnp.exp(masked - local_peak[..., None]), 0.0)
     local_total = jnp.sum(weights, axis=-1)
-    local_mixed = jnp.einsum("rgqs,rgsd->rgqd", weights, value_rows, precision=HIGHEST)
+    high = lax.reduce_precision(weights, 8, 7)
+    halves = jnp.concatenate([high, weights - high], axis=2).astype(BF16)
+    local_mixed = jnp.einsum(
+        "rgqs,rgsd->rgqd", halves, value_rows, preferred_element_type=F32
+    )
+    local_mixed = local_mixed[:, :, :per_group] + local_mixed[:, :, per_group:]
 
     def lane_row(values):
         row = jnp.concatenate(pieces_of(values.reshape(group_reqs, heads)), axis=1)
@@ -192,18 +200,19 @@
     all_projected = lax.all_gather(projected, "dp", axis=0, tiled=True)
     line_rows = placing.reshape(dp_size, lines, posts)
     line_rows = lax.dynamic_slice_in_dim(line_rows, line, 1, axis=1).reshape(1, dp_size * posts)
-    lane_ids = jnp.arange(group_reqs, dtype=jnp.int32)[:, None]
+    lane_ids = jnp.tile(jnp.arange(group_reqs, dtype=jnp.int32), lines)[:, None]
     from_cache = (dp_group * group_reqs + lane_ids == line_rows).astype(BF16)
     from_line = lane_ids == line * posts + jnp.arange(posts, dtype=jnp.int32)[None, :]
     at_home = jnp.dot(from_cache, all_projected, preferred_element_type=F32)
     at_home = at_home + jnp.dot(from_line.astype(BF16), line_resid, preferred_element_type=F32)
     at_home = at_home.astype(BF16)
     at_home, returned = lax.optimization_barrier((at_home, returned))
-    hidden_share = jnp.sum(spread(at_home, "y").astype(F32), axis=0).astype(BF16)
+    at_home = swap(at_home.reshape(lines, group_reqs, post_columns), "y")
+    hidden_share = jnp.sum(at_home.astype(F32), axis=0).astype(BF16)
     hidden_all = jnp.transpose(spread(hidden_share, "x"), (1, 0, 2)).reshape(group_reqs, width)
     hidden_f32 = lax.dynamic_slice_in_dim(hidden_all, tp_lane, 1).astype(F32)
 
-    dec_out = expert_units(rms(hidden_all.astype(F32), moe_gain), units)
+    dec_out = expert_units(rms(hidden_all.astype(F32), moe_gain), units, joined=True)
     dec_back = swap(dec_out.reshape(group_reqs, heads, head_size), TP).astype(F32)
     dec_weight = weight_of[pre_rows:].reshape(experts, 1, 1)
     dec_mixture = jnp.sum(dec_weight * dec_back, axis=0).reshape(1, width)

time: 227 us -> 228 us (level)
  waiting for transfers between devices: 46.5 us -> 40.7 us
  local copies, waits for them, and re-layouts: 5.67 us -> 9.27 us
  matrix products: 26.6 us -> 28.9 us
    all_to_all x8, waiting for transfers between devices: 46.5 us -> 40.7 us  [swap(): lax.all_to_all(blocks, axis_name, split_axis=0, concat_axis=0, tiled=True)]
    slice x0 -> x1, local copies, waits for them, and re-layouts: none -> 4.88 us  [expert_units(): both = contract_rows(rows, units[:2].reshape(-1, units.shape[2]))]
    dot_general x3, matrix products: 7.18 us -> 9.72 us  [contract_rows(): lax.dot_general(left_rows, unit_rows, (((1,), (1,)), ((), ())), preferred...]
  transfers between devices with their start and end apart: 10 -> 10, of which waited for: 7 -> 7; matrix products, arithmetic and copies ran while one was open for 12% -> 15% of each run, Pallas kernels for 0% -> 0%
where the time goes in v6:
time: 228 us; the launch traced here: 226 us
  starting transfers between devices  64.9 us (28%)
  blocking collectives  63 us (28%)
  waiting for transfers between devices  40.7 us (18%)
  matrix products  28.9 us (13%)
  between operations  14.6 us (6%)
  local copies, waits for them, and re-layouts  9.27 us (4%)
  other arithmetic  4.96 us (2%)
    all_to_all x8, starting transfers between devices, swap(): lax.all_to_all(blocks, axis_name, split_axis=0, concat_axis=0, tiled=True)  58.8 us
    all_to_all x8, waiting for transfers between devices, swap(): lax.all_to_all(blocks, axis_name, split_axis=0, concat_axis=0, tiled=True)  40.7 us
    all_gather x1, blocking collectives, on_device(): all_rows = lax.all_gather(line_share, 'dp', axis=0, tiled=True)  19.3 us
    all_gather x1, blocking collectives, on_device(): all_projected = lax.all_gather(projected, 'dp', axis=0, tiled=True)  19.1 us
    all_gather x1, blocking collectives, on_device(): line_fresh = lax.all_gather(fresh, 'x', axis=0, tiled=True)  12.3 us
    all_gather x1, blocking collectives, on_device(): lax.all_gather(attention_row.reshape(1, width), 'x', axis=0, tiled=True)  12.3 us
    dot_general x3, matrix products, contract_rows(): lax.dot_general(left_rows, unit_rows, (((1,), (1,)), ((), ())), preferred...  9.72 us
    dot_general x2, matrix products, expert_units(): return jnp.dot(active, units[2], preferred_element_type=F32).astype(BF16)  9.37 us
  transfers between devices with their start and end apart: 10, of which 7 were waited for; matrix products, arithmetic and copies ran while one was open for 15% of the time, Pallas kernels for 0%

profile of v6, /device:TPU:8, one launch (start us, length us, event | category | flops | bytes accessed | tf_op | source)
XLA Modules:
  0.0 226.4 jit_solution(9543318880846451137)
XLA Ops:
  7.2 6.1 %collective-permute-start = (bf16[48,1536]{1,0:T(8,128)(2,1)}, bf16[48,1536]{1,0:T(8,128)(2,1)S(1)}, u32[]{:S(2)}, u32[]{:S(2)}) collective-permute-start(bf16[48,1536]{1,0:T(8,128)(2,1)} %bitcast.120), channel_id=1, source_target_pairs={{0,0},{1,32},{2,64},{3,96},{4,128},{5,160},{6,192},{7,224},{8,1},{... | collective-permute-start | bytes 442376 | tf_op jit(solution)/shard_map/ppermute | solution.py:92
  13.4 1.1 fusion.19
  14.4 0.7 iota_compare_fusion.1
  15.4 0.1 fusion.31
  15.6 2.8 %convolution_convert_fusion.1 = bf16[512,1536]{1,0:T(8,128)(2,1)} fusion(pred[63,512]{0,1:T(32,128)(4,1)S(1)} %fusion.31, bf16[63,1536]{1,0:T(8,128)(2,1)} %param.25, f32[1536]{0:T(1024)} %param.28, f32[63]{0:T(128)S(1)} %add_rsqrt_fusion.1), kind=kOutput, calls=%fused_computation.1 | convolution fusion | flops 100263936 | bytes 1805052 | tf_op jit(solution)/shard_map/dot_general | solution.py:111
  18.4 0.9 pad_maximum_fusion
  19.3 19.6 %all-to-all-start = ((bf16[32,16,1536]{2,1,0:T(8,128)(2,1)}), bf16[32,16,1536]{2,1,0:T(8,128)(2,1)S(1)}, u32[]{:S(2)}, u32[]{:S(2)}) async-start(bf16[32,16,1536]{2,1,0:T(8,128)(2,1)} %bitcast.4), calls=%async_computation | async-start | bytes 3145728 | tf_op jit(solution)/shard_map/all_to_all | solution.py:19
  39.3 12.3 %all-gather = bf16[4,1,3584]{2,1,0:T(2,128)(2,1)S(1)} all-gather(bf16[1,1,3584]{2,1,0:T(2,128)(2,1)S(1)} %bitcast.117), channel_id=1, replica_groups=mesh['dp'=16,'y'=8,'x'=4] {'x'}, dimensions={0}, use_global_device_ids=true | all-gather | bytes 35840 | tf_op jit(solution)/shard_map/all_gather | solution.py:133
  51.7 19.3 %all-gather.1 = bf16[16,4,512]{2,1,0:T(4,128)(2,1)S(1)} all-gather(bf16[1,4,512]{2,1,0:T(4,128)(2,1)S(1)} %bitcast.119), channel_id=1, replica_groups=mesh['dp'=16,'y'=8,'x'=4] {'dp'}, dimensions={0}, use_global_device_ids=true | all-gather | bytes 69632 | tf_op jit(solution)/shard_map/all_gather | solution.py:139
  71.1 1.0 convolution_convert_fusion.3
  72.0 6.2 %all-to-all-done = bf16[32,16,1536]{2,1,0:T(8,128)(2,1)S(1)} async-done(((bf16[32,16,1536]{2,1,0:T(8,128)(2,1)}), bf16[32,16,1536]{2,1,0:T(8,128)(2,1)S(1)}, u32[]{:S(2)}, u32[]{:S(2)}) %all-to-all-start) | async-done | bytes 1572896 | tf_op jit(solution)/shard_map/all_to_all | solution.py:19
  78.2 5.3 %all-to-all-start.1 = ((bf16[8,32,512]{2,1,0:T(8,128)(2,1)}), bf16[8,32,512]{2,1,0:T(8,128)(2,1)S(1)}, u32[]{:S(2)}, u32[]{:S(2)}) async-start(bf16[8,32,512]{2,1,0:T(8,128)(2,1)} %bitcast.5), calls=%async_computation.1 | async-start | bytes 524288 | tf_op jit(solution)/shard_map/all_to_all | solution.py:19
  83.5 9.4 %all-to-all-done.1 = bf16[8,32,512]{2,1,0:T(8,128)(2,1)S(1)} async-done(((bf16[8,32,512]{2,1,0:T(8,128)(2,1)}), bf16[8,32,512]{2,1,0:T(8,128)(2,1)S(1)}, u32[]{:S(2)}, u32[]{:S(2)}) %all-to-all-start.1) | async-done | bytes 262176 | tf_op jit(solution)/shard_map/all_to_all | solution.py:19
  92.9 0.7 broadcast_in_dim.138
  93.6 4.3 %all-to-all-start.2 = ((bf16[4,32,512]{2,1,0:T(8,128)(2,1)}), bf16[4,32,512]{2,1,0:T(8,128)(2,1)S(1)}, u32[]{:S(2)}, u32[]{:S(2)}) async-start(bf16[4,32,512]{2,1,0:T(8,128)(2,1)} %broadcast_in_dim.138), calls=%async_computation.2 | async-start | bytes 262144 | tf_op jit(solution)/shard_map/all_to_all | solution.py:19
  98.0 5.8 %all-to-all-done.2 = bf16[4,32,512]{2,1,0:T(8,128)(2,1)S(1)} async-done(((bf16[4,32,512]{2,1,0:T(8,128)(2,1)}), bf16[4,32,512]{2,1,0:T(8,128)(2,1)S(1)}, u32[]{:S(2)}, u32[]{:S(2)}) %all-to-all-start.2) | async-done | bytes 131104 | tf_op jit(solution)/shard_map/all_to_all | solution.py:19
  104.0 1.1 fusion.88
  105.3 0.3 reduce-precision_convert_fusion
  105.8 1.7 fusion.11
  107.8 0.7 copy.125
  108.5 5.0 %all-to-all-start.3 = ((bf16[32,16,128]{2,1,0:T(8,128)(2,1)}), bf16[32,16,128]{2,1,0:T(8,128)(2,1)S(1)}, u32[]{:S(2)}, u32[]{:S(2)}) async-start(bf16[32,16,128]{2,1,0:T(8,128)(2,1)} %copy.125), calls=%async_computation.3 | async-start | bytes 262144 | tf_op jit(solution)/shard_map/all_to_all | solution.py:19
  113.5 4.2 %fusion = f32[512,768]{1,0:T(8,128)} fusion(bf16[512,1536]{1,0:T(8,128)(2,1)S(1)} %bitcast.103, bf16[4,768,1536]{2,1,0:T(8,128)(2,1)} %all-gather.6.cloned.1.call-done), kind=kOutput, calls=%fused_computation.4 | convolution fusion | flops 1207959552 | bytes 5505024 | tf_op jit(solution)/shard_map/dot_general | solution.py:13
  117.7 7.2 %convolution_convert_fusion = bf16[512,1536]{1,0:T(8,128)(2,1)} fusion(bf16[4,768,1536]{2,1,0:T(8,128)(2,1)} %all-gather.6.cloned.1.call-done, f32[512,768]{1,0:T(8,128)} %fusion, bf16[512,1536]{1,0:T(8,128)(2,1)S(1)} %bitcast.104), kind=kOutput, calls=%fused_computation | convolution fusion | flops 2417885184 | bytes 9437184 | tf_op jit(solution)/shard_map/dot_general | solution.py:51
  124.9 10.0 %all-to-all-start.4 = ((bf16[32,16,1536]{2,1,0:T(8,128)(2,1)}), bf16[32,16,1536]{2,1,0:T(8,128)(2,1)S(1)}, u32[]{:S(2)}, u32[]{:S(2)}) async-start(bf16[32,16,1536]{2,1,0:T(8,128)(2,1)} %bitcast.21), calls=%async_computation.4 | async-start | bytes 3145728 | tf_op jit(solution)/shard_map/all_to_all | solution.py:19
  135.4 0.2 fusion.46
  135.7 0.1 slice_add_fusion.1
  135.9 0.1 multiply_reduce_fusion.1
  136.1 12.3 %all-gather.2 = bf16[4,1,1536]{2,1,0:T(2,128)(2,1)S(1)} all-gather(bf16[1,1,1536]{2,1,0:T(2,128)(2,1)S(1)} %reshape.255), channel_id=1, replica_groups=mesh['dp'=16,'y'=8,'x'=4] {'x'}, dimensions={0}, use_global_device_ids=true | all-gather | bytes 15360 | tf_op jit(solution)/shard_map/all_gather | solution.py:198
  148.4 1.7 fusion.10
  150.1 19.1 %all-gather.3 = bf16[16,4,384]{2,1,0:T(4,128)(2,1)S(1)} all-gather(bf16[1,4,384]{2,1,0:T(4,128)(2,1)S(1)} %fusion.10), channel_id=1, replica_groups=mesh['dp'=16,'y'=8,'x'=4] {'dp'}, dimensions={0}, use_global_device_ids=true | all-gather | bytes 52224 | tf_op jit(solution)/shard_map/all_gather | solution.py:200
  169.1 0.9 fusion.7
  170.1 1.4 all-to-all-done.4
  171.5 5.9 %all-to-all-start.5 = ((bf16[8,32,384]{2,1,0:T(8,128)(2,1)}), bf16[8,32,384]{2,1,0:T(8,128)(2,1)S(1)}, u32[]{:S(2)}, u32[]{:S(2)}) async-start(bf16[8,32,384]{2,1,0:T(8,128)(2,1)} %bitcast.25), calls=%async_computation.5 | async-start | bytes 393216 | tf_op jit(solution)/shard_map/all_to_all | solution.py:19
  177.4 0.2 slice_reduce_fusion.1
  177.6 4.9 %slice.106 = bf16[2,768,1536]{2,1,0:T(8,128)(2,1)} slice(bf16[4,768,1536]{2,1,0:T(8,128)(2,1)} %all-gather.6.cloned.1.call-done), slice={[0:2], [0:768], [0:1536]} | slice | bytes 9437184 | tf_op jit(solution)/shard_map/slice | solution.py:45
  182.4 0.4 convolution_bitcast_fusion.2
  182.9 4.0 %all-to-all-done.5 = bf16[8,32,384]{2,1,0:T(8,128)(2,1)S(1)} async-done(((bf16[8,32,384]{2,1,0:T(8,128)(2,1)}), bf16[8,32,384]{2,1,0:T(8,128)(2,1)S(1)}, u32[]{:S(2)}, u32[]{:S(2)}) %all-to-all-start.5) | async-done | bytes 196640 | tf_op jit(solution)/shard_map/all_to_all | solution.py:19
  186.9 0.7 broadcast_in_dim.150
  187.6 3.8 %all-to-all-start.6 = ((bf16[4,32,384]{2,1,0:T(8,128)(2,1)}), bf16[4,32,384]{2,1,0:T(8,128)(2,1)S(1)}, u32[]{:S(2)}, u32[]{:S(2)}) async-start(bf16[4,32,384]{2,1,0:T(8,128)(2,1)} %broadcast_in_dim.150), calls=%async_computation.6 | async-start | bytes 196608 | tf_op jit(solution)/shard_map/all_to_all | solution.py:19
  191.4 0.4 fusion.4
  191.8 5.4 %all-to-all-done.6 = bf16[4,32,384]{2,1,0:T(8,128)(2,1)S(1)} async-done(((bf16[4,32,384]{2,1,0:T(8,128)(2,1)}), bf16[4,32,384]{2,1,0:T(8,128)(2,1)S(1)}, u32[]{:S(2)}, u32[]{:S(2)}) %all-to-all-start.6) | async-done | bytes 98336 | tf_op jit(solution)/shard_map/all_to_all | solution.py:19
  197.5 3.8 %fusion.89 = f32[32,1536]{1,0:T(8,128)S(1)} fusion(bf16[32,1536]{1,0:T(8,128)(2,1)S(1)} %bitcast.110, bf16[1536,1536]{1,0:T(8,128)(2,1)} %bitcast.102), kind=kOutput, calls=%fused_computation.158 | convolution fusion | flops 150994944 | bytes 5013504 | tf_op jit(solution)/shard_map/dot_general | solution.py:13
  201.2 2.2 convolution_convert_fusion.2
  203.5 0.7 reshape.249
  204.2 5.0 %all-to-all-start.7 = ((bf16[32,12,128]{2,1,0:T(8,128)(2,1)}), bf16[32,12,128]{2,1,0:T(8,128)(2,1)S(1)}, u32[]{:S(2)}, u32[]{:S(2)}) async-start(bf16[32,12,128]{2,1,0:T(8,128)(2,1)} %reshape.249), calls=%async_computation.7 | async-start | bytes 262144 | tf_op jit(solution)/shard_map/all_to_all | solution.py:19
  209.2 1.1 fusion.5
  210.3 8.5 %all-to-all-done.7 = bf16[32,12,128]{2,1,0:T(8,128)(2,1)S(1)} async-done(((bf16[32,12,128]{2,1,0:T(8,128)(2,1)}), bf16[32,12,128]{2,1,0:T(8,128)(2,1)S(1)}, u32[]{:S(2)}, u32[]{:S(2)}) %all-to-all-start.7) | async-done | bytes 98336 | tf_op jit(solution)/shard_map/all_to_all | solution.py:19
  218.9 0.6 fusion.77
  (100 shorter events, 2.6 us)
Async XLA Ops:
  7.2 11.2 %copy-start.1 = (bf16[1,48,1536]{2,1,0:T(8,128)(2,1)S(1)}, bf16[1,48,1536]{2,1,0:T(8,128)(2,1)}, u32[]{:S(2)}) copy-start(bf16[1,48,1536]{2,1,0:T(8,128)(2,1)} %param.31) | copy-start | bytes 442372
  7.2 11.2 %copy-start.2 = (bf16[1,48,1536]{2,1,0:T(8,128)(2,1)S(1)}, bf16[1,48,1536]{2,1,0:T(8,128)(2,1)}, u32[]{:S(2)}) copy-start(bf16[1,48,1536]{2,1,0:T(8,128)(2,1)} %param.30) | copy-start | bytes 442372
  7.2 11.2 %copy-start.3 = (bf16[1,48,1536]{2,1,0:T(8,128)(2,1)S(1)}, bf16[1,48,1536]{2,1,0:T(8,128)(2,1)}, u32[]{:S(2)}) copy-start(bf16[1,48,1536]{2,1,0:T(8,128)(2,1)} %param.29) | copy-start | bytes 442372
  7.2 106.3 %all-gather.6.cloned.1.call-start = ((), (), s32[]{:S(2)}) async-start(), calls=%async_computation.8 | async-start | bytes 10027008 | tf_op jit(solution)/shard_map/all_gather | solution.py:119
  7.2 11.1 %collective-permute-start = (bf16[48,1536]{1,0:T(8,128)(2,1)}, bf16[48,1536]{1,0:T(8,128)(2,1)S(1)}, u32[]{:S(2)}, u32[]{:S(2)}) collective-permute-start(bf16[48,1536]{1,0:T(8,128)(2,1)} %bitcast.120), channel_id=1, source_target_pairs={{0,0},{1,32},{2,64},{3,96},{4,128},{5,160},{6,192},{7,224},{8,1},{... | collective-permute-start | bytes 442376 | tf_op jit(solution)/shard_map/ppermute | solution.py:92
  15.5 3.7 %copy-start.7 = (bf16[1,1536]{1,0:T(2,128)(2,1)S(1)}, bf16[1,1536]{1,0:T(2,128)(2,1)}, u32[]{:S(2)}) copy-start(bf16[1,1536]{1,0:T(2,128)(2,1)} %param.18) | copy-start | bytes 9220
  15.6 3.7 %copy-start.8 = (bf16[1,1536]{1,0:T(2,128)(2,1)S(1)}, bf16[1,1536]{1,0:T(2,128)(2,1)}, u32[]{:S(2)}) copy-start(bf16[1,1536]{1,0:T(2,128)(2,1)} %param.16) | copy-start | bytes 9220
  15.6 3.7 %copy-start.9 = (bf16[1,512]{1,0:T(2,128)(2,1)S(1)}, bf16[1,512]{1,0:T(2,128)(2,1)}, u32[]{:S(2)}) copy-start(bf16[1,512]{1,0:T(2,128)(2,1)} %param.17) | copy-start | bytes 3076
  19.3 19.7 %copy-start.10 = (s32[512]{0:T(512)S(1)}, s32[512]{0:T(512)}, u32[]{:S(2)}) copy-start(s32[512]{0:T(512)} %param.19) | copy-start | bytes 6148
  19.3 58.9 %all-to-all-start = ((bf16[32,16,1536]{2,1,0:T(8,128)(2,1)}), bf16[32,16,1536]{2,1,0:T(8,128)(2,1)S(1)}, u32[]{:S(2)}, u32[]{:S(2)}) async-start(bf16[32,16,1536]{2,1,0:T(8,128)(2,1)} %bitcast.4), calls=%async_computation | async-start | bytes 3145728 | tf_op jit(solution)/shard_map/all_to_all | solution.py:19
  38.9 58.9 %copy-start.11 = (s32[32]{0:T(128)S(1)}, s32[32]{0:T(128)}, u32[]{:S(2)}) copy-start(s32[32]{0:T(128)} %param.20) | copy-start | bytes 388
  39.0 58.9 %copy-start.12 = (s32[32]{0:T(128)S(1)}, s32[32]{0:T(128)}, u32[]{:S(2)}) copy-start(s32[32]{0:T(128)} %param.21) | copy-start | bytes 388
  39.0 65.0 %copy-start.13 = (bf16[32,2,64,128]{3,2,1,0:T(8,128)(2,1)S(1)}, bf16[32,2,64,128]{3,2,1,0:T(8,128)(2,1)}, u32[]{:S(2)}) copy-start(bf16[32,2,64,128]{3,2,1,0:T(8,128)(2,1)} %param.22) | copy-start | bytes 3145732
  78.2 14.7 %all-to-all-start.1 = ((bf16[8,32,512]{2,1,0:T(8,128)(2,1)}), bf16[8,32,512]{2,1,0:T(8,128)(2,1)S(1)}, u32[]{:S(2)}, u32[]{:S(2)}) async-start(bf16[8,32,512]{2,1,0:T(8,128)(2,1)} %bitcast.5), calls=%async_computation.1 | async-start | bytes 524288 | tf_op jit(solution)/shard_map/all_to_all | solution.py:19
  93.6 10.2 %all-to-all-start.2 = ((bf16[4,32,512]{2,1,0:T(8,128)(2,1)}), bf16[4,32,512]{2,1,0:T(8,128)(2,1)S(1)}, u32[]{:S(2)}, u32[]{:S(2)}) async-start(bf16[4,32,512]{2,1,0:T(8,128)(2,1)} %broadcast_in_dim.138), calls=%async_computation.2 | async-start | bytes 262144 | tf_op jit(solution)/shard_map/all_to_all | solution.py:19
  108.5 16.4 %all-to-all-start.3 = ((bf16[32,16,128]{2,1,0:T(8,128)(2,1)}), bf16[32,16,128]{2,1,0:T(8,128)(2,1)S(1)}, u32[]{:S(2)}, u32[]{:S(2)}) async-start(bf16[32,16,128]{2,1,0:T(8,128)(2,1)} %copy.125), calls=%async_computation.3 | async-start | bytes 262144 | tf_op jit(solution)/shard_map/all_to_all | solution.py:19
  124.9 10.4 %copy-start.6 = (f32[64,4]{0,1:T(4,128)S(1)}, f32[64,4]{0,1:T(4,128)}, u32[]{:S(2)}) copy-start(f32[64,4]{0,1:T(4,128)} %param.27) | copy-start | bytes 3076
  124.9 10.4 %copy-start.5 = (s32[64,4]{0,1:T(4,128)S(1)}, s32[64,4]{0,1:T(4,128)}, u32[]{:S(2)}) copy-start(s32[64,4]{0,1:T(4,128)} %param.26) | copy-start | bytes 3076
  124.9 46.6 %all-to-all-start.4 = ((bf16[32,16,1536]{2,1,0:T(8,128)(2,1)}), bf16[32,16,1536]{2,1,0:T(8,128)(2,1)S(1)}, u32[]{:S(2)}, u32[]{:S(2)}) async-start(bf16[32,16,1536]{2,1,0:T(8,128)(2,1)} %bitcast.21), calls=%async_computation.4 | async-start | bytes 3145728 | tf_op jit(solution)/shard_map/all_to_all | solution.py:19
  135.6 41.7 %copy-start.4 = (f32[1536]{0:T(1024)S(1)}, f32[1536]{0:T(1024)}, u32[]{:S(2)}) copy-start(f32[1536]{0:T(1024)} %param.28) | copy-start | bytes 18436
  171.5 15.4 %all-to-all-start.5 = ((bf16[8,32,384]{2,1,0:T(8,128)(2,1)}), bf16[8,32,384]{2,1,0:T(8,128)(2,1)S(1)}, u32[]{:S(2)}, u32[]{:S(2)}) async-start(bf16[8,32,384]{2,1,0:T(8,128)(2,1)} %bitcast.25), calls=%async_computation.5 | async-start | bytes 393216 | tf_op jit(solution)/shard_map/all_to_all | solution.py:19
  187.6 9.6 %all-to-all-start.6 = ((bf16[4,32,384]{2,1,0:T(8,128)(2,1)}), bf16[4,32,384]{2,1,0:T(8,128)(2,1)S(1)}, u32[]{:S(2)}, u32[]{:S(2)}) async-start(bf16[4,32,384]{2,1,0:T(8,128)(2,1)} %broadcast_in_dim.150), calls=%async_computation.6 | async-start | bytes 196608 | tf_op jit(solution)/shard_map/all_to_all | solution.py:19
  201.2 8.0 %copy-start = (bf16[63,1536]{1,0:T(8,128)(2,1)S(1)}, bf16[63,1536]{1,0:T(8,128)(2,1)}, u32[]{:S(2)}) copy-start(bf16[63,1536]{1,0:T(8,128)(2,1)} %param.25) | copy-start | bytes 580612
  204.2 14.6 %all-to-all-start.7 = ((bf16[32,12,128]{2,1,0:T(8,128)(2,1)}), bf16[32,12,128]{2,1,0:T(8,128)(2,1)S(1)}, u32[]{:S(2)}, u32[]{:S(2)}) async-start(bf16[32,12,128]{2,1,0:T(8,128)(2,1)} %reshape.249), calls=%async_computation.7 | async-start | bytes 262144 | tf_op jit(solution)/shard_map/all_to_all | solution.py:19
Sparse Core Ops, SparseCore 0:
  19.4 78.8 all-gather.5

commit v7 on v6

--- a/solution.py
+++ b/solution.py
@@ -19,11 +19,6 @@
     return lax.all_to_all(blocks, axis_name, split_axis=0, concat_axis=0, tiled=True)
 
 
-def spread(block, axis_name):
-    members = lax.axis_size(axis_name) if isinstance(axis_name, str) else lax.psum(1, axis_name)
-    return swap(jnp.broadcast_to(block[None], (members,) + block.shape), axis_name)
-
-
 def choose_rows(table, rows):
     return jnp.dot(table.astype(BF16), rows, preferred_element_type=F32).astype(BF16)
 
@@ -40,13 +35,16 @@
     return (rows_f32 * lax.rsqrt(mean_square + 1e-06) * gain).astype(BF16)
 
 
-def expert_units(rows, units, joined=False):
-    if joined:
-        both = contract_rows(rows, units[:2].reshape(-1, units.shape[2]))
-        gate, upper = both[:, : units.shape[1]], both[:, units.shape[1] :]
-    else:
-        gate = contract_rows(rows, units[0])
-        upper = contract_rows(rows, units[1])
+def sum_and_copy(parts, copies):
+    count, rows, columns = parts.shape
+    same = jnp.arange(copies * rows, dtype=jnp.int32)[:, None] % rows
+    same = same == jnp.arange(count * rows, dtype=jnp.int32)[None, :] % rows
+    return choose_rows(same, parts.reshape(count * rows, columns)).reshape(copies, rows, columns)
+
+
+def expert_units(rows, units):
+    gate = contract_rows(rows, units[0])
+    upper = contract_rows(rows, units[1])
     active = (jnp.maximum(gate, 0.0) * upper).astype(BF16)
     return jnp.dot(active, units[2], preferred_element_type=F32).astype(BF16)
 
@@ -110,7 +108,7 @@
     x_f32 = x_pre.astype(F32)
     outgoing = lax.dot_general(
         pick_table.astype(BF16),
-        rms(x_f32, moe_gain),
+        lax.optimization_barrier(rms(x_f32, moe_gain)),
         (((0,), (0,)), ((), ())),
         preferred_element_type=F32,
     ).astype(BF16)
@@ -142,8 +140,8 @@
     held = (held + jnp.arange(posts, dtype=jnp.int32)[None, :]).reshape(1, dp_size * posts)
     mine = choose_rows(jnp.tile(wanted, lines)[:, None] == held, all_rows)
     mine, received = lax.optimization_barrier((mine, received))
-    chosen = jnp.sum(swap(mine.reshape(lines, group_reqs, share), "y").astype(F32), axis=0).astype(BF16)
-    cached = spread(chosen, "x").reshape(posts, group_reqs, columns // posts, head_size)
+    chosen = swap(mine.reshape(lines, group_reqs, share), "y")
+    cached = swap(sum_and_copy(chosen, posts), "x").reshape(posts, group_reqs, columns // posts, head_size)
     cached = jnp.transpose(cached, (1, 0, 2, 3)).reshape(group_reqs, columns, head_size)
     query_head_list = cached[:, :heads].reshape(group_reqs, kv_heads, per_group, head_size)
     incoming_key = cached[:, heads : heads + kv_heads][:, :, None, :]
@@ -208,11 +206,10 @@
     at_home = at_home.astype(BF16)
     at_home, returned = lax.optimization_barrier((at_home, returned))
     at_home = swap(at_home.reshape(lines, group_reqs, post_columns), "y")
-    hidden_share = jnp.sum(at_home.astype(F32), axis=0).astype(BF16)
-    hidden_all = jnp.transpose(spread(hidden_share, "x"), (1, 0, 2)).reshape(group_reqs, width)
+    hidden_all = jnp.transpose(swap(sum_and_copy(at_home, posts), "x"), (1, 0, 2)).reshape(group_reqs, width)
     hidden_f32 = lax.dynamic_slice_in_dim(hidden_all, tp_lane, 1).astype(F32)
 
-    dec_out = expert_units(rms(hidden_all.astype(F32), moe_gain), units, joined=True)
+    dec_out = expert_units(rms(hidden_all.astype(F32), moe_gain), units)
     dec_back = swap(dec_out.reshape(group_reqs, heads, head_size), TP).astype(F32)
     dec_weight = weight_of[pre_rows:].reshape(experts, 1, 1)
     dec_mixture = jnp.sum(dec_weight * dec_back, axis=0).reshape(1, width)

time: 228 us -> 227 us (level)
  local copies, waits for them, and re-layouts: 9.27 us -> 3.07 us
  waiting for transfers between devices: 40.7 us -> 45.6 us
    slice x1 -> x0, local copies, waits for them, and re-layouts: 4.88 us -> none  [expert_units(): both = contract_rows(rows, units[:2].reshape(-1, units.shape[2]))]
    all_to_all x8, waiting for transfers between devices: 40.7 us -> 45.5 us  [swap(): lax.all_to_all(blocks, axis_name, split_axis=0, concat_axis=0, tiled=True)]
    dot_general x3, matrix products: 9.72 us -> 7.18 us  [contract_rows(): lax.dot_general(left_rows, unit_rows, (((1,), (1,)), ((), ())), preferred...]
  transfers between devices with their start and end apart: 10 -> 10, of which waited for: 7 -> 7; matrix products, arithmetic and copies ran while one was open for 15% -> 12% of each run, Pallas kernels for 0% -> 0%
where the time goes in v7:
time: 227 us; the launch traced here: 225 us
  starting transfers between devices  64.9 us (29%)
  blocking collectives  63 us (28%)
  waiting for transfers between devices  45.6 us (20%)
  matrix products  28.3 us (12%)
  between operations  14.6 us (6%)
  other arithmetic  5.94 us (3%)
  local copies, waits for them, and re-layouts  3.07 us (1%)
    all_to_all x8, starting transfers between devices, swap(): lax.all_to_all(blocks, axis_name, split_axis=0, concat_axis=0, tiled=True)  58.8 us
    all_to_all x8, waiting for transfers between devices, swap(): lax.all_to_all(blocks, axis_name, split_axis=0, concat_axis=0, tiled=True)  45.5 us
    all_gather x1, blocking collectives, on_device(): all_rows = lax.all_gather(line_share, 'dp', axis=0, tiled=True)  19.3 us
    all_gather x1, blocking collectives, on_device(): all_projected = lax.all_gather(projected, 'dp', axis=0, tiled=True)  19 us
    all_gather x1, blocking collectives, on_device(): line_fresh = lax.all_gather(fresh, 'x', axis=0, tiled=True)  12.3 us
    all_gather x1, blocking collectives, on_device(): lax.all_gather(attention_row.reshape(1, width), 'x', axis=0, tiled=True)  12.3 us
    dot_general x2, matrix products, expert_units(): return jnp.dot(active, units[2], preferred_element_type=F32).astype(BF16)  10.6 us
    dot_general x3, matrix products, contract_rows(): lax.dot_general(left_rows, unit_rows, (((1,), (1,)), ((), ())), preferred...  7.18 us
  transfers between devices with their start and end apart: 10, of which 7 were waited for; matrix products, arithmetic and copies ran while one was open for 12% of the time, Pallas kernels for 0%

profile of v7, /device:TPU:8, one launch (start us, length us, event | category | flops | bytes accessed | tf_op | source)
XLA Modules:
  0.0 225.4 jit_solution(9326636744582163755)
XLA Ops:
  7.2 6.1 %collective-permute-start = (bf16[48,1536]{1,0:T(8,128)(2,1)}, bf16[48,1536]{1,0:T(8,128)(2,1)S(1)}, u32[]{:S(2)}, u32[]{:S(2)}) collective-permute-start(bf16[48,1536]{1,0:T(8,128)(2,1)} %bitcast.143), channel_id=1, source_target_pairs={{0,0},{1,32},{2,64},{3,96},{4,128},{5,160},{6,192},{7,224},{8,1},{... | collective-permute-start | bytes 442376 | tf_op jit(solution)/shard_map/ppermute | solution.py:90
  13.4 0.7 iota_compare_fusion.1
  14.3 1.1 fusion.24
  15.4 1.1 fusion.26
  16.4 0.1 fusion.36
  16.6 1.7 convolution_convert_fusion.1
  18.4 0.9 pad_maximum_fusion
  19.4 19.6 %all-to-all-start = ((bf16[32,16,1536]{2,1,0:T(8,128)(2,1)}), bf16[32,16,1536]{2,1,0:T(8,128)(2,1)S(1)}, u32[]{:S(2)}, u32[]{:S(2)}) async-start(bf16[32,16,1536]{2,1,0:T(8,128)(2,1)} %bitcast.4), calls=%async_computation | async-start | bytes 3145728 | tf_op jit(solution)/shard_map/all_to_all | solution.py:19
  39.3 12.3 %all-gather = bf16[4,1,3584]{2,1,0:T(2,128)(2,1)S(1)} all-gather(bf16[1,1,3584]{2,1,0:T(2,128)(2,1)S(1)} %bitcast.140), channel_id=1, replica_groups=mesh['dp'=16,'y'=8,'x'=4] {'x'}, dimensions={0}, use_global_device_ids=true | all-gather | bytes 35840 | tf_op jit(solution)/shard_map/all_gather | solution.py:131
  51.7 19.3 %all-gather.1 = bf16[16,4,512]{2,1,0:T(4,128)(2,1)S(1)} all-gather(bf16[1,4,512]{2,1,0:T(4,128)(2,1)S(1)} %bitcast.142), channel_id=1, replica_groups=mesh['dp'=16,'y'=8,'x'=4] {'dp'}, dimensions={0}, use_global_device_ids=true | all-gather | bytes 69632 | tf_op jit(solution)/shard_map/all_gather | solution.py:137
  71.1 1.0 convolution_convert_fusion.3
  72.0 6.2 %all-to-all-done = bf16[32,16,1536]{2,1,0:T(8,128)(2,1)S(1)} async-done(((bf16[32,16,1536]{2,1,0:T(8,128)(2,1)}), bf16[32,16,1536]{2,1,0:T(8,128)(2,1)S(1)}, u32[]{:S(2)}, u32[]{:S(2)}) %all-to-all-start) | async-done | bytes 1572896 | tf_op jit(solution)/shard_map/all_to_all | solution.py:19
  78.2 5.3 %all-to-all-start.1 = ((bf16[8,32,512]{2,1,0:T(8,128)(2,1)}), bf16[8,32,512]{2,1,0:T(8,128)(2,1)S(1)}, u32[]{:S(2)}, u32[]{:S(2)}) async-start(bf16[8,32,512]{2,1,0:T(8,128)(2,1)} %bitcast.5), calls=%async_computation.1 | async-start | bytes 524288 | tf_op jit(solution)/shard_map/all_to_all | solution.py:19
  83.5 9.4 %all-to-all-done.1 = bf16[8,32,512]{2,1,0:T(8,128)(2,1)S(1)} async-done(((bf16[8,32,512]{2,1,0:T(8,128)(2,1)}), bf16[8,32,512]{2,1,0:T(8,128)(2,1)S(1)}, u32[]{:S(2)}, u32[]{:S(2)}) %all-to-all-start.1) | async-done | bytes 262176 | tf_op jit(solution)/shard_map/all_to_all | solution.py:19
  92.9 0.9 convolution_convert_fusion.4
  93.8 4.3 %all-to-all-start.2 = ((bf16[4,32,512]{2,1,0:T(8,128)(2,1)}), bf16[4,32,512]{2,1,0:T(8,128)(2,1)S(1)}, u32[]{:S(2)}, u32[]{:S(2)}) async-start(bf16[4,32,512]{2,1,0:T(8,128)(2,1)} %bitcast.7), calls=%async_computation.2 | async-start | bytes 262144 | tf_op jit(solution)/shard_map/all_to_all | solution.py:19
  98.2 5.8 %all-to-all-done.2 = bf16[4,32,512]{2,1,0:T(8,128)(2,1)S(1)} async-done(((bf16[4,32,512]{2,1,0:T(8,128)(2,1)}), bf16[4,32,512]{2,1,0:T(8,128)(2,1)S(1)}, u32[]{:S(2)}, u32[]{:S(2)}) %all-to-all-start.2) | async-done | bytes 131104 | tf_op jit(solution)/shard_map/all_to_all | solution.py:19
  104.1 1.1 fusion.92
  105.3 0.3 reduce-precision_convert_fusion
  105.6 1.7 fusion.16
  107.9 0.7 copy.103
  108.6 5.0 %all-to-all-start.3 = ((bf16[32,16,128]{2,1,0:T(8,128)(2,1)}), bf16[32,16,128]{2,1,0:T(8,128)(2,1)S(1)}, u32[]{:S(2)}, u32[]{:S(2)}) async-start(bf16[32,16,128]{2,1,0:T(8,128)(2,1)} %copy.103), calls=%async_computation.3 | async-start | bytes 262144 | tf_op jit(solution)/shard_map/all_to_all | solution.py:19
  113.6 3.1 %fusion.5 = f32[512,768]{1,0:T(8,128)S(1)} fusion(bf16[512,1536]{1,0:T(8,128)(2,1)S(1)} %bitcast.124, bf16[4,768,1536]{2,1,0:T(8,128)(2,1)} %all-gather.6.cloned.1.call-done), kind=kOutput, calls=%fused_computation.14 | convolution fusion | flops 1207959552 | bytes 5505024 | tf_op jit(solution)/shard_map/dot_general | solution.py:13
  116.7 6.7 %convolution_convert_fusion = bf16[512,1536]{1,0:T(8,128)(2,1)} fusion(bf16[4,768,1536]{2,1,0:T(8,128)(2,1)} %all-gather.6.cloned.1.call-done, f32[512,768]{1,0:T(8,128)S(1)} %fusion.5, bf16[512,1536]{1,0:T(8,128)(2,1)S(1)} %bitcast.125), kind=kOutput, calls=%fused_computation | convolution fusion | flops 2417885184 | bytes 9437184 | tf_op jit(solution)/shard_map/dot_general | solution.py:49
  123.4 10.0 %all-to-all-start.4 = ((bf16[32,16,1536]{2,1,0:T(8,128)(2,1)}), bf16[32,16,1536]{2,1,0:T(8,128)(2,1)S(1)}, u32[]{:S(2)}, u32[]{:S(2)}) async-start(bf16[32,16,1536]{2,1,0:T(8,128)(2,1)} %bitcast.24), calls=%async_computation.4 | async-start | bytes 3145728 | tf_op jit(solution)/shard_map/all_to_all | solution.py:19
  133.9 0.2 fusion.50
  134.2 0.1 slice_add_fusion.1
  134.4 0.1 multiply_reduce_fusion.1
  134.6 12.3 %all-gather.2 = bf16[4,1,1536]{2,1,0:T(2,128)(2,1)S(1)} all-gather(bf16[1,1,1536]{2,1,0:T(2,128)(2,1)S(1)} %reshape.305), channel_id=1, replica_groups=mesh['dp'=16,'y'=8,'x'=4] {'x'}, dimensions={0}, use_global_device_ids=true | all-gather | bytes 15360 | tf_op jit(solution)/shard_map/all_gather | solution.py:196
  146.9 1.7 fusion.15
  148.6 19.0 %all-gather.3 = bf16[16,4,384]{2,1,0:T(4,128)(2,1)S(1)} all-gather(bf16[1,4,384]{2,1,0:T(4,128)(2,1)S(1)} %fusion.15), channel_id=1, replica_groups=mesh['dp'=16,'y'=8,'x'=4] {'dp'}, dimensions={0}, use_global_device_ids=true | all-gather | bytes 52224 | tf_op jit(solution)/shard_map/all_gather | solution.py:198
  167.6 0.9 fusion.9
  168.6 1.4 all-to-all-done.4
  170.0 5.9 %all-to-all-start.5 = ((bf16[8,32,384]{2,1,0:T(8,128)(2,1)}), bf16[8,32,384]{2,1,0:T(8,128)(2,1)S(1)}, u32[]{:S(2)}, u32[]{:S(2)}) async-start(bf16[8,32,384]{2,1,0:T(8,128)(2,1)} %bitcast.28), calls=%async_computation.5 | async-start | bytes 393216 | tf_op jit(solution)/shard_map/all_to_all | solution.py:19
  175.9 0.2 slice_reduce_fusion.1
  176.0 0.4 convolution_bitcast_fusion.2
  176.5 8.9 %all-to-all-done.5 = bf16[8,32,384]{2,1,0:T(8,128)(2,1)S(1)} async-done(((bf16[8,32,384]{2,1,0:T(8,128)(2,1)}), bf16[8,32,384]{2,1,0:T(8,128)(2,1)S(1)}, u32[]{:S(2)}, u32[]{:S(2)}) %all-to-all-start.5) | async-done | bytes 196640 | tf_op jit(solution)/shard_map/all_to_all | solution.py:19
  185.4 0.9 convolution_convert_fusion.5
  186.2 3.9 %all-to-all-start.6 = ((bf16[4,32,384]{2,1,0:T(8,128)(2,1)}), bf16[4,32,384]{2,1,0:T(8,128)(2,1)S(1)}, u32[]{:S(2)}, u32[]{:S(2)}) async-start(bf16[4,32,384]{2,1,0:T(8,128)(2,1)} %bitcast.30), calls=%async_computation.6 | async-start | bytes 196608 | tf_op jit(solution)/shard_map/all_to_all | solution.py:19
  190.1 0.4 fusion.2
  190.5 5.4 %all-to-all-done.6 = bf16[4,32,384]{2,1,0:T(8,128)(2,1)S(1)} async-done(((bf16[4,32,384]{2,1,0:T(8,128)(2,1)}), bf16[4,32,384]{2,1,0:T(8,128)(2,1)S(1)}, u32[]{:S(2)}, u32[]{:S(2)}) %all-to-all-start.6) | async-done | bytes 98336 | tf_op jit(solution)/shard_map/all_to_all | solution.py:19
  196.2 2.4 %fusion.12 = f32[32,768]{1,0:T(8,128)S(1)} fusion(bf16[32,1536]{1,0:T(8,128)(2,1)S(1)} %bitcast.137, bf16[4,768,1536]{2,1,0:T(8,128)(2,1)} %all-gather.6.cloned.1.call-done), kind=kOutput, calls=%fused_computation.28 | convolution fusion | flops 75522048 | bytes 2555904 | tf_op jit(solution)/shard_map/dot_general | solution.py:13
  198.6 3.9 %convolution_convert_fusion.2 = bf16[32,1536]{1,0:T(8,128)(2,1)S(1)} fusion(bf16[4,768,1536]{2,1,0:T(8,128)(2,1)} %all-gather.6.cloned.1.call-done, f32[32,768]{1,0:T(8,128)S(1)} %fusion.12, bf16[32,1536]{1,0:T(8,128)(2,1)S(1)} %bitcast.138), kind=kOutput, calls=%fused_computation.12 | convolution fusion | flops 151093248 | bytes 5013504 | tf_op jit(solution)/shard_map/dot_general | solution.py:49
  202.5 0.7 reshape.299
  203.3 5.0 %all-to-all-start.7 = ((bf16[32,12,128]{2,1,0:T(8,128)(2,1)}), bf16[32,12,128]{2,1,0:T(8,128)(2,1)S(1)}, u32[]{:S(2)}, u32[]{:S(2)}) async-start(bf16[32,12,128]{2,1,0:T(8,128)(2,1)} %reshape.299), calls=%async_computation.7 | async-start | bytes 262144 | tf_op jit(solution)/shard_map/all_to_all | solution.py:19
  208.3 1.1 fusion.3
  209.4 8.5 %all-to-all-done.7 = bf16[32,12,128]{2,1,0:T(8,128)(2,1)S(1)} async-done(((bf16[32,12,128]{2,1,0:T(8,128)(2,1)}), bf16[32,12,128]{2,1,0:T(8,128)(2,1)S(1)}, u32[]{:S(2)}, u32[]{:S(2)}) %all-to-all-start.7) | async-done | bytes 98336 | tf_op jit(solution)/shard_map/all_to_all | solution.py:19
  218.0 0.6 fusion.82
  (99 shorter events, 2.6 us)
Async XLA Ops:
  7.2 11.2 %copy-start.3 = (bf16[1,48,1536]{2,1,0:T(8,128)(2,1)S(1)}, bf16[1,48,1536]{2,1,0:T(8,128)(2,1)}, u32[]{:S(2)}) copy-start(bf16[1,48,1536]{2,1,0:T(8,128)(2,1)} %param.29) | copy-start | bytes 442372
  7.2 11.2 %copy-start.2 = (bf16[1,48,1536]{2,1,0:T(8,128)(2,1)S(1)}, bf16[1,48,1536]{2,1,0:T(8,128)(2,1)}, u32[]{:S(2)}) copy-start(bf16[1,48,1536]{2,1,0:T(8,128)(2,1)} %param.30) | copy-start | bytes 442372
  7.2 11.2 %copy-start.1 = (bf16[1,48,1536]{2,1,0:T(8,128)(2,1)S(1)}, bf16[1,48,1536]{2,1,0:T(8,128)(2,1)}, u32[]{:S(2)}) copy-start(bf16[1,48,1536]{2,1,0:T(8,128)(2,1)} %param.31) | copy-start | bytes 442372
  7.2 106.4 %all-gather.6.cloned.1.call-start = ((), (), s32[]{:S(2)}) async-start(), calls=%async_computation.8 | async-start | bytes 10027008 | tf_op jit(solution)/shard_map/all_gather | solution.py:117
  7.2 11.1 %collective-permute-start = (bf16[48,1536]{1,0:T(8,128)(2,1)}, bf16[48,1536]{1,0:T(8,128)(2,1)S(1)}, u32[]{:S(2)}, u32[]{:S(2)}) collective-permute-start(bf16[48,1536]{1,0:T(8,128)(2,1)} %bitcast.143), channel_id=1, source_target_pairs={{0,0},{1,32},{2,64},{3,96},{4,128},{5,160},{6,192},{7,224},{8,1},{... | collective-permute-start | bytes 442376 | tf_op jit(solution)/shard_map/ppermute | solution.py:90
  16.6 2.7 %copy-start.7 = (bf16[1,1536]{1,0:T(2,128)(2,1)S(1)}, bf16[1,1536]{1,0:T(2,128)(2,1)}, u32[]{:S(2)}) copy-start(bf16[1,1536]{1,0:T(2,128)(2,1)} %param.18) | copy-start | bytes 9220
  16.6 2.7 %copy-start.8 = (bf16[1,1536]{1,0:T(2,128)(2,1)S(1)}, bf16[1,1536]{1,0:T(2,128)(2,1)}, u32[]{:S(2)}) copy-start(bf16[1,1536]{1,0:T(2,128)(2,1)} %param.16) | copy-start | bytes 9220
  16.6 2.7 %copy-start.9 = (bf16[1,512]{1,0:T(2,128)(2,1)S(1)}, bf16[1,512]{1,0:T(2,128)(2,1)}, u32[]{:S(2)}) copy-start(bf16[1,512]{1,0:T(2,128)(2,1)} %param.17) | copy-start | bytes 3076
  19.3 19.6 %copy-start.10 = (s32[512]{0:T(512)S(1)}, s32[512]{0:T(512)}, u32[]{:S(2)}) copy-start(s32[512]{0:T(512)} %param.19) | copy-start | bytes 6148
  19.4 58.9 %all-to-all-start = ((bf16[32,16,1536]{2,1,0:T(8,128)(2,1)}), bf16[32,16,1536]{2,1,0:T(8,128)(2,1)S(1)}, u32[]{:S(2)}, u32[]{:S(2)}) async-start(bf16[32,16,1536]{2,1,0:T(8,128)(2,1)} %bitcast.4), calls=%async_computation | async-start | bytes 3145728 | tf_op jit(solution)/shard_map/all_to_all | solution.py:19
  38.9 59.1 %copy-start.11 = (s32[32]{0:T(128)S(1)}, s32[32]{0:T(128)}, u32[]{:S(2)}) copy-start(s32[32]{0:T(128)} %param.20) | copy-start | bytes 388
  39.0 59.1 %copy-start.12 = (s32[32]{0:T(128)S(1)}, s32[32]{0:T(128)}, u32[]{:S(2)}) copy-start(s32[32]{0:T(128)} %param.21) | copy-start | bytes 388
  39.0 65.2 %copy-start.13 = (bf16[32,2,64,128]{3,2,1,0:T(8,128)(2,1)S(1)}, bf16[32,2,64,128]{3,2,1,0:T(8,128)(2,1)}, u32[]{:S(2)}) copy-start(bf16[32,2,64,128]{3,2,1,0:T(8,128)(2,1)} %param.22) | copy-start | bytes 3145732
  78.2 14.7 %all-to-all-start.1 = ((bf16[8,32,512]{2,1,0:T(8,128)(2,1)}), bf16[8,32,512]{2,1,0:T(8,128)(2,1)S(1)}, u32[]{:S(2)}, u32[]{:S(2)}) async-start(bf16[8,32,512]{2,1,0:T(8,128)(2,1)} %bitcast.5), calls=%async_computation.1 | async-start | bytes 524288 | tf_op jit(solution)/shard_map/all_to_all | solution.py:19
  93.8 10.2 %all-to-all-start.2 = ((bf16[4,32,512]{2,1,0:T(8,128)(2,1)}), bf16[4,32,512]{2,1,0:T(8,128)(2,1)S(1)}, u32[]{:S(2)}, u32[]{:S(2)}) async-start(bf16[4,32,512]{2,1,0:T(8,128)(2,1)} %bitcast.7), calls=%async_computation.2 | async-start | bytes 262144 | tf_op jit(solution)/shard_map/all_to_all | solution.py:19
  108.6 14.8 %all-to-all-start.3 = ((bf16[32,16,128]{2,1,0:T(8,128)(2,1)}), bf16[32,16,128]{2,1,0:T(8,128)(2,1)S(1)}, u32[]{:S(2)}, u32[]{:S(2)}) async-start(bf16[32,16,128]{2,1,0:T(8,128)(2,1)} %copy.103), calls=%async_computation.3 | async-start | bytes 262144 | tf_op jit(solution)/shard_map/all_to_all | solution.py:19
  123.4 10.3 %copy-start.6 = (f32[64,4]{0,1:T(4,128)S(1)}, f32[64,4]{0,1:T(4,128)}, u32[]{:S(2)}) copy-start(f32[64,4]{0,1:T(4,128)} %param.27) | copy-start | bytes 3076
  123.4 10.4 %copy-start.5 = (s32[64,4]{0,1:T(4,128)S(1)}, s32[64,4]{0,1:T(4,128)}, u32[]{:S(2)}) copy-start(s32[64,4]{0,1:T(4,128)} %param.26) | copy-start | bytes 3076
  123.4 46.6 %all-to-all-start.4 = ((bf16[32,16,1536]{2,1,0:T(8,128)(2,1)}), bf16[32,16,1536]{2,1,0:T(8,128)(2,1)S(1)}, u32[]{:S(2)}, u32[]{:S(2)}) async-start(bf16[32,16,1536]{2,1,0:T(8,128)(2,1)} %bitcast.24), calls=%async_computation.4 | async-start | bytes 3145728 | tf_op jit(solution)/shard_map/all_to_all | solution.py:19
  134.1 41.7 %copy-start.4 = (f32[1536]{0:T(1024)S(1)}, f32[1536]{0:T(1024)}, u32[]{:S(2)}) copy-start(f32[1536]{0:T(1024)} %param.28) | copy-start | bytes 18436
  170.0 15.4 %all-to-all-start.5 = ((bf16[8,32,384]{2,1,0:T(8,128)(2,1)}), bf16[8,32,384]{2,1,0:T(8,128)(2,1)S(1)}, u32[]{:S(2)}, u32[]{:S(2)}) async-start(bf16[8,32,384]{2,1,0:T(8,128)(2,1)} %bitcast.28), calls=%async_computation.5 | async-start | bytes 393216 | tf_op jit(solution)/shard_map/all_to_all | solution.py:19
  186.2 9.7 %all-to-all-start.6 = ((bf16[4,32,384]{2,1,0:T(8,128)(2,1)}), bf16[4,32,384]{2,1,0:T(8,128)(2,1)S(1)}, u32[]{:S(2)}, u32[]{:S(2)}) async-start(bf16[4,32,384]{2,1,0:T(8,128)(2,1)} %bitcast.30), calls=%async_computation.6 | async-start | bytes 196608 | tf_op jit(solution)/shard_map/all_to_all | solution.py:19
  198.6 9.7 %copy-start = (bf16[63,1536]{1,0:T(8,128)(2,1)S(1)}, bf16[63,1536]{1,0:T(8,128)(2,1)}, u32[]{:S(2)}) copy-start(bf16[63,1536]{1,0:T(8,128)(2,1)} %param.25) | copy-start | bytes 580612
  203.3 14.6 %all-to-all-start.7 = ((bf16[32,12,128]{2,1,0:T(8,128)(2,1)}), bf16[32,12,128]{2,1,0:T(8,128)(2,1)S(1)}, u32[]{:S(2)}, u32[]{:S(2)}) async-start(bf16[32,12,128]{2,1,0:T(8,128)(2,1)} %reshape.299), calls=%async_computation.7 | async-start | bytes 262144 | tf_op jit(solution)/shard_map/all_to_all | solution.py:19
Sparse Core Ops, SparseCore 0:
  19.4 78.8 all-gather.5

commit v8 on v7

--- a/solution.py
+++ b/solution.py
@@ -81,14 +81,6 @@
     experts = tp_size * w_gate.shape[0]
     assert group_reqs == tp_size and experts == tp_size
 
-    turned = []
-    for group in range(dp_size):
-        for lane in range(tp_size):
-            taker = lane % lines + group // lines * lines
-            place = (taker * lines + group % lines) * posts + lane // lines
-            turned.append((group * tp_size + lane, place))
-    post_part = lax.ppermute(w_out.T, ("dp", "y", "x"), turned)
-
     no_value = jnp.zeros((), BF16)
     rows_dev, top_count = routes.shape
     pre_rows = rows_dev - 1
@@ -113,27 +105,18 @@
         preferred_element_type=F32,
     ).astype(BF16)
 
-    post_part, outgoing = lax.optimization_barrier((post_part, outgoing))
     units = lax.all_gather(
-        jnp.concatenate([w_gate, w_up, w_down, post_part[None]], axis=0),
-        "dp",
-        axis=1,
-        tiled=True,
-    )
-    out_rows = units[3, : lines * w_out.shape[1]]
+        jnp.concatenate([w_gate, w_up, w_down], axis=0), "dp", axis=1, tiled=True
+    )
 
     columns = heads + 2 * kv_heads
     share = columns * head_size // posts
     post = lax.axis_index("x")
-    fresh = jnp.concatenate([q_new, new_key_value, resid_dec], axis=1)
+    fresh = jnp.concatenate([q_new, new_key_value], axis=1)
     fresh, outgoing = lax.optimization_barrier((fresh, outgoing))
     received = swap(outgoing.reshape(experts, capacity, width), TP)
     line_fresh = lax.all_gather(fresh, "x", axis=0, tiled=True)
     line_share = lax.dynamic_slice_in_dim(line_fresh, post * share, share, axis=1)
-    post_columns = width // posts
-    line_resid = lax.dynamic_slice_in_dim(
-        line_fresh, columns * head_size + post * post_columns, post_columns, axis=1
-    )
     all_rows = lax.all_gather(line_share, "dp", axis=0, tiled=True)
     wanted = lax.dynamic_slice_in_dim(placing, dp_group * group_reqs, group_reqs)
     held = jnp.arange(dp_size, dtype=jnp.int32)[:, None] * tp_size + line * posts
@@ -181,10 +164,6 @@
     )
     gathered = swap(parts, TP)
 
-    pre_out = expert_units(received.reshape(experts * capacity, width), units)
-    gathered, pre_out = lax.optimization_barrier((gathered, pre_out))
-    returned = swap(pre_out.reshape(experts, capacity, width), TP)
-
     tail = gathered[:, heads : heads + 2, : 3 * heads].astype(F32)
     tail = tail[..., :heads] + tail[..., heads : 2 * heads] + tail[..., 2 * heads :]
     peaks, totals = tail[:, 0], tail[:, 1]
@@ -193,20 +172,25 @@
     mixed = jnp.sum(scale[:, :, None] * gathered[:, :heads].astype(F32), axis=0)
     attention_row = (mixed / total[:, None]).astype(BF16)
 
-    attention = lax.all_gather(attention_row.reshape(1, width), "x", axis=0, tiled=True)
-    projected = contract_rows(attention, out_rows).astype(BF16)
+    rows = jnp.concatenate([attention_row, resid_dec.reshape(heads, head_size)], axis=0)
+    group_rows = swap(jnp.broadcast_to(rows[None], (tp_size,) + rows.shape), TP)
+
+    pre_out = expert_units(received.reshape(experts * capacity, width), units)
+    group_rows, pre_out = lax.optimization_barrier((group_rows, pre_out))
+    returned = swap(pre_out.reshape(experts, capacity, width), TP)
+
+    attention = group_rows[:, :heads].reshape(group_reqs, width)
+    resid_rows = group_rows[:, heads:].reshape(group_reqs, width)
+    projected = jnp.dot(attention, w_out, preferred_element_type=F32).astype(BF16)
     all_projected = lax.all_gather(projected, "dp", axis=0, tiled=True)
-    line_rows = placing.reshape(dp_size, lines, posts)
-    line_rows = lax.dynamic_slice_in_dim(line_rows, line, 1, axis=1).reshape(1, dp_size * posts)
-    lane_ids = jnp.tile(jnp.arange(group_reqs, dtype=jnp.int32), lines)[:, None]
-    from_cache = (dp_group * group_reqs + lane_ids == line_rows).astype(BF16)
-    from_line = lane_ids == line * posts + jnp.arange(posts, dtype=jnp.int32)[None, :]
-    at_home = jnp.dot(from_cache, all_projected, preferred_element_type=F32)
-    at_home = at_home + jnp.dot(from_line.astype(BF16), line_resid, preferred_element_type=F32)
-    at_home = at_home.astype(BF16)
+    home_ids = dp_group * group_reqs + jnp.arange(group_reqs, dtype=jnp.int32)
+    at_home = choose_rows(home_ids[:, None] == placing[None, :], all_projected)
     at_home, returned = lax.optimization_barrier((at_home, returned))
-    at_home = swap(at_home.reshape(lines, group_reqs, post_columns), "y")
-    hidden_all = jnp.transpose(swap(sum_and_copy(at_home, posts), "x"), (1, 0, 2)).reshape(group_reqs, width)
+    packed = at_home.reshape(heads, head_size)
+    packed = swap(jnp.broadcast_to(packed[None], (tp_size,) + packed.shape), TP)
+    proj_home = packed.reshape(tp_size, group_reqs, width // tp_size)
+    proj_home = jnp.transpose(proj_home, (1, 0, 2)).reshape(group_reqs, width)
+    hidden_all = (resid_rows.astype(F32) + proj_home.astype(F32)).astype(BF16)
     hidden_f32 = lax.dynamic_slice_in_dim(hidden_all, tp_lane, 1).astype(F32)
 
     dec_out = expert_units(rms(hidden_all.astype(F32), moe_gain), units)

time: 227 us -> 225 us (level)
  starting transfers between devices: 64.9 us -> 52.5 us
  waiting for transfers between devices: 45.6 us -> 57.7 us
  blocking collectives: 63 us -> 56 us
  local copies, waits for them, and re-layouts: 3.07 us -> 6.37 us
  other arithmetic: 5.94 us -> 8.47 us
    all_gather x1 -> x0, blocking collectives: 12.3 us -> none  [on_device(): lax.all_gather(attention_row.reshape(1, width), 'x', axis=0, tiled=True)]
    all_to_all x8, waiting for transfers between devices: 45.5 us -> 57.7 us  [swap(): lax.all_to_all(blocks, axis_name, split_axis=0, concat_axis=0, tiled=True)]
    all_to_all x8, starting transfers between devices: 58.8 us -> 52.5 us  [swap(): lax.all_to_all(blocks, axis_name, split_axis=0, concat_axis=0, tiled=True)]
    ppermute x1 -> x0, starting transfers between devices: 6.11 us -> none  [on_device(): post_part = lax.ppermute(w_out.T, ('dp', 'y', 'x'), turned)]
    all_gather x1, blocking collectives: 19.3 us -> 23.5 us  [on_device(): all_rows = lax.all_gather(line_share, 'dp', axis=0, tiled=True)]
    dot_general x3 -> x2, matrix products: 7.18 us -> 6.69 us  [contract_rows(): lax.dot_general(left_rows, unit_rows, (((1,), (1,)), ((), ())), preferred...]
  transfers between devices with their start and end apart: 10 -> 9, of which waited for: 7 -> 7; matrix products, arithmetic and copies ran while one was open for 12% -> 13% of each run, Pallas kernels for 0% -> 0%
where the time goes in v8:
time: 225 us; the launch traced here: 223 us
  waiting for transfers between devices  57.7 us (26%)
  blocking collectives  56 us (25%)
  starting transfers between devices  52.5 us (23%)
  matrix products  27.8 us (12%)
  between operations  14.6 us (6%)
  other arithmetic  8.47 us (4%)
  local copies, waits for them, and re-layouts  6.37 us (3%)
    all_to_all x8, waiting for transfers between devices, swap(): lax.all_to_all(blocks, axis_name, split_axis=0, concat_axis=0, tiled=True)  57.7 us
    all_to_all x8, starting transfers between devices, swap(): lax.all_to_all(blocks, axis_name, split_axis=0, concat_axis=0, tiled=True)  52.5 us
    all_gather x1, blocking collectives, on_device(): all_rows = lax.all_gather(line_share, 'dp', axis=0, tiled=True)  23.5 us
    all_gather x1, blocking collectives, on_device(): all_projected = lax.all_gather(projected, 'dp', axis=0, tiled=True)  20.2 us
    all_gather x1, blocking collectives, on_device(): line_fresh = lax.all_gather(fresh, 'x', axis=0, tiled=True)  12.3 us
    dot_general x2, matrix products, expert_units(): return jnp.dot(active, units[2], preferred_element_type=F32).astype(BF16)  11.1 us
    dot_general x2, matrix products, contract_rows(): lax.dot_general(left_rows, unit_rows, (((1,), (1,)), ((), ())), preferred...  6.69 us
  transfers between devices with their start and end apart: 9, of which 7 were waited for; matrix products, arithmetic and copies ran while one was open for 13% of the time, Pallas kernels for 0%

profile of v8, /device:TPU:8, one launch (start us, length us, event | category | flops | bytes accessed | tf_op | source)
XLA Modules:
  0.0 223.4 jit_solution(14227344772144781334)
XLA Ops:
  7.3 2.0 pad_maximum_fusion
  9.4 1.1 fusion.20
  10.5 0.8 fusion.22
  11.7 1.8 convolution_convert_fusion.1
  13.5 10.3 %all-to-all-start = ((bf16[32,16,1536]{2,1,0:T(8,128)(2,1)}), bf16[32,16,1536]{2,1,0:T(8,128)(2,1)S(1)}, u32[]{:S(2)}, u32[]{:S(2)}) async-start(bf16[32,16,1536]{2,1,0:T(8,128)(2,1)} %bitcast.3), calls=%async_computation | async-start | bytes 3145728 | tf_op jit(solution)/shard_map/all_to_all | solution.py:19
  23.8 12.3 %all-gather = bf16[4,1,2048]{2,1,0:T(2,128)(2,1)S(1)} all-gather(bf16[1,1,2048]{2,1,0:T(2,128)(2,1)S(1)} %bitcast.130), channel_id=1, replica_groups=mesh['dp'=16,'y'=8,'x'=4] {'x'}, dimensions={0}, use_global_device_ids=true | all-gather | bytes 20480 | tf_op jit(solution)/shard_map/all_gather | solution.py:118
  36.1 23.5 %all-gather.1 = bf16[16,4,512]{2,1,0:T(4,128)(2,1)S(1)} all-gather(bf16[1,4,512]{2,1,0:T(4,128)(2,1)S(1)} %bitcast.132), channel_id=1, replica_groups=mesh['dp'=16,'y'=8,'x'=4] {'dp'}, dimensions={0}, use_global_device_ids=true | all-gather | bytes 69632 | tf_op jit(solution)/shard_map/all_gather | solution.py:120
  60.0 1.0 convolution_convert_fusion.3
  61.0 1.2 all-to-all-done
  62.2 8.0 %all-to-all-start.1 = ((bf16[8,32,512]{2,1,0:T(8,128)(2,1)}), bf16[8,32,512]{2,1,0:T(8,128)(2,1)S(1)}, u32[]{:S(2)}, u32[]{:S(2)}) async-start(bf16[8,32,512]{2,1,0:T(8,128)(2,1)} %bitcast.4), calls=%async_computation.1 | async-start | bytes 524288 | tf_op jit(solution)/shard_map/all_to_all | solution.py:19
  70.2 10.9 %all-to-all-done.1 = bf16[8,32,512]{2,1,0:T(8,128)(2,1)S(1)} async-done(((bf16[8,32,512]{2,1,0:T(8,128)(2,1)}), bf16[8,32,512]{2,1,0:T(8,128)(2,1)S(1)}, u32[]{:S(2)}, u32[]{:S(2)}) %all-to-all-start.1) | async-done | bytes 262176 | tf_op jit(solution)/shard_map/all_to_all | solution.py:19
  81.1 0.9 convolution_convert_fusion.4
  81.9 3.3 %all-to-all-start.2 = ((bf16[4,32,512]{2,1,0:T(8,128)(2,1)}), bf16[4,32,512]{2,1,0:T(8,128)(2,1)S(1)}, u32[]{:S(2)}, u32[]{:S(2)}) async-start(bf16[4,32,512]{2,1,0:T(8,128)(2,1)} %bitcast.6), calls=%async_computation.2 | async-start | bytes 262144 | tf_op jit(solution)/shard_map/all_to_all | solution.py:19
  85.5 5.8 %all-to-all-done.2 = bf16[4,32,512]{2,1,0:T(8,128)(2,1)S(1)} async-done(((bf16[4,32,512]{2,1,0:T(8,128)(2,1)}), bf16[4,32,512]{2,1,0:T(8,128)(2,1)S(1)}, u32[]{:S(2)}, u32[]{:S(2)}) %all-to-all-start.2) | async-done | bytes 131104 | tf_op jit(solution)/shard_map/all_to_all | solution.py:19
  91.3 2.2 fusion.86
  93.6 0.3 reduce-precision_convert_fusion
  93.9 1.7 fusion.12
  96.1 0.7 copy.86
  96.8 5.0 %all-to-all-start.3 = ((bf16[32,16,128]{2,1,0:T(8,128)(2,1)}), bf16[32,16,128]{2,1,0:T(8,128)(2,1)S(1)}, u32[]{:S(2)}, u32[]{:S(2)}) async-start(bf16[32,16,128]{2,1,0:T(8,128)(2,1)} %copy.86), calls=%async_computation.3 | async-start | bytes 262144 | tf_op jit(solution)/shard_map/all_to_all | solution.py:19
  101.9 9.6 %all-to-all-done.3 = bf16[32,16,128]{2,1,0:T(8,128)(2,1)S(1)} async-done(((bf16[32,16,128]{2,1,0:T(8,128)(2,1)}), bf16[32,16,128]{2,1,0:T(8,128)(2,1)S(1)}, u32[]{:S(2)}, u32[]{:S(2)}) %all-to-all-start.3) | async-done | bytes 131104 | tf_op jit(solution)/shard_map/all_to_all | solution.py:19
  112.0 0.7 broadcast_in_dim.147
  112.7 4.7 %all-to-all-start.4 = ((bf16[32,24,128]{2,1,0:T(8,128)(2,1)}), bf16[32,24,128]{2,1,0:T(8,128)(2,1)S(1)}, u32[]{:S(2)}, u32[]{:S(2)}) async-start(bf16[32,24,128]{2,1,0:T(8,128)(2,1)} %broadcast_in_dim.147), calls=%async_computation.4 | async-start | bytes 393216 | tf_op jit(solution)/shard_map/all_to_all | solution.py:19
  117.4 4.3 %fusion.5 = f32[512,768]{1,0:T(8,128)} fusion(bf16[512,1536]{1,0:T(8,128)(2,1)S(1)} %bitcast.113, bf16[3,768,1536]{2,1,0:T(8,128)(2,1)} %all-gather.4.cloned.1.call-done), kind=kOutput, calls=%fused_computation.14 | convolution fusion | flops 1207959552 | bytes 5505024 | tf_op jit(solution)/shard_map/dot_general | solution.py:13
  121.7 7.2 %convolution_convert_fusion = bf16[512,1536]{1,0:T(8,128)(2,1)} fusion(bf16[3,768,1536]{2,1,0:T(8,128)(2,1)} %all-gather.4.cloned.1.call-done, f32[512,768]{1,0:T(8,128)} %fusion.5, bf16[512,1536]{1,0:T(8,128)(2,1)S(1)} %bitcast.114), kind=kOutput, calls=%fused_computation | convolution fusion | flops 2417885184 | bytes 9437184 | tf_op jit(solution)/shard_map/dot_general | solution.py:49
  129.0 10.0 %all-to-all-start.5 = ((bf16[32,16,1536]{2,1,0:T(8,128)(2,1)}), bf16[32,16,1536]{2,1,0:T(8,128)(2,1)S(1)}, u32[]{:S(2)}, u32[]{:S(2)}) async-start(bf16[32,16,1536]{2,1,0:T(8,128)(2,1)} %bitcast.115), calls=%async_computation.5 | async-start | bytes 3145728 | tf_op jit(solution)/shard_map/all_to_all | solution.py:19
  139.0 0.7 slice_reduce_fusion.1
  139.7 0.6 fusion.71
  140.4 0.7 copy.120
  141.2 20.2 %all_gather.15 = bf16[512,48]{1,0:T(8,128)(2,1)S(1)} all-gather(bf16[32,48]{1,0:T(8,128)(2,1)S(1)} %convolution_convert_fusion.7), channel_id=1, replica_groups=mesh['dp'=16,'y'=8,'x'=4] {'dp'}, dimensions={0}, use_global_device_ids=true | all-gather | bytes 52224 | tf_op jit(solution)/shard_map/all_gather | solution.py:185
  161.4 0.2 convolution_convert_fusion.6
  161.6 13.4 %all-to-all-done.5 = bf16[32,16,1536]{2,1,0:T(8,128)(2,1)S(1)} async-done(((bf16[32,16,1536]{2,1,0:T(8,128)(2,1)}), bf16[32,16,1536]{2,1,0:T(8,128)(2,1)S(1)}, u32[]{:S(2)}, u32[]{:S(2)}) %all-to-all-start.5) | async-done | bytes 1572896 | tf_op jit(solution)/shard_map/all_to_all | solution.py:19
  175.1 0.7 broadcast_in_dim.151
  175.7 6.5 %all-to-all-start.6 = ((bf16[32,12,128]{2,1,0:T(8,128)(2,1)}), bf16[32,12,128]{2,1,0:T(8,128)(2,1)S(1)}, u32[]{:S(2)}, u32[]{:S(2)}) async-start(bf16[32,12,128]{2,1,0:T(8,128)(2,1)} %broadcast_in_dim.151), calls=%async_computation.6 | async-start | bytes 262144 | tf_op jit(solution)/shard_map/all_to_all | solution.py:19
  182.2 0.4 convolution_bitcast_fusion.2
  182.7 0.4 fusion.2
  183.1 8.7 %all-to-all-done.6 = bf16[32,12,128]{2,1,0:T(8,128)(2,1)S(1)} async-done(((bf16[32,12,128]{2,1,0:T(8,128)(2,1)}), bf16[32,12,128]{2,1,0:T(8,128)(2,1)S(1)}, u32[]{:S(2)}, u32[]{:S(2)}) %all-to-all-start.6) | async-done | bytes 98336 | tf_op jit(solution)/shard_map/all_to_all | solution.py:19
  191.8 0.2 reshape.275
  192.0 0.3 copy.88
  192.5 0.3 fusion.23
  192.8 0.8 fusion.25
  193.6 2.4 %fusion.10 = f32[32,768]{1,0:T(8,128)S(1)} fusion(bf16[3,768,1536]{2,1,0:T(8,128)(2,1)} %all-gather.4.cloned.1.call-done, bf16[4,8,12,128]{3,2,1,0:T(8,128)(2,1)S(1)} %bitcast.125), kind=kOutput, calls=%fused_computation.23 | convolution fusion | flops 75522048 | bytes 2555904 | tf_op jit(solution)/shard_map/dot_general | solution.py:13
  196.1 3.9 %convolution_convert_fusion.2 = bf16[32,1536]{1,0:T(8,128)(2,1)S(1)} fusion(bf16[3,768,1536]{2,1,0:T(8,128)(2,1)} %all-gather.4.cloned.1.call-done, f32[32,768]{1,0:T(8,128)S(1)} %fusion.10, bf16[4,8,12,128]{3,2,1,0:T(8,128)(2,1)S(1)} %bitcast.126), kind=kOutput, calls=%fused_computation.12 | convolution fusion | flops 151093248 | bytes 5013504 | tf_op jit(solution)/shard_map/dot_general | solution.py:49
  200.0 0.8 reshape.270
  200.7 4.7 %all-to-all-start.7 = ((bf16[32,12,128]{2,1,0:T(8,128)(2,1)}), bf16[32,12,128]{2,1,0:T(8,128)(2,1)S(1)}, u32[]{:S(2)}, u32[]{:S(2)}) async-start(bf16[32,12,128]{2,1,0:T(8,128)(2,1)} %reshape.270), calls=%async_computation.7 | async-start | bytes 262144 | tf_op jit(solution)/shard_map/all_to_all | solution.py:19
  205.5 1.1 fusion.3
  206.6 0.3 reshape.273
  206.9 8.2 %all-to-all-done.7 = bf16[32,12,128]{2,1,0:T(8,128)(2,1)S(1)} async-done(((bf16[32,12,128]{2,1,0:T(8,128)(2,1)}), bf16[32,12,128]{2,1,0:T(8,128)(2,1)S(1)}, u32[]{:S(2)}, u32[]{:S(2)}) %all-to-all-start.7) | async-done | bytes 98336 | tf_op jit(solution)/shard_map/all_to_all | solution.py:19
  215.2 1.4 fusion.76
  (97 shorter events, 2.9 us)
Async XLA Ops:
  7.2 133.9 %copy-start = (bf16[1536,48]{0,1:T(8,128)(2,1)S(1)}, bf16[1536,48]{0,1:T(8,128)(2,1)}, u32[]{:S(2)}) copy-start(bf16[1536,48]{0,1:T(8,128)(2,1)} %param.24) | copy-start | bytes 442372
  7.2 3.3 %copy-start.1 = (bf16[63,1536]{1,0:T(8,128)(2,1)S(1)}, bf16[63,1536]{1,0:T(8,128)(2,1)}, u32[]{:S(2)}) copy-start(bf16[63,1536]{1,0:T(8,128)(2,1)} %param.25) | copy-start | bytes 580612
  7.2 4.1 %copy-start.7 = (s32[64,4]{0,1:T(4,128)S(1)}, s32[64,4]{0,1:T(4,128)}, u32[]{:S(2)}) copy-start(s32[64,4]{0,1:T(4,128)} %param.26) | copy-start | bytes 3076
  7.2 4.4 %copy-start.9 = (bf16[1,1536]{1,0:T(2,128)(2,1)S(1)}, bf16[1,1536]{1,0:T(2,128)(2,1)}, u32[]{:S(2)}) copy-start(bf16[1,1536]{1,0:T(2,128)(2,1)} %param.16) | copy-start | bytes 9220
  7.2 4.4 %copy-start.12 = (bf16[1,512]{1,0:T(2,128)(2,1)S(1)}, bf16[1,512]{1,0:T(2,128)(2,1)}, u32[]{:S(2)}) copy-start(bf16[1,512]{1,0:T(2,128)(2,1)} %param.17) | copy-start | bytes 3076
  7.2 110.2 %all-gather.4.cloned.1.call-start = ((), (), s32[]{:S(2)}) async-start(), calls=%async_computation.8 | async-start | bytes 7520256 | tf_op jit(solution)/shard_map/all_gather | solution.py:108
  11.3 171.3 %copy-start.4 = (pred[63,32]{0,1:T(8,128)(4,1)}, pred[63,32]{0,1:T(8,128)(4,1)S(1)}, u32[]{:S(2)}) copy-start(pred[63,32]{0,1:T(8,128)(4,1)S(1)} %slice_reduce_fusion) | copy-start | bytes 6052
  11.5 171.2 %copy-start.2 = (s32[63,32]{0,1:T(8,128)}, s32[63,32]{0,1:T(8,128)S(1)}, u32[]{:S(2)}) copy-start(s32[63,32]{0,1:T(8,128)S(1)} %convolution_convert_fusion.5) | copy-start | bytes 24196
  13.5 46.2 %copy-start.15 = (s32[512]{0:T(512)S(1)}, s32[512]{0:T(512)}, u32[]{:S(2)}) copy-start(s32[512]{0:T(512)} %param.19) | copy-start | bytes 6148
  13.5 48.7 %all-to-all-start = ((bf16[32,16,1536]{2,1,0:T(8,128)(2,1)}), bf16[32,16,1536]{2,1,0:T(8,128)(2,1)S(1)}, u32[]{:S(2)}, u32[]{:S(2)}) async-start(bf16[32,16,1536]{2,1,0:T(8,128)(2,1)} %bitcast.3), calls=%async_computation | async-start | bytes 3145728 | tf_op jit(solution)/shard_map/all_to_all | solution.py:19
  23.8 61.5 %copy-start.13 = (s32[32]{0:T(128)S(1)}, s32[32]{0:T(128)}, u32[]{:S(2)}) copy-start(s32[32]{0:T(128)} %param.20) | copy-start | bytes 388
  23.8 61.5 %copy-start.14 = (s32[32]{0:T(128)S(1)}, s32[32]{0:T(128)}, u32[]{:S(2)}) copy-start(s32[32]{0:T(128)} %param.21) | copy-start | bytes 388
  62.2 18.9 %all-to-all-start.1 = ((bf16[8,32,512]{2,1,0:T(8,128)(2,1)}), bf16[8,32,512]{2,1,0:T(8,128)(2,1)S(1)}, u32[]{:S(2)}, u32[]{:S(2)}) async-start(bf16[8,32,512]{2,1,0:T(8,128)(2,1)} %bitcast.4), calls=%async_computation.1 | async-start | bytes 524288 | tf_op jit(solution)/shard_map/all_to_all | solution.py:19
  81.9 9.3 %all-to-all-start.2 = ((bf16[4,32,512]{2,1,0:T(8,128)(2,1)}), bf16[4,32,512]{2,1,0:T(8,128)(2,1)S(1)}, u32[]{:S(2)}, u32[]{:S(2)}) async-start(bf16[4,32,512]{2,1,0:T(8,128)(2,1)} %bitcast.6), calls=%async_computation.2 | async-start | bytes 262144 | tf_op jit(solution)/shard_map/all_to_all | solution.py:19
  93.9 8.0 %copy-start.10 = (bf16[1,1536]{1,0:T(2,128)(2,1)S(1)}, bf16[1,1536]{1,0:T(2,128)(2,1)}, u32[]{:S(2)}) copy-start(bf16[1,1536]{1,0:T(2,128)(2,1)} %param.18) | copy-start | bytes 9220
  96.8 14.6 %all-to-all-start.3 = ((bf16[32,16,128]{2,1,0:T(8,128)(2,1)}), bf16[32,16,128]{2,1,0:T(8,128)(2,1)S(1)}, u32[]{:S(2)}, u32[]{:S(2)}) async-start(bf16[32,16,128]{2,1,0:T(8,128)(2,1)} %copy.86), calls=%async_computation.3 | async-start | bytes 262144 | tf_op jit(solution)/shard_map/all_to_all | solution.py:19
  112.7 16.3 %all-to-all-start.4 = ((bf16[32,24,128]{2,1,0:T(8,128)(2,1)}), bf16[32,24,128]{2,1,0:T(8,128)(2,1)S(1)}, u32[]{:S(2)}, u32[]{:S(2)}) async-start(bf16[32,24,128]{2,1,0:T(8,128)(2,1)} %broadcast_in_dim.147), calls=%async_computation.4 | async-start | bytes 393216 | tf_op jit(solution)/shard_map/all_to_all | solution.py:19
  129.0 10.0 %copy-start.8 = (f32[64,4]{0,1:T(4,128)S(1)}, f32[64,4]{0,1:T(4,128)}, u32[]{:S(2)}) copy-start(f32[64,4]{0,1:T(4,128)} %param.27) | copy-start | bytes 3076
  129.0 46.0 %all-to-all-start.5 = ((bf16[32,16,1536]{2,1,0:T(8,128)(2,1)}), bf16[32,16,1536]{2,1,0:T(8,128)(2,1)S(1)}, u32[]{:S(2)}, u32[]{:S(2)}) async-start(bf16[32,16,1536]{2,1,0:T(8,128)(2,1)} %bitcast.115), calls=%async_computation.5 | async-start | bytes 3145728 | tf_op jit(solution)/shard_map/all_to_all | solution.py:19
  175.7 16.0 %all-to-all-start.6 = ((bf16[32,12,128]{2,1,0:T(8,128)(2,1)}), bf16[32,12,128]{2,1,0:T(8,128)(2,1)S(1)}, u32[]{:S(2)}, u32[]{:S(2)}) async-start(bf16[32,12,128]{2,1,0:T(8,128)(2,1)} %broadcast_in_dim.151), calls=%async_computation.6 | async-start | bytes 262144 | tf_op jit(solution)/shard_map/all_to_all | solution.py:19
  196.0 9.4 %copy-start.3 = (s32[63,32]{0,1:T(8,128)S(1)}, s32[63,32]{0,1:T(8,128)}, u32[]{:S(2)}) copy-start(s32[63,32]{0,1:T(8,128)} %copy-done.2) | copy-start | bytes 24196
  196.1 9.4 %copy-start.5 = (pred[63,32]{0,1:T(8,128)(4,1)S(1)}, pred[63,32]{0,1:T(8,128)(4,1)}, u32[]{:S(2)}) copy-start(pred[63,32]{0,1:T(8,128)(4,1)} %copy-done.4) | copy-start | bytes 6052
  196.1 9.4 %copy-start.6 = (bf16[63,32]{0,1:T(8,128)(2,1)S(1)}, bf16[63,32]{0,1:T(8,128)(2,1)}, u32[]{:S(2)}) copy-start(bf16[63,32]{0,1:T(8,128)(2,1)} %get-tuple-element.29) | copy-start | bytes 12100
  200.7 14.3 %all-to-all-start.7 = ((bf16[32,12,128]{2,1,0:T(8,128)(2,1)}), bf16[32,12,128]{2,1,0:T(8,128)(2,1)S(1)}, u32[]{:S(2)}, u32[]{:S(2)}) async-start(bf16[32,12,128]{2,1,0:T(8,128)(2,1)} %reshape.270), calls=%async_computation.7 | async-start | bytes 262144 | tf_op jit(solution)/shard_map/all_to_all | solution.py:19
  205.4 9.6 %copy-start.11 = (f32[32]{0:T(128)S(1)}, f32[32]{0:T(128)}, u32[]{:S(2)}) copy-start(f32[32]{0:T(128)} %slice_reduce_fusion.1) | copy-start | bytes 388
Sparse Core Ops, SparseCore 0:
  10.2 58.0 all-gather.3

commit v9 on v8

--- a/solution.py
+++ b/solution.py
@@ -191,13 +191,14 @@
     proj_home = packed.reshape(tp_size, group_reqs, width // tp_size)
     proj_home = jnp.transpose(proj_home, (1, 0, 2)).reshape(group_reqs, width)
     hidden_all = (resid_rows.astype(F32) + proj_home.astype(F32)).astype(BF16)
-    hidden_f32 = lax.dynamic_slice_in_dim(hidden_all, tp_lane, 1).astype(F32)
+    own_row = lax.dynamic_slice_in_dim(hidden_all, tp_lane, 1)
 
     dec_out = expert_units(rms(hidden_all.astype(F32), moe_gain), units)
+    own_row, dec_out = lax.optimization_barrier((own_row, dec_out))
     dec_back = swap(dec_out.reshape(group_reqs, heads, head_size), TP).astype(F32)
     dec_weight = weight_of[pre_rows:].reshape(experts, 1, 1)
     dec_mixture = jnp.sum(dec_weight * dec_back, axis=0).reshape(1, width)
-    out_dec = (hidden_f32 + dec_mixture).astype(BF16)
+    out_dec = (own_row.astype(F32) + dec_mixture).astype(BF16)
 
     flat_back = returned.reshape(experts * capacity, width)
     high, middle, low = pieces_of(weight_of[:pre_rows])

time: 225 us -> 225 us (level)
  no operation moved by 1% of the time
where the time goes in v9:
time: 225 us; the launch traced here: 224 us
  waiting for transfers between devices  57.9 us (26%)
  blocking collectives  56 us (25%)
  starting transfers between devices  52.5 us (23%)
  matrix products  27.8 us (12%)
  between operations  14.6 us (6%)
  other arithmetic  8.49 us (4%)
  local copies, waits for them, and re-layouts  6.39 us (3%)
    all_to_all x8, waiting for transfers between devices, swap(): lax.all_to_all(blocks, axis_name, split_axis=0, concat_axis=0, tiled=True)  57.9 us
    all_to_all x8, starting transfers between devices, swap(): lax.all_to_all(blocks, axis_name, split_axis=0, concat_axis=0, tiled=True)  52.5 us
    all_gather x1, blocking collectives, on_device(): all_rows = lax.all_gather(line_share, 'dp', axis=0, tiled=True)  23.5 us
    all_gather x1, blocking collectives, on_device(): all_projected = lax.all_gather(projected, 'dp', axis=0, tiled=True)  20.2 us
    all_gather x1, blocking collectives, on_device(): line_fresh = lax.all_gather(fresh, 'x', axis=0, tiled=True)  12.3 us
    dot_general x2, matrix products, expert_units(): return jnp.dot(active, units[2], preferred_element_type=F32).astype(BF16)  11.1 us
    dot_general x2, matrix products, contract_rows(): lax.dot_general(left_rows, unit_rows, (((1,), (1,)), ((), ())), preferred...  6.68 us
  transfers between devices with their start and end apart: 9, of which 7 were waited for; matrix products, arithmetic and copies ran while one was open for 13% of the time, Pallas kernels for 0%

profile of v9, /device:TPU:8, one launch (start us, length us, event | category | flops | bytes accessed | tf_op | source)
XLA Modules:
  0.0 223.7 jit_solution(17548990016549502649)
XLA Ops:
  7.3 2.0 pad_maximum_fusion
  9.4 1.1 fusion.20
  10.5 0.8 fusion.22
  11.7 1.8 convolution_convert_fusion.1
  13.5 10.3 %all-to-all-start = ((bf16[32,16,1536]{2,1,0:T(8,128)(2,1)}), bf16[32,16,1536]{2,1,0:T(8,128)(2,1)S(1)}, u32[]{:S(2)}, u32[]{:S(2)}) async-start(bf16[32,16,1536]{2,1,0:T(8,128)(2,1)} %bitcast.3), calls=%async_computation | async-start | bytes 3145728 | tf_op jit(solution)/shard_map/all_to_all | solution.py:19
  23.8 12.3 %all-gather = bf16[4,1,2048]{2,1,0:T(2,128)(2,1)S(1)} all-gather(bf16[1,1,2048]{2,1,0:T(2,128)(2,1)S(1)} %bitcast.130), channel_id=1, replica_groups=mesh['dp'=16,'y'=8,'x'=4] {'x'}, dimensions={0}, use_global_device_ids=true | all-gather | bytes 20480 | tf_op jit(solution)/shard_map/all_gather | solution.py:118
  36.1 23.5 %all-gather.1 = bf16[16,4,512]{2,1,0:T(4,128)(2,1)S(1)} all-gather(bf16[1,4,512]{2,1,0:T(4,128)(2,1)S(1)} %bitcast.132), channel_id=1, replica_groups=mesh['dp'=16,'y'=8,'x'=4] {'dp'}, dimensions={0}, use_global_device_ids=true | all-gather | bytes 69632 | tf_op jit(solution)/shard_map/all_gather | solution.py:120
  60.0 1.0 convolution_convert_fusion.3
  61.0 1.1 all-to-all-done
  62.2 8.0 %all-to-all-start.1 = ((bf16[8,32,512]{2,1,0:T(8,128)(2,1)}), bf16[8,32,512]{2,1,0:T(8,128)(2,1)S(1)}, u32[]{:S(2)}, u32[]{:S(2)}) async-start(bf16[8,32,512]{2,1,0:T(8,128)(2,1)} %bitcast.4), calls=%async_computation.1 | async-start | bytes 524288 | tf_op jit(solution)/shard_map/all_to_all | solution.py:19
  70.1 10.9 %all-to-all-done.1 = bf16[8,32,512]{2,1,0:T(8,128)(2,1)S(1)} async-done(((bf16[8,32,512]{2,1,0:T(8,128)(2,1)}), bf16[8,32,512]{2,1,0:T(8,128)(2,1)S(1)}, u32[]{:S(2)}, u32[]{:S(2)}) %all-to-all-start.1) | async-done | bytes 262176 | tf_op jit(solution)/shard_map/all_to_all | solution.py:19
  81.1 0.9 convolution_convert_fusion.4
  81.9 3.3 %all-to-all-start.2 = ((bf16[4,32,512]{2,1,0:T(8,128)(2,1)}), bf16[4,32,512]{2,1,0:T(8,128)(2,1)S(1)}, u32[]{:S(2)}, u32[]{:S(2)}) async-start(bf16[4,32,512]{2,1,0:T(8,128)(2,1)} %bitcast.6), calls=%async_computation.2 | async-start | bytes 262144 | tf_op jit(solution)/shard_map/all_to_all | solution.py:19
  85.5 5.8 %all-to-all-done.2 = bf16[4,32,512]{2,1,0:T(8,128)(2,1)S(1)} async-done(((bf16[4,32,512]{2,1,0:T(8,128)(2,1)}), bf16[4,32,512]{2,1,0:T(8,128)(2,1)S(1)}, u32[]{:S(2)}, u32[]{:S(2)}) %all-to-all-start.2) | async-done | bytes 131104 | tf_op jit(solution)/shard_map/all_to_all | solution.py:19
  91.3 2.2 fusion.85
  93.6 0.3 reduce-precision_convert_fusion
  93.9 1.7 fusion.12
  96.1 0.7 copy.86
  96.8 5.0 %all-to-all-start.3 = ((bf16[32,16,128]{2,1,0:T(8,128)(2,1)}), bf16[32,16,128]{2,1,0:T(8,128)(2,1)S(1)}, u32[]{:S(2)}, u32[]{:S(2)}) async-start(bf16[32,16,128]{2,1,0:T(8,128)(2,1)} %copy.86), calls=%async_computation.3 | async-start | bytes 262144 | tf_op jit(solution)/shard_map/all_to_all | solution.py:19
  101.9 9.6 %all-to-all-done.3 = bf16[32,16,128]{2,1,0:T(8,128)(2,1)S(1)} async-done(((bf16[32,16,128]{2,1,0:T(8,128)(2,1)}), bf16[32,16,128]{2,1,0:T(8,128)(2,1)S(1)}, u32[]{:S(2)}, u32[]{:S(2)}) %all-to-all-start.3) | async-done | bytes 131104 | tf_op jit(solution)/shard_map/all_to_all | solution.py:19
  112.0 0.7 broadcast_in_dim.147
  112.7 4.7 %all-to-all-start.4 = ((bf16[32,24,128]{2,1,0:T(8,128)(2,1)}), bf16[32,24,128]{2,1,0:T(8,128)(2,1)S(1)}, u32[]{:S(2)}, u32[]{:S(2)}) async-start(bf16[32,24,128]{2,1,0:T(8,128)(2,1)} %broadcast_in_dim.147), calls=%async_computation.4 | async-start | bytes 393216 | tf_op jit(solution)/shard_map/all_to_all | solution.py:19
  117.4 4.3 %fusion.5 = f32[512,768]{1,0:T(8,128)} fusion(bf16[512,1536]{1,0:T(8,128)(2,1)S(1)} %bitcast.113, bf16[3,768,1536]{2,1,0:T(8,128)(2,1)} %all-gather.4.cloned.1.call-done), kind=kOutput, calls=%fused_computation.14 | convolution fusion | flops 1207959552 | bytes 5505024 | tf_op jit(solution)/shard_map/dot_general | solution.py:13
  121.7 7.2 %convolution_convert_fusion = bf16[512,1536]{1,0:T(8,128)(2,1)} fusion(bf16[3,768,1536]{2,1,0:T(8,128)(2,1)} %all-gather.4.cloned.1.call-done, f32[512,768]{1,0:T(8,128)} %fusion.5, bf16[512,1536]{1,0:T(8,128)(2,1)S(1)} %bitcast.114), kind=kOutput, calls=%fused_computation | convolution fusion | flops 2417885184 | bytes 9437184 | tf_op jit(solution)/shard_map/dot_general | solution.py:49
  129.0 10.0 %all-to-all-start.5 = ((bf16[32,16,1536]{2,1,0:T(8,128)(2,1)}), bf16[32,16,1536]{2,1,0:T(8,128)(2,1)S(1)}, u32[]{:S(2)}, u32[]{:S(2)}) async-start(bf16[32,16,1536]{2,1,0:T(8,128)(2,1)} %bitcast.115), calls=%async_computation.5 | async-start | bytes 3145728 | tf_op jit(solution)/shard_map/all_to_all | solution.py:19
  139.0 0.7 slice_reduce_fusion.1
  139.7 0.6 fusion.71
  140.4 0.7 copy.120
  141.3 20.2 %all_gather.15 = bf16[512,48]{1,0:T(8,128)(2,1)S(1)} all-gather(bf16[32,48]{1,0:T(8,128)(2,1)S(1)} %convolution_convert_fusion.7), channel_id=1, replica_groups=mesh['dp'=16,'y'=8,'x'=4] {'dp'}, dimensions={0}, use_global_device_ids=true | all-gather | bytes 52224 | tf_op jit(solution)/shard_map/all_gather | solution.py:185
  161.6 13.4 %all-to-all-done.5 = bf16[32,16,1536]{2,1,0:T(8,128)(2,1)S(1)} async-done(((bf16[32,16,1536]{2,1,0:T(8,128)(2,1)}), bf16[32,16,1536]{2,1,0:T(8,128)(2,1)S(1)}, u32[]{:S(2)}, u32[]{:S(2)}) %all-to-all-start.5) | async-done | bytes 1572896 | tf_op jit(solution)/shard_map/all_to_all | solution.py:19
  175.1 0.7 broadcast_in_dim.151
  175.7 6.5 %all-to-all-start.6 = ((bf16[32,12,128]{2,1,0:T(8,128)(2,1)}), bf16[32,12,128]{2,1,0:T(8,128)(2,1)S(1)}, u32[]{:S(2)}, u32[]{:S(2)}) async-start(bf16[32,12,128]{2,1,0:T(8,128)(2,1)} %broadcast_in_dim.151), calls=%async_computation.6 | async-start | bytes 262144 | tf_op jit(solution)/shard_map/all_to_all | solution.py:19
  182.2 0.4 convolution_bitcast_fusion.2
  182.7 0.4 fusion.2
  183.1 8.7 %all-to-all-done.6 = bf16[32,12,128]{2,1,0:T(8,128)(2,1)S(1)} async-done(((bf16[32,12,128]{2,1,0:T(8,128)(2,1)}), bf16[32,12,128]{2,1,0:T(8,128)(2,1)S(1)}, u32[]{:S(2)}, u32[]{:S(2)}) %all-to-all-start.6) | async-done | bytes 98336 | tf_op jit(solution)/shard_map/all_to_all | solution.py:19
  191.8 0.2 reshape.275
  192.0 0.3 copy.88
  192.5 0.3 reshape.273
  192.7 0.3 fusion.23
  193.1 0.8 fusion.25
  193.9 0.8 fusion.77
  194.7 2.4 %fusion.10 = f32[32,768]{1,0:T(8,128)S(1)} fusion(bf16[3,768,1536]{2,1,0:T(8,128)(2,1)} %all-gather.4.cloned.1.call-done, bf16[4,8,12,128]{3,2,1,0:T(8,128)(2,1)S(1)} %bitcast.125), kind=kOutput, calls=%fused_computation.23 | convolution fusion | flops 75522048 | bytes 2555904 | tf_op jit(solution)/shard_map/dot_general | solution.py:13
  197.2 3.9 %convolution_convert_fusion.2 = bf16[32,1536]{1,0:T(8,128)(2,1)S(1)} fusion(bf16[3,768,1536]{2,1,0:T(8,128)(2,1)} %all-gather.4.cloned.1.call-done, f32[32,768]{1,0:T(8,128)S(1)} %fusion.10, bf16[4,8,12,128]{3,2,1,0:T(8,128)(2,1)S(1)} %bitcast.126), kind=kOutput, calls=%fused_computation.12 | convolution fusion | flops 151093248 | bytes 5013504 | tf_op jit(solution)/shard_map/dot_general | solution.py:49
  201.1 0.7 reshape.270
  201.8 4.7 %all-to-all-start.7 = ((bf16[32,12,128]{2,1,0:T(8,128)(2,1)}), bf16[32,12,128]{2,1,0:T(8,128)(2,1)S(1)}, u32[]{:S(2)}, u32[]{:S(2)}) async-start(bf16[32,12,128]{2,1,0:T(8,128)(2,1)} %reshape.270), calls=%async_computation.7 | async-start | bytes 262144 | tf_op jit(solution)/shard_map/all_to_all | solution.py:19
  206.6 1.1 fusion.3
  207.7 8.5 %all-to-all-done.7 = bf16[32,12,128]{2,1,0:T(8,128)(2,1)S(1)} async-done(((bf16[32,12,128]{2,1,0:T(8,128)(2,1)}), bf16[32,12,128]{2,1,0:T(8,128)(2,1)S(1)}, u32[]{:S(2)}, u32[]{:S(2)}) %all-to-all-start.7) | async-done | bytes 98336 | tf_op jit(solution)/shard_map/all_to_all | solution.py:19
  216.3 0.6 fusion.76
  (98 shorter events, 3.1 us)
Async XLA Ops:
  7.2 133.9 %copy-start = (bf16[1536,48]{0,1:T(8,128)(2,1)S(1)}, bf16[1536,48]{0,1:T(8,128)(2,1)}, u32[]{:S(2)}) copy-start(bf16[1536,48]{0,1:T(8,128)(2,1)} %param.24) | copy-start | bytes 442372
  7.2 3.3 %copy-start.1 = (bf16[63,1536]{1,0:T(8,128)(2,1)S(1)}, bf16[63,1536]{1,0:T(8,128)(2,1)}, u32[]{:S(2)}) copy-start(bf16[63,1536]{1,0:T(8,128)(2,1)} %param.25) | copy-start | bytes 580612
  7.2 4.1 %copy-start.7 = (s32[64,4]{0,1:T(4,128)S(1)}, s32[64,4]{0,1:T(4,128)}, u32[]{:S(2)}) copy-start(s32[64,4]{0,1:T(4,128)} %param.26) | copy-start | bytes 3076
  7.2 4.4 %copy-start.9 = (bf16[1,1536]{1,0:T(2,128)(2,1)S(1)}, bf16[1,1536]{1,0:T(2,128)(2,1)}, u32[]{:S(2)}) copy-start(bf16[1,1536]{1,0:T(2,128)(2,1)} %param.16) | copy-start | bytes 9220
  7.2 4.4 %copy-start.12 = (bf16[1,512]{1,0:T(2,128)(2,1)S(1)}, bf16[1,512]{1,0:T(2,128)(2,1)}, u32[]{:S(2)}) copy-start(bf16[1,512]{1,0:T(2,128)(2,1)} %param.17) | copy-start | bytes 3076
  7.2 110.2 %all-gather.4.cloned.1.call-start = ((), (), s32[]{:S(2)}) async-start(), calls=%async_computation.8 | async-start | bytes 7520256 | tf_op jit(solution)/shard_map/all_gather | solution.py:108
  11.3 171.3 %copy-start.4 = (pred[63,32]{0,1:T(8,128)(4,1)}, pred[63,32]{0,1:T(8,128)(4,1)S(1)}, u32[]{:S(2)}) copy-start(pred[63,32]{0,1:T(8,128)(4,1)S(1)} %slice_reduce_fusion) | copy-start | bytes 6052
  11.5 171.2 %copy-start.2 = (s32[63,32]{0,1:T(8,128)}, s32[63,32]{0,1:T(8,128)S(1)}, u32[]{:S(2)}) copy-start(s32[63,32]{0,1:T(8,128)S(1)} %convolution_convert_fusion.5) | copy-start | bytes 24196
  13.5 46.2 %copy-start.15 = (s32[512]{0:T(512)S(1)}, s32[512]{0:T(512)}, u32[]{:S(2)}) copy-start(s32[512]{0:T(512)} %param.19) | copy-start | bytes 6148
  13.5 48.7 %all-to-all-start = ((bf16[32,16,1536]{2,1,0:T(8,128)(2,1)}), bf16[32,16,1536]{2,1,0:T(8,128)(2,1)S(1)}, u32[]{:S(2)}, u32[]{:S(2)}) async-start(bf16[32,16,1536]{2,1,0:T(8,128)(2,1)} %bitcast.3), calls=%async_computation | async-start | bytes 3145728 | tf_op jit(solution)/shard_map/all_to_all | solution.py:19
  23.8 61.5 %copy-start.13 = (s32[32]{0:T(128)S(1)}, s32[32]{0:T(128)}, u32[]{:S(2)}) copy-start(s32[32]{0:T(128)} %param.20) | copy-start | bytes 388
  23.8 61.5 %copy-start.14 = (s32[32]{0:T(128)S(1)}, s32[32]{0:T(128)}, u32[]{:S(2)}) copy-start(s32[32]{0:T(128)} %param.21) | copy-start | bytes 388
  62.2 18.9 %all-to-all-start.1 = ((bf16[8,32,512]{2,1,0:T(8,128)(2,1)}), bf16[8,32,512]{2,1,0:T(8,128)(2,1)S(1)}, u32[]{:S(2)}, u32[]{:S(2)}) async-start(bf16[8,32,512]{2,1,0:T(8,128)(2,1)} %bitcast.4), calls=%async_computation.1 | async-start | bytes 524288 | tf_op jit(solution)/shard_map/all_to_all | solution.py:19
  81.9 9.3 %all-to-all-start.2 = ((bf16[4,32,512]{2,1,0:T(8,128)(2,1)}), bf16[4,32,512]{2,1,0:T(8,128)(2,1)S(1)}, u32[]{:S(2)}, u32[]{:S(2)}) async-start(bf16[4,32,512]{2,1,0:T(8,128)(2,1)} %bitcast.6), calls=%async_computation.2 | async-start | bytes 262144 | tf_op jit(solution)/shard_map/all_to_all | solution.py:19
  93.8 8.0 %copy-start.10 = (bf16[1,1536]{1,0:T(2,128)(2,1)S(1)}, bf16[1,1536]{1,0:T(2,128)(2,1)}, u32[]{:S(2)}) copy-start(bf16[1,1536]{1,0:T(2,128)(2,1)} %param.18) | copy-start | bytes 9220
  96.8 14.6 %all-to-all-start.3 = ((bf16[32,16,128]{2,1,0:T(8,128)(2,1)}), bf16[32,16,128]{2,1,0:T(8,128)(2,1)S(1)}, u32[]{:S(2)}, u32[]{:S(2)}) async-start(bf16[32,16,128]{2,1,0:T(8,128)(2,1)} %copy.86), calls=%async_computation.3 | async-start | bytes 262144 | tf_op jit(solution)/shard_map/all_to_all | solution.py:19
  112.7 16.3 %all-to-all-start.4 = ((bf16[32,24,128]{2,1,0:T(8,128)(2,1)}), bf16[32,24,128]{2,1,0:T(8,128)(2,1)S(1)}, u32[]{:S(2)}, u32[]{:S(2)}) async-start(bf16[32,24,128]{2,1,0:T(8,128)(2,1)} %broadcast_in_dim.147), calls=%async_computation.4 | async-start | bytes 393216 | tf_op jit(solution)/shard_map/all_to_all | solution.py:19
  128.9 10.0 %copy-start.8 = (f32[64,4]{0,1:T(4,128)S(1)}, f32[64,4]{0,1:T(4,128)}, u32[]{:S(2)}) copy-start(f32[64,4]{0,1:T(4,128)} %param.27) | copy-start | bytes 3076
  129.0 46.0 %all-to-all-start.5 = ((bf16[32,16,1536]{2,1,0:T(8,128)(2,1)}), bf16[32,16,1536]{2,1,0:T(8,128)(2,1)S(1)}, u32[]{:S(2)}, u32[]{:S(2)}) async-start(bf16[32,16,1536]{2,1,0:T(8,128)(2,1)} %bitcast.115), calls=%async_computation.5 | async-start | bytes 3145728 | tf_op jit(solution)/shard_map/all_to_all | solution.py:19
  175.7 16.0 %all-to-all-start.6 = ((bf16[32,12,128]{2,1,0:T(8,128)(2,1)}), bf16[32,12,128]{2,1,0:T(8,128)(2,1)S(1)}, u32[]{:S(2)}, u32[]{:S(2)}) async-start(bf16[32,12,128]{2,1,0:T(8,128)(2,1)} %broadcast_in_dim.151), calls=%async_computation.6 | async-start | bytes 262144 | tf_op jit(solution)/shard_map/all_to_all | solution.py:19
  197.1 9.4 %copy-start.3 = (s32[63,32]{0,1:T(8,128)S(1)}, s32[63,32]{0,1:T(8,128)}, u32[]{:S(2)}) copy-start(s32[63,32]{0,1:T(8,128)} %copy-done.2) | copy-start | bytes 24196
  197.2 9.4 %copy-start.5 = (pred[63,32]{0,1:T(8,128)(4,1)S(1)}, pred[63,32]{0,1:T(8,128)(4,1)}, u32[]{:S(2)}) copy-start(pred[63,32]{0,1:T(8,128)(4,1)} %copy-done.4) | copy-start | bytes 6052
  197.2 9.4 %copy-start.6 = (bf16[63,32]{0,1:T(8,128)(2,1)S(1)}, bf16[63,32]{0,1:T(8,128)(2,1)}, u32[]{:S(2)}) copy-start(bf16[63,32]{0,1:T(8,128)(2,1)} %get-tuple-element.33) | copy-start | bytes 12100
  201.1 15.1 %copy-start.11 = (f32[32]{0:T(128)S(1)}, f32[32]{0:T(128)}, u32[]{:S(2)}) copy-start(f32[32]{0:T(128)} %slice_reduce_fusion.1) | copy-start | bytes 388
  201.8 14.3 %all-to-all-start.7 = ((bf16[32,12,128]{2,1,0:T(8,128)(2,1)}), bf16[32,12,128]{2,1,0:T(8,128)(2,1)S(1)}, u32[]{:S(2)}, u32[]{:S(2)}) async-start(bf16[32,12,128]{2,1,0:T(8,128)(2,1)} %reshape.270), calls=%async_computation.7 | async-start | bytes 262144 | tf_op jit(solution)/shard_map/all_to_all | solution.py:19
Sparse Core Ops, SparseCore 0:
  10.2 58.0 all-gather.3

commit v10 on v9

--- a/solution.py
+++ b/solution.py
@@ -42,8 +42,7 @@
     return choose_rows(same, parts.reshape(count * rows, columns)).reshape(copies, rows, columns)
 
 
-def expert_units(rows, units):
-    gate = contract_rows(rows, units[0])
+def expert_units(rows, units, gate):
     upper = contract_rows(rows, units[1])
     active = (jnp.maximum(gate, 0.0) * upper).astype(BF16)
     return jnp.dot(active, units[2], preferred_element_type=F32).astype(BF16)
@@ -105,9 +104,8 @@
         preferred_element_type=F32,
     ).astype(BF16)
 
-    units = lax.all_gather(
-        jnp.concatenate([w_gate, w_up, w_down], axis=0), "dp", axis=1, tiled=True
-    )
+    stored, outgoing = lax.optimization_barrier(((w_gate, w_up, w_down), outgoing))
+    units = lax.all_gather(jnp.concatenate(stored, axis=0), "dp", axis=1, tiled=True)
 
     columns = heads + 2 * kv_heads
     share = columns * head_size // posts
@@ -163,6 +161,8 @@
         axis=1,
     )
     gathered = swap(parts, TP)
+    arrived = received.reshape(experts * capacity, width)
+    gathered, gate = lax.optimization_barrier((gathered, contract_rows(arrived, units[0])))
 
     tail = gathered[:, heads : heads + 2, : 3 * heads].astype(F32)
     tail = tail[..., :heads] + tail[..., heads : 2 * heads] + tail[..., 2 * heads :]
@@ -175,7 +175,7 @@
     rows = jnp.concatenate([attention_row, resid_dec.reshape(heads, head_size)], axis=0)
     group_rows = swap(jnp.broadcast_to(rows[None], (tp_size,) + rows.shape), TP)
 
-    pre_out = expert_units(received.reshape(experts * capacity, width), units)
+    pre_out = expert_units(arrived, units, gate)
     group_rows, pre_out = lax.optimization_barrier((group_rows, pre_out))
     returned = swap(pre_out.reshape(experts, capacity, width), TP)
 
@@ -193,7 +193,8 @@
     hidden_all = (resid_rows.astype(F32) + proj_home.astype(F32)).astype(BF16)
     own_row = lax.dynamic_slice_in_dim(hidden_all, tp_lane, 1)
 
-    dec_out = expert_units(rms(hidden_all.astype(F32), moe_gain), units)
+    normed_dec = rms(hidden_all.astype(F32), moe_gain)
+    dec_out = expert_units(normed_dec, units, contract_rows(normed_dec, units[0]))
     own_row, dec_out = lax.optimization_barrier((own_row, dec_out))
     dec_back = swap(dec_out.reshape(group_reqs, heads, head_size), TP).astype(F32)
     dec_weight = weight_of[pre_rows:].reshape(experts, 1, 1)

time: 225 us -> 220 us (0.978)
  starting transfers between devices: 52.5 us -> 49.4 us
    all_to_all x8, starting transfers between devices: 52.5 us -> 49.3 us  [swap(): lax.all_to_all(blocks, axis_name, split_axis=0, concat_axis=0, tiled=True)]
  transfers between devices with their start and end apart: 9 -> 9, of which waited for: 7 -> 8; matrix products, arithmetic and copies ran while one was open for 13% -> 10% of each run, Pallas kernels for 0% -> 0%
where the time goes in v10:
time: 220 us; the launch traced here: 219 us
  waiting for transfers between devices  58.1 us (26%)
  blocking collectives  55.9 us (25%)
  starting transfers between devices  49.4 us (22%)
  matrix products  27.8 us (13%)
  between operations  14.6 us (7%)
  other arithmetic  7.09 us (3%)
  local copies, waits for them, and re-layouts  5.88 us (3%)
    all_to_all x8, waiting for transfers between devices, swap(): lax.all_to_all(blocks, axis_name, split_axis=0, concat_axis=0, tiled=True)  58.1 us
    all_to_all x8, starting transfers between devices, swap(): lax.all_to_all(blocks, axis_name, split_axis=0, concat_axis=0, tiled=True)  49.3 us
    all_gather x1, blocking collectives, on_device(): all_rows = lax.all_gather(line_share, 'dp', axis=0, tiled=True)  23.4 us
    all_gather x1, blocking collectives, on_device(): all_projected = lax.all_gather(projected, 'dp', axis=0, tiled=True)  20.1 us
    all_gather x1, blocking collectives, on_device(): line_fresh = lax.all_gather(fresh, 'x', axis=0, tiled=True)  12.4 us
    dot_general x2, matrix products, expert_units(): return jnp.dot(active, units[2], preferred_element_type=F32).astype(BF16)  11.2 us
    dot_general x2, matrix products, contract_rows(): lax.dot_general(left_rows, unit_rows, (((1,), (1,)), ((), ())), preferred...  6.7 us
  transfers between devices with their start and end apart: 9, of which 8 were waited for; matrix products, arithmetic and copies ran while one was open for 10% of the time, Pallas kernels for 0%

profile of v10, /device:TPU:8, one launch (start us, length us, event | category | flops | bytes accessed | tf_op | source)
XLA Modules:
  0.0 218.8 jit_solution(2742729060871628576)
XLA Ops:
  7.3 0.8 iota_compare_fusion.1
  8.3 1.1 fusion.20
  9.4 1.1 fusion.22
  10.6 1.8 convolution_convert_fusion.1
  12.4 0.8 pad_maximum_fusion
  13.3 10.2 %all-to-all-start = ((bf16[32,16,1536]{2,1,0:T(8,128)(2,1)}), bf16[32,16,1536]{2,1,0:T(8,128)(2,1)S(1)}, u32[]{:S(2)}, u32[]{:S(2)}) async-start(bf16[32,16,1536]{2,1,0:T(8,128)(2,1)} %bitcast.3), calls=%async_computation | async-start | bytes 3145728 | tf_op jit(solution)/shard_map/all_to_all | solution.py:19
  23.6 12.4 %all-gather = bf16[4,1,2048]{2,1,0:T(2,128)(2,1)S(1)} all-gather(bf16[1,1,2048]{2,1,0:T(2,128)(2,1)S(1)} %bitcast.130), channel_id=1, replica_groups=mesh['dp'=16,'y'=8,'x'=4] {'x'}, dimensions={0}, use_global_device_ids=true | all-gather | bytes 20480 | tf_op jit(solution)/shard_map/all_gather | solution.py:116
  35.9 23.4 %all-gather.1 = bf16[16,4,512]{2,1,0:T(4,128)(2,1)S(1)} all-gather(bf16[1,4,512]{2,1,0:T(4,128)(2,1)S(1)} %bitcast.132), channel_id=1, replica_groups=mesh['dp'=16,'y'=8,'x'=4] {'dp'}, dimensions={0}, use_global_device_ids=true | all-gather | bytes 69632 | tf_op jit(solution)/shard_map/all_gather | solution.py:118
  59.7 1.0 convolution_convert_fusion.3
  60.7 1.2 all-to-all-done
  61.9 8.0 %all-to-all-start.1 = ((bf16[8,32,512]{2,1,0:T(8,128)(2,1)}), bf16[8,32,512]{2,1,0:T(8,128)(2,1)S(1)}, u32[]{:S(2)}, u32[]{:S(2)}) async-start(bf16[8,32,512]{2,1,0:T(8,128)(2,1)} %bitcast.4), calls=%async_computation.1 | async-start | bytes 524288 | tf_op jit(solution)/shard_map/all_to_all | solution.py:19
  69.9 10.9 %all-to-all-done.1 = bf16[8,32,512]{2,1,0:T(8,128)(2,1)S(1)} async-done(((bf16[8,32,512]{2,1,0:T(8,128)(2,1)}), bf16[8,32,512]{2,1,0:T(8,128)(2,1)S(1)}, u32[]{:S(2)}, u32[]{:S(2)}) %all-to-all-start.1) | async-done | bytes 262176 | tf_op jit(solution)/shard_map/all_to_all | solution.py:19
  80.8 0.9 convolution_convert_fusion.4
  81.7 3.3 %all-to-all-start.2 = ((bf16[4,32,512]{2,1,0:T(8,128)(2,1)}), bf16[4,32,512]{2,1,0:T(8,128)(2,1)S(1)}, u32[]{:S(2)}, u32[]{:S(2)}) async-start(bf16[4,32,512]{2,1,0:T(8,128)(2,1)} %bitcast.6), calls=%async_computation.2 | async-start | bytes 262144 | tf_op jit(solution)/shard_map/all_to_all | solution.py:19
  85.3 5.7 %all-to-all-done.2 = bf16[4,32,512]{2,1,0:T(8,128)(2,1)S(1)} async-done(((bf16[4,32,512]{2,1,0:T(8,128)(2,1)}), bf16[4,32,512]{2,1,0:T(8,128)(2,1)S(1)}, u32[]{:S(2)}, u32[]{:S(2)}) %all-to-all-start.2) | async-done | bytes 131104 | tf_op jit(solution)/shard_map/all_to_all | solution.py:19
  91.1 2.2 fusion.85
  93.3 0.3 reduce-precision_convert_fusion
  93.6 1.7 fusion.12
  95.9 0.7 copy.86
  96.6 5.0 %all-to-all-start.3 = ((bf16[32,16,128]{2,1,0:T(8,128)(2,1)}), bf16[32,16,128]{2,1,0:T(8,128)(2,1)S(1)}, u32[]{:S(2)}, u32[]{:S(2)}) async-start(bf16[32,16,128]{2,1,0:T(8,128)(2,1)} %copy.86), calls=%async_computation.3 | async-start | bytes 262144 | tf_op jit(solution)/shard_map/all_to_all | solution.py:19
  101.6 4.3 %fusion.5 = f32[512,768]{1,0:T(8,128)} fusion(bf16[512,1536]{1,0:T(8,128)(2,1)S(1)} %bitcast.113, bf16[3,768,1536]{2,1,0:T(8,128)(2,1)} %all-gather.4.cloned.1.call-done), kind=kOutput, calls=%fused_computation.14 | convolution fusion | flops 1207959552 | bytes 5505024 | tf_op jit(solution)/shard_map/dot_general | solution.py:13
  105.9 5.3 %all-to-all-done.3 = bf16[32,16,128]{2,1,0:T(8,128)(2,1)S(1)} async-done(((bf16[32,16,128]{2,1,0:T(8,128)(2,1)}), bf16[32,16,128]{2,1,0:T(8,128)(2,1)S(1)}, u32[]{:S(2)}, u32[]{:S(2)}) %all-to-all-start.3) | async-done | bytes 131104 | tf_op jit(solution)/shard_map/all_to_all | solution.py:19
  111.7 0.7 broadcast_in_dim.147
  112.4 4.7 %all-to-all-start.4 = ((bf16[32,24,128]{2,1,0:T(8,128)(2,1)}), bf16[32,24,128]{2,1,0:T(8,128)(2,1)S(1)}, u32[]{:S(2)}, u32[]{:S(2)}) async-start(bf16[32,24,128]{2,1,0:T(8,128)(2,1)} %broadcast_in_dim.147), calls=%async_computation.4 | async-start | bytes 393216 | tf_op jit(solution)/shard_map/all_to_all | solution.py:19
  117.2 7.2 %convolution_convert_fusion = bf16[512,1536]{1,0:T(8,128)(2,1)} fusion(bf16[3,768,1536]{2,1,0:T(8,128)(2,1)} %all-gather.4.cloned.1.call-done, f32[512,768]{1,0:T(8,128)} %fusion.5, bf16[512,1536]{1,0:T(8,128)(2,1)S(1)} %bitcast.114), kind=kOutput, calls=%fused_computation | convolution fusion | flops 2417885184 | bytes 9437184 | tf_op jit(solution)/shard_map/dot_general | solution.py:48
  124.4 3.0 %all-to-all-done.4 = bf16[32,24,128]{2,1,0:T(8,128)(2,1)S(1)} async-done(((bf16[32,24,128]{2,1,0:T(8,128)(2,1)}), bf16[32,24,128]{2,1,0:T(8,128)(2,1)S(1)}, u32[]{:S(2)}, u32[]{:S(2)}) %all-to-all-start.4) | async-done | bytes 196640 | tf_op jit(solution)/shard_map/all_to_all | solution.py:19
  127.4 7.0 %all-to-all-start.5 = ((bf16[32,16,1536]{2,1,0:T(8,128)(2,1)}), bf16[32,16,1536]{2,1,0:T(8,128)(2,1)S(1)}, u32[]{:S(2)}, u32[]{:S(2)}) async-start(bf16[32,16,1536]{2,1,0:T(8,128)(2,1)} %bitcast.115), calls=%async_computation.5 | async-start | bytes 3145728 | tf_op jit(solution)/shard_map/all_to_all | solution.py:19
  134.7 0.7 copy.120
  135.6 20.1 %all_gather.15 = bf16[512,48]{1,0:T(8,128)(2,1)S(1)} all-gather(bf16[32,48]{1,0:T(8,128)(2,1)S(1)} %convolution_convert_fusion.7), channel_id=1, replica_groups=mesh['dp'=16,'y'=8,'x'=4] {'dp'}, dimensions={0}, use_global_device_ids=true | all-gather | bytes 52224 | tf_op jit(solution)/shard_map/all_gather | solution.py:185
  155.8 0.2 convolution_convert_fusion.6
  156.0 14.7 %all-to-all-done.5 = bf16[32,16,1536]{2,1,0:T(8,128)(2,1)S(1)} async-done(((bf16[32,16,1536]{2,1,0:T(8,128)(2,1)}), bf16[32,16,1536]{2,1,0:T(8,128)(2,1)S(1)}, u32[]{:S(2)}, u32[]{:S(2)}) %all-to-all-start.5) | async-done | bytes 1572896 | tf_op jit(solution)/shard_map/all_to_all | solution.py:19
  170.8 0.7 broadcast_in_dim.151
  171.5 6.5 %all-to-all-start.6 = ((bf16[32,12,128]{2,1,0:T(8,128)(2,1)}), bf16[32,12,128]{2,1,0:T(8,128)(2,1)S(1)}, u32[]{:S(2)}, u32[]{:S(2)}) async-start(bf16[32,12,128]{2,1,0:T(8,128)(2,1)} %broadcast_in_dim.151), calls=%async_computation.6 | async-start | bytes 262144 | tf_op jit(solution)/shard_map/all_to_all | solution.py:19
  177.9 0.4 convolution_bitcast_fusion.2
  178.4 0.4 fusion.2
  178.8 8.7 %all-to-all-done.6 = bf16[32,12,128]{2,1,0:T(8,128)(2,1)S(1)} async-done(((bf16[32,12,128]{2,1,0:T(8,128)(2,1)}), bf16[32,12,128]{2,1,0:T(8,128)(2,1)S(1)}, u32[]{:S(2)}, u32[]{:S(2)}) %all-to-all-start.6) | async-done | bytes 98336 | tf_op jit(solution)/shard_map/all_to_all | solution.py:19
  187.5 0.2 reshape.275
  187.7 0.3 copy.88
  188.2 0.3 reshape.273
  188.5 0.3 fusion.23
  188.9 0.8 fusion.77
  189.8 2.4 %fusion.10 = f32[32,768]{1,0:T(8,128)S(1)} fusion(bf16[3,768,1536]{2,1,0:T(8,128)(2,1)} %all-gather.4.cloned.1.call-done, bf16[4,8,12,128]{3,2,1,0:T(8,128)(2,1)S(1)} %bitcast.125), kind=kOutput, calls=%fused_computation.23 | convolution fusion | flops 75522048 | bytes 2555904 | tf_op jit(solution)/shard_map/dot_general | solution.py:13
  192.2 3.9 %convolution_convert_fusion.2 = bf16[32,1536]{1,0:T(8,128)(2,1)S(1)} fusion(bf16[3,768,1536]{2,1,0:T(8,128)(2,1)} %all-gather.4.cloned.1.call-done, f32[32,768]{1,0:T(8,128)S(1)} %fusion.10, bf16[4,8,12,128]{3,2,1,0:T(8,128)(2,1)S(1)} %bitcast.126), kind=kOutput, calls=%fused_computation.12 | convolution fusion | flops 151093248 | bytes 5013504 | tf_op jit(solution)/shard_map/dot_general | solution.py:48
  196.1 0.7 reshape.270
  196.9 4.7 %all-to-all-start.7 = ((bf16[32,12,128]{2,1,0:T(8,128)(2,1)}), bf16[32,12,128]{2,1,0:T(8,128)(2,1)S(1)}, u32[]{:S(2)}, u32[]{:S(2)}) async-start(bf16[32,12,128]{2,1,0:T(8,128)(2,1)} %reshape.270), calls=%async_computation.7 | async-start | bytes 262144 | tf_op jit(solution)/shard_map/all_to_all | solution.py:19
  201.6 1.1 fusion.3
  202.7 8.5 %all-to-all-done.7 = bf16[32,12,128]{2,1,0:T(8,128)(2,1)S(1)} async-done(((bf16[32,12,128]{2,1,0:T(8,128)(2,1)}), bf16[32,12,128]{2,1,0:T(8,128)(2,1)S(1)}, u32[]{:S(2)}, u32[]{:S(2)}) %all-to-all-start.7) | async-done | bytes 98336 | tf_op jit(solution)/shard_map/all_to_all | solution.py:19
  211.3 0.6 fusion.76
  (94 shorter events, 3.1 us)
Async XLA Ops:
  7.2 128.3 %copy-start = (bf16[1536,48]{0,1:T(8,128)(2,1)S(1)}, bf16[1536,48]{0,1:T(8,128)(2,1)}, u32[]{:S(2)}) copy-start(bf16[1536,48]{0,1:T(8,128)(2,1)} %param.24) | copy-start | bytes 442372
  7.2 5.2 %copy-start.4 = (bf16[1,48,1536]{2,1,0:T(8,128)(2,1)S(1)}, bf16[1,48,1536]{2,1,0:T(8,128)(2,1)}, u32[]{:S(2)}) copy-start(bf16[1,48,1536]{2,1,0:T(8,128)(2,1)} %param.29) | copy-start | bytes 442372
  7.2 5.2 %copy-start.3 = (bf16[1,48,1536]{2,1,0:T(8,128)(2,1)S(1)}, bf16[1,48,1536]{2,1,0:T(8,128)(2,1)}, u32[]{:S(2)}) copy-start(bf16[1,48,1536]{2,1,0:T(8,128)(2,1)} %param.30) | copy-start | bytes 442372
  7.2 5.2 %copy-start.2 = (bf16[1,48,1536]{2,1,0:T(8,128)(2,1)S(1)}, bf16[1,48,1536]{2,1,0:T(8,128)(2,1)}, u32[]{:S(2)}) copy-start(bf16[1,48,1536]{2,1,0:T(8,128)(2,1)} %param.31) | copy-start | bytes 442372
  7.2 94.4 %all-gather.4.cloned.1.call-start = ((), (), s32[]{:S(2)}) async-start(), calls=%async_computation.8 | async-start | bytes 7520256 | tf_op jit(solution)/shard_map/all_gather | solution.py:108
  10.6 2.7 %copy-start.8 = (bf16[1,1536]{1,0:T(2,128)(2,1)S(1)}, bf16[1,1536]{1,0:T(2,128)(2,1)}, u32[]{:S(2)}) copy-start(bf16[1,1536]{1,0:T(2,128)(2,1)} %param.16) | copy-start | bytes 9220
  10.6 2.7 %copy-start.10 = (bf16[1,512]{1,0:T(2,128)(2,1)S(1)}, bf16[1,512]{1,0:T(2,128)(2,1)}, u32[]{:S(2)}) copy-start(bf16[1,512]{1,0:T(2,128)(2,1)} %param.17) | copy-start | bytes 3076
  13.3 46.1 %copy-start.13 = (s32[512]{0:T(512)S(1)}, s32[512]{0:T(512)}, u32[]{:S(2)}) copy-start(s32[512]{0:T(512)} %param.19) | copy-start | bytes 6148
  13.3 48.6 %all-to-all-start = ((bf16[32,16,1536]{2,1,0:T(8,128)(2,1)}), bf16[32,16,1536]{2,1,0:T(8,128)(2,1)S(1)}, u32[]{:S(2)}, u32[]{:S(2)}) async-start(bf16[32,16,1536]{2,1,0:T(8,128)(2,1)} %bitcast.3), calls=%async_computation | async-start | bytes 3145728 | tf_op jit(solution)/shard_map/all_to_all | solution.py:19
  23.5 61.5 %copy-start.11 = (s32[32]{0:T(128)S(1)}, s32[32]{0:T(128)}, u32[]{:S(2)}) copy-start(s32[32]{0:T(128)} %param.20) | copy-start | bytes 388
  23.5 61.5 %copy-start.12 = (s32[32]{0:T(128)S(1)}, s32[32]{0:T(128)}, u32[]{:S(2)}) copy-start(s32[32]{0:T(128)} %param.21) | copy-start | bytes 388
  23.5 61.7 %copy-start.9 = (bf16[1,1536]{1,0:T(2,128)(2,1)S(1)}, bf16[1,1536]{1,0:T(2,128)(2,1)}, u32[]{:S(2)}) copy-start(bf16[1,1536]{1,0:T(2,128)(2,1)} %param.18) | copy-start | bytes 9220
  61.9 18.9 %all-to-all-start.1 = ((bf16[8,32,512]{2,1,0:T(8,128)(2,1)}), bf16[8,32,512]{2,1,0:T(8,128)(2,1)S(1)}, u32[]{:S(2)}, u32[]{:S(2)}) async-start(bf16[8,32,512]{2,1,0:T(8,128)(2,1)} %bitcast.4), calls=%async_computation.1 | async-start | bytes 524288 | tf_op jit(solution)/shard_map/all_to_all | solution.py:19
  81.7 9.3 %all-to-all-start.2 = ((bf16[4,32,512]{2,1,0:T(8,128)(2,1)}), bf16[4,32,512]{2,1,0:T(8,128)(2,1)S(1)}, u32[]{:S(2)}, u32[]{:S(2)}) async-start(bf16[4,32,512]{2,1,0:T(8,128)(2,1)} %bitcast.6), calls=%async_computation.2 | async-start | bytes 262144 | tf_op jit(solution)/shard_map/all_to_all | solution.py:19
  96.6 14.6 %all-to-all-start.3 = ((bf16[32,16,128]{2,1,0:T(8,128)(2,1)}), bf16[32,16,128]{2,1,0:T(8,128)(2,1)S(1)}, u32[]{:S(2)}, u32[]{:S(2)}) async-start(bf16[32,16,128]{2,1,0:T(8,128)(2,1)} %copy.86), calls=%async_computation.3 | async-start | bytes 262144 | tf_op jit(solution)/shard_map/all_to_all | solution.py:19
  112.4 15.0 %all-to-all-start.4 = ((bf16[32,24,128]{2,1,0:T(8,128)(2,1)}), bf16[32,24,128]{2,1,0:T(8,128)(2,1)S(1)}, u32[]{:S(2)}, u32[]{:S(2)}) async-start(bf16[32,24,128]{2,1,0:T(8,128)(2,1)} %broadcast_in_dim.147), calls=%async_computation.4 | async-start | bytes 393216 | tf_op jit(solution)/shard_map/all_to_all | solution.py:19
  127.4 7.0 %copy-start.7 = (f32[64,4]{0,1:T(4,128)S(1)}, f32[64,4]{0,1:T(4,128)}, u32[]{:S(2)}) copy-start(f32[64,4]{0,1:T(4,128)} %param.27) | copy-start | bytes 3076
  127.4 7.0 %copy-start.6 = (s32[64,4]{0,1:T(4,128)S(1)}, s32[64,4]{0,1:T(4,128)}, u32[]{:S(2)}) copy-start(s32[64,4]{0,1:T(4,128)} %param.26) | copy-start | bytes 3076
  127.4 43.2 %all-to-all-start.5 = ((bf16[32,16,1536]{2,1,0:T(8,128)(2,1)}), bf16[32,16,1536]{2,1,0:T(8,128)(2,1)S(1)}, u32[]{:S(2)}, u32[]{:S(2)}) async-start(bf16[32,16,1536]{2,1,0:T(8,128)(2,1)} %bitcast.115), calls=%async_computation.5 | async-start | bytes 3145728 | tf_op jit(solution)/shard_map/all_to_all | solution.py:19
  171.5 16.0 %all-to-all-start.6 = ((bf16[32,12,128]{2,1,0:T(8,128)(2,1)}), bf16[32,12,128]{2,1,0:T(8,128)(2,1)S(1)}, u32[]{:S(2)}, u32[]{:S(2)}) async-start(bf16[32,12,128]{2,1,0:T(8,128)(2,1)} %broadcast_in_dim.151), calls=%async_computation.6 | async-start | bytes 262144 | tf_op jit(solution)/shard_map/all_to_all | solution.py:19
  187.7 1.1 copy-start.5
  192.2 9.4 %copy-start.1 = (bf16[63,1536]{1,0:T(8,128)(2,1)S(1)}, bf16[63,1536]{1,0:T(8,128)(2,1)}, u32[]{:S(2)}) copy-start(bf16[63,1536]{1,0:T(8,128)(2,1)} %param.25) | copy-start | bytes 580612
  196.9 14.3 %all-to-all-start.7 = ((bf16[32,12,128]{2,1,0:T(8,128)(2,1)}), bf16[32,12,128]{2,1,0:T(8,128)(2,1)S(1)}, u32[]{:S(2)}, u32[]{:S(2)}) async-start(bf16[32,12,128]{2,1,0:T(8,128)(2,1)} %reshape.270), calls=%async_computation.7 | async-start | bytes 262144 | tf_op jit(solution)/shard_map/all_to_all | solution.py:19
Sparse Core Ops, SparseCore 0:
  13.4 58.0 all-gather.3

commit v11 on v10

--- a/solution.py
+++ b/solution.py
@@ -190,6 +190,7 @@
     packed = swap(jnp.broadcast_to(packed[None], (tp_size,) + packed.shape), TP)
     proj_home = packed.reshape(tp_size, group_reqs, width // tp_size)
     proj_home = jnp.transpose(proj_home, (1, 0, 2)).reshape(group_reqs, width)
+    proj_home = lax.optimization_barrier(proj_home)
     hidden_all = (resid_rows.astype(F32) + proj_home.astype(F32)).astype(BF16)
     own_row = lax.dynamic_slice_in_dim(hidden_all, tp_lane, 1)
 

time: 220 us -> 217 us (0.986)
  no operation moved by 1% of the time
where the time goes in v11:
time: 217 us; the launch traced here: 216 us
  waiting for transfers between devices  58.8 us (27%)
  blocking collectives  56 us (26%)
  starting transfers between devices  49.3 us (23%)
  matrix products  26.8 us (12%)
  between operations  14.6 us (7%)
  other arithmetic  6.01 us (3%)
  local copies, waits for them, and re-layouts  4.88 us (2%)
    all_to_all x8, waiting for transfers between devices, swap(): lax.all_to_all(blocks, axis_name, split_axis=0, concat_axis=0, tiled=True)  58.7 us
    all_to_all x8, starting transfers between devices, swap(): lax.all_to_all(blocks, axis_name, split_axis=0, concat_axis=0, tiled=True)  49.3 us
    all_gather x1, blocking collectives, on_device(): all_rows = lax.all_gather(line_share, 'dp', axis=0, tiled=True)  23.4 us
    all_gather x1, blocking collectives, on_device(): all_projected = lax.all_gather(projected, 'dp', axis=0, tiled=True)  20.2 us
    all_gather x1, blocking collectives, on_device(): line_fresh = lax.all_gather(fresh, 'x', axis=0, tiled=True)  12.4 us
    dot_general x2, matrix products, expert_units(): return jnp.dot(active, units[2], preferred_element_type=F32).astype(BF16)  11.1 us
    dot_general x2, matrix products, contract_rows(): lax.dot_general(left_rows, unit_rows, (((1,), (1,)), ((), ())), preferred...  6.75 us
  transfers between devices with their start and end apart: 9, of which 8 were waited for; matrix products, arithmetic and copies ran while one was open for 10% of the time, Pallas kernels for 0%

profile of v11, /device:TPU:8, one launch (start us, length us, event | category | flops | bytes accessed | tf_op | source)
XLA Modules:
  0.0 216.4 jit_solution(434798193457296705)
XLA Ops:
  7.3 0.8 iota_compare_fusion.1
  8.3 1.1 fusion.20
  9.4 1.1 fusion.22
  10.5 0.1 fusion.32
  10.6 1.8 convolution_convert_fusion.1
  12.4 0.8 pad_maximum_fusion
  13.3 10.2 %all-to-all-start = ((bf16[32,16,1536]{2,1,0:T(8,128)(2,1)}), bf16[32,16,1536]{2,1,0:T(8,128)(2,1)S(1)}, u32[]{:S(2)}, u32[]{:S(2)}) async-start(bf16[32,16,1536]{2,1,0:T(8,128)(2,1)} %bitcast.3), calls=%async_computation | async-start | bytes 3145728 | tf_op jit(solution)/shard_map/all_to_all | solution.py:19
  23.6 12.4 %all-gather = bf16[4,1,2048]{2,1,0:T(2,128)(2,1)S(1)} all-gather(bf16[1,1,2048]{2,1,0:T(2,128)(2,1)S(1)} %bitcast.119), channel_id=1, replica_groups=mesh['dp'=16,'y'=8,'x'=4] {'x'}, dimensions={0}, use_global_device_ids=true | all-gather | bytes 20480 | tf_op jit(solution)/shard_map/all_gather | solution.py:116
  36.0 23.4 %all-gather.1 = bf16[16,4,512]{2,1,0:T(4,128)(2,1)S(1)} all-gather(bf16[1,4,512]{2,1,0:T(4,128)(2,1)S(1)} %bitcast.121), channel_id=1, replica_groups=mesh['dp'=16,'y'=8,'x'=4] {'dp'}, dimensions={0}, use_global_device_ids=true | all-gather | bytes 69632 | tf_op jit(solution)/shard_map/all_gather | solution.py:118
  59.8 1.0 convolution_convert_fusion.3
  60.8 1.1 all-to-all-done
  61.9 8.0 %all-to-all-start.1 = ((bf16[8,32,512]{2,1,0:T(8,128)(2,1)}), bf16[8,32,512]{2,1,0:T(8,128)(2,1)S(1)}, u32[]{:S(2)}, u32[]{:S(2)}) async-start(bf16[8,32,512]{2,1,0:T(8,128)(2,1)} %bitcast.4), calls=%async_computation.1 | async-start | bytes 524288 | tf_op jit(solution)/shard_map/all_to_all | solution.py:19
  69.9 10.9 %all-to-all-done.1 = bf16[8,32,512]{2,1,0:T(8,128)(2,1)S(1)} async-done(((bf16[8,32,512]{2,1,0:T(8,128)(2,1)}), bf16[8,32,512]{2,1,0:T(8,128)(2,1)S(1)}, u32[]{:S(2)}, u32[]{:S(2)}) %all-to-all-start.1) | async-done | bytes 262176 | tf_op jit(solution)/shard_map/all_to_all | solution.py:19
  80.8 0.9 convolution_convert_fusion.4
  81.7 3.3 %all-to-all-start.2 = ((bf16[4,32,512]{2,1,0:T(8,128)(2,1)}), bf16[4,32,512]{2,1,0:T(8,128)(2,1)S(1)}, u32[]{:S(2)}, u32[]{:S(2)}) async-start(bf16[4,32,512]{2,1,0:T(8,128)(2,1)} %bitcast.6), calls=%async_computation.2 | async-start | bytes 262144 | tf_op jit(solution)/shard_map/all_to_all | solution.py:19
  85.3 5.7 %all-to-all-done.2 = bf16[4,32,512]{2,1,0:T(8,128)(2,1)S(1)} async-done(((bf16[4,32,512]{2,1,0:T(8,128)(2,1)}), bf16[4,32,512]{2,1,0:T(8,128)(2,1)S(1)}, u32[]{:S(2)}, u32[]{:S(2)}) %all-to-all-start.2) | async-done | bytes 131104 | tf_op jit(solution)/shard_map/all_to_all | solution.py:19
  91.1 1.1 fusion.83
  92.3 0.3 reduce-precision_convert_fusion
  92.6 1.7 fusion.12
  94.9 0.7 copy.83
  95.6 5.0 %all-to-all-start.3 = ((bf16[32,16,128]{2,1,0:T(8,128)(2,1)}), bf16[32,16,128]{2,1,0:T(8,128)(2,1)S(1)}, u32[]{:S(2)}, u32[]{:S(2)}) async-start(bf16[32,16,128]{2,1,0:T(8,128)(2,1)} %copy.83), calls=%async_computation.3 | async-start | bytes 262144 | tf_op jit(solution)/shard_map/all_to_all | solution.py:19
  100.6 4.3 %fusion.5 = f32[512,768]{1,0:T(8,128)} fusion(bf16[512,1536]{1,0:T(8,128)(2,1)S(1)} %bitcast.106, bf16[3,768,1536]{2,1,0:T(8,128)(2,1)} %all-gather.4.cloned.1.call-done), kind=kOutput, calls=%fused_computation.14 | convolution fusion | flops 1207959552 | bytes 5505024 | tf_op jit(solution)/shard_map/dot_general | solution.py:13
  104.9 5.3 %all-to-all-done.3 = bf16[32,16,128]{2,1,0:T(8,128)(2,1)S(1)} async-done(((bf16[32,16,128]{2,1,0:T(8,128)(2,1)}), bf16[32,16,128]{2,1,0:T(8,128)(2,1)S(1)}, u32[]{:S(2)}, u32[]{:S(2)}) %all-to-all-start.3) | async-done | bytes 131104 | tf_op jit(solution)/shard_map/all_to_all | solution.py:19
  110.7 0.7 broadcast_in_dim.147
  111.4 4.7 %all-to-all-start.4 = ((bf16[32,24,128]{2,1,0:T(8,128)(2,1)}), bf16[32,24,128]{2,1,0:T(8,128)(2,1)S(1)}, u32[]{:S(2)}, u32[]{:S(2)}) async-start(bf16[32,24,128]{2,1,0:T(8,128)(2,1)} %broadcast_in_dim.147), calls=%async_computation.4 | async-start | bytes 393216 | tf_op jit(solution)/shard_map/all_to_all | solution.py:19
  116.1 7.2 %convolution_convert_fusion = bf16[512,1536]{1,0:T(8,128)(2,1)} fusion(bf16[3,768,1536]{2,1,0:T(8,128)(2,1)} %all-gather.4.cloned.1.call-done, f32[512,768]{1,0:T(8,128)} %fusion.5, bf16[512,1536]{1,0:T(8,128)(2,1)S(1)} %bitcast.107), kind=kOutput, calls=%fused_computation | convolution fusion | flops 2417885184 | bytes 9437184 | tf_op jit(solution)/shard_map/dot_general | solution.py:48
  123.4 3.1 %all-to-all-done.4 = bf16[32,24,128]{2,1,0:T(8,128)(2,1)S(1)} async-done(((bf16[32,24,128]{2,1,0:T(8,128)(2,1)}), bf16[32,24,128]{2,1,0:T(8,128)(2,1)S(1)}, u32[]{:S(2)}, u32[]{:S(2)}) %all-to-all-start.4) | async-done | bytes 196640 | tf_op jit(solution)/shard_map/all_to_all | solution.py:19
  126.4 6.9 %all-to-all-start.5 = ((bf16[32,16,1536]{2,1,0:T(8,128)(2,1)}), bf16[32,16,1536]{2,1,0:T(8,128)(2,1)S(1)}, u32[]{:S(2)}, u32[]{:S(2)}) async-start(bf16[32,16,1536]{2,1,0:T(8,128)(2,1)} %bitcast.20), calls=%async_computation.5 | async-start | bytes 3145728 | tf_op jit(solution)/shard_map/all_to_all | solution.py:19
  133.5 0.2 slice_reduce_fusion.1
  133.7 0.1 convolution_convert_fusion.7
  133.9 20.2 %all_gather.15 = bf16[512,48]{1,0:T(8,128)(2,1)S(1)} all-gather(bf16[32,48]{1,0:T(8,128)(2,1)S(1)} %convolution_convert_fusion.7), channel_id=1, replica_groups=mesh['dp'=16,'y'=8,'x'=4] {'dp'}, dimensions={0}, use_global_device_ids=true | all-gather | bytes 52224 | tf_op jit(solution)/shard_map/all_gather | solution.py:185
  154.0 0.2 convolution_convert_fusion.6
  154.2 15.4 %all-to-all-done.5 = bf16[32,16,1536]{2,1,0:T(8,128)(2,1)S(1)} async-done(((bf16[32,16,1536]{2,1,0:T(8,128)(2,1)}), bf16[32,16,1536]{2,1,0:T(8,128)(2,1)S(1)}, u32[]{:S(2)}, u32[]{:S(2)}) %all-to-all-start.5) | async-done | bytes 1572896 | tf_op jit(solution)/shard_map/all_to_all | solution.py:19
  169.7 0.7 broadcast_in_dim.151
  170.4 6.5 %all-to-all-start.6 = ((bf16[32,12,128]{2,1,0:T(8,128)(2,1)}), bf16[32,12,128]{2,1,0:T(8,128)(2,1)S(1)}, u32[]{:S(2)}, u32[]{:S(2)}) async-start(bf16[32,12,128]{2,1,0:T(8,128)(2,1)} %broadcast_in_dim.151), calls=%async_computation.6 | async-start | bytes 262144 | tf_op jit(solution)/shard_map/all_to_all | solution.py:19
  176.9 0.4 convolution_bitcast_fusion.2
  177.3 0.4 fusion.2
  177.8 8.7 %all-to-all-done.6 = bf16[32,12,128]{2,1,0:T(8,128)(2,1)S(1)} async-done(((bf16[32,12,128]{2,1,0:T(8,128)(2,1)}), bf16[32,12,128]{2,1,0:T(8,128)(2,1)S(1)}, u32[]{:S(2)}, u32[]{:S(2)}) %all-to-all-start.6) | async-done | bytes 98336 | tf_op jit(solution)/shard_map/all_to_all | solution.py:19
  186.4 0.2 reshape.243
  186.8 0.3 reshape.244
  187.1 0.2 fusion.33
  187.4 2.4 %fusion.10 = f32[32,768]{1,0:T(8,128)S(1)} fusion(bf16[3,768,1536]{2,1,0:T(8,128)(2,1)} %all-gather.4.cloned.1.call-done, bf16[32,1536]{1,0:T(8,128)(2,1)S(1)} %get-tuple-element.35, f32[1536]{0:T(1024)S(1)} %copy-done.5, f32[32]{0:T(128)S(1)} %add_rsqrt_fusion), kind=kOutput, calls=%fused_computation.23 | convolution fusion | flops 75718656 | bytes 2562176 | tf_op jit(solution)/shard_map/dot_general | solution.py:13
  189.8 3.9 %convolution_convert_fusion.2 = bf16[32,1536]{1,0:T(8,128)(2,1)S(1)} fusion(bf16[3,768,1536]{2,1,0:T(8,128)(2,1)} %all-gather.4.cloned.1.call-done, f32[32,768]{1,0:T(8,128)S(1)} %fusion.10, bf16[32,1536]{1,0:T(8,128)(2,1)S(1)} %get-tuple-element.35, f32[1536]{0:T(1024)S(1)} %copy-done.5, f32[32]{0:T(128)S(1)} %add_rsqrt_fusion), kind=kOutput, calls=%fused_computation.12 | convolution fusion | flops 151289856 | bytes 5019776 | tf_op jit(solution)/shard_map/dot_general | solution.py:48
  193.8 0.8 reshape.245
  194.5 4.7 %all-to-all-start.7 = ((bf16[32,12,128]{2,1,0:T(8,128)(2,1)}), bf16[32,12,128]{2,1,0:T(8,128)(2,1)S(1)}, u32[]{:S(2)}, u32[]{:S(2)}) async-start(bf16[32,12,128]{2,1,0:T(8,128)(2,1)} %reshape.245), calls=%async_computation.7 | async-start | bytes 262144 | tf_op jit(solution)/shard_map/all_to_all | solution.py:19
  199.2 1.1 fusion.3
  200.3 8.5 %all-to-all-done.7 = bf16[32,12,128]{2,1,0:T(8,128)(2,1)S(1)} async-done(((bf16[32,12,128]{2,1,0:T(8,128)(2,1)}), bf16[32,12,128]{2,1,0:T(8,128)(2,1)S(1)}, u32[]{:S(2)}, u32[]{:S(2)}) %all-to-all-start.7) | async-done | bytes 98336 | tf_op jit(solution)/shard_map/all_to_all | solution.py:19
  208.9 0.6 fusion.74
  (93 shorter events, 2.5 us)
Async XLA Ops:
  7.2 126.5 %copy-start = (bf16[1536,48]{0,1:T(8,128)(2,1)S(1)}, bf16[1536,48]{0,1:T(8,128)(2,1)}, u32[]{:S(2)}) copy-start(bf16[1536,48]{0,1:T(8,128)(2,1)} %param.24) | copy-start | bytes 442372
  7.2 5.2 %copy-start.4 = (bf16[1,48,1536]{2,1,0:T(8,128)(2,1)S(1)}, bf16[1,48,1536]{2,1,0:T(8,128)(2,1)}, u32[]{:S(2)}) copy-start(bf16[1,48,1536]{2,1,0:T(8,128)(2,1)} %param.29) | copy-start | bytes 442372
  7.2 5.2 %copy-start.3 = (bf16[1,48,1536]{2,1,0:T(8,128)(2,1)S(1)}, bf16[1,48,1536]{2,1,0:T(8,128)(2,1)}, u32[]{:S(2)}) copy-start(bf16[1,48,1536]{2,1,0:T(8,128)(2,1)} %param.30) | copy-start | bytes 442372
  7.2 5.2 %copy-start.2 = (bf16[1,48,1536]{2,1,0:T(8,128)(2,1)S(1)}, bf16[1,48,1536]{2,1,0:T(8,128)(2,1)}, u32[]{:S(2)}) copy-start(bf16[1,48,1536]{2,1,0:T(8,128)(2,1)} %param.31) | copy-start | bytes 442372
  7.2 93.4 %all-gather.4.cloned.1.call-start = ((), (), s32[]{:S(2)}) async-start(), calls=%async_computation.8 | async-start | bytes 7520256 | tf_op jit(solution)/shard_map/all_gather | solution.py:108
  10.6 2.7 %copy-start.8 = (bf16[1,1536]{1,0:T(2,128)(2,1)S(1)}, bf16[1,1536]{1,0:T(2,128)(2,1)}, u32[]{:S(2)}) copy-start(bf16[1,1536]{1,0:T(2,128)(2,1)} %param.16) | copy-start | bytes 9220
  10.6 2.7 %copy-start.10 = (bf16[1,512]{1,0:T(2,128)(2,1)S(1)}, bf16[1,512]{1,0:T(2,128)(2,1)}, u32[]{:S(2)}) copy-start(bf16[1,512]{1,0:T(2,128)(2,1)} %param.17) | copy-start | bytes 3076
  13.3 46.1 %copy-start.14 = (s32[512]{0:T(512)S(1)}, s32[512]{0:T(512)}, u32[]{:S(2)}) copy-start(s32[512]{0:T(512)} %param.19) | copy-start | bytes 6148
  13.3 48.6 %all-to-all-start = ((bf16[32,16,1536]{2,1,0:T(8,128)(2,1)}), bf16[32,16,1536]{2,1,0:T(8,128)(2,1)S(1)}, u32[]{:S(2)}, u32[]{:S(2)}) async-start(bf16[32,16,1536]{2,1,0:T(8,128)(2,1)} %bitcast.3), calls=%async_computation | async-start | bytes 3145728 | tf_op jit(solution)/shard_map/all_to_all | solution.py:19
  23.5 61.5 %copy-start.11 = (s32[32]{0:T(128)S(1)}, s32[32]{0:T(128)}, u32[]{:S(2)}) copy-start(s32[32]{0:T(128)} %param.20) | copy-start | bytes 388
  23.5 61.5 %copy-start.12 = (s32[32]{0:T(128)S(1)}, s32[32]{0:T(128)}, u32[]{:S(2)}) copy-start(s32[32]{0:T(128)} %param.21) | copy-start | bytes 388
  23.5 61.7 %copy-start.9 = (bf16[1,1536]{1,0:T(2,128)(2,1)S(1)}, bf16[1,1536]{1,0:T(2,128)(2,1)}, u32[]{:S(2)}) copy-start(bf16[1,1536]{1,0:T(2,128)(2,1)} %param.18) | copy-start | bytes 9220
  23.6 67.5 %copy-start.13 = (bf16[32,2,64,128]{3,2,1,0:T(8,128)(2,1)S(1)}, bf16[32,2,64,128]{3,2,1,0:T(8,128)(2,1)}, u32[]{:S(2)}) copy-start(bf16[32,2,64,128]{3,2,1,0:T(8,128)(2,1)} %param.22) | copy-start | bytes 3145732
  61.9 18.9 %all-to-all-start.1 = ((bf16[8,32,512]{2,1,0:T(8,128)(2,1)}), bf16[8,32,512]{2,1,0:T(8,128)(2,1)S(1)}, u32[]{:S(2)}, u32[]{:S(2)}) async-start(bf16[8,32,512]{2,1,0:T(8,128)(2,1)} %bitcast.4), calls=%async_computation.1 | async-start | bytes 524288 | tf_op jit(solution)/shard_map/all_to_all | solution.py:19
  81.7 9.3 %all-to-all-start.2 = ((bf16[4,32,512]{2,1,0:T(8,128)(2,1)}), bf16[4,32,512]{2,1,0:T(8,128)(2,1)S(1)}, u32[]{:S(2)}, u32[]{:S(2)}) async-start(bf16[4,32,512]{2,1,0:T(8,128)(2,1)} %bitcast.6), calls=%async_computation.2 | async-start | bytes 262144 | tf_op jit(solution)/shard_map/all_to_all | solution.py:19
  95.6 14.6 %all-to-all-start.3 = ((bf16[32,16,128]{2,1,0:T(8,128)(2,1)}), bf16[32,16,128]{2,1,0:T(8,128)(2,1)S(1)}, u32[]{:S(2)}, u32[]{:S(2)}) async-start(bf16[32,16,128]{2,1,0:T(8,128)(2,1)} %copy.83), calls=%async_computation.3 | async-start | bytes 262144 | tf_op jit(solution)/shard_map/all_to_all | solution.py:19
  111.4 15.0 %all-to-all-start.4 = ((bf16[32,24,128]{2,1,0:T(8,128)(2,1)}), bf16[32,24,128]{2,1,0:T(8,128)(2,1)S(1)}, u32[]{:S(2)}, u32[]{:S(2)}) async-start(bf16[32,24,128]{2,1,0:T(8,128)(2,1)} %broadcast_in_dim.147), calls=%async_computation.4 | async-start | bytes 393216 | tf_op jit(solution)/shard_map/all_to_all | solution.py:19
  126.4 7.0 %copy-start.7 = (f32[64,4]{0,1:T(4,128)S(1)}, f32[64,4]{0,1:T(4,128)}, u32[]{:S(2)}) copy-start(f32[64,4]{0,1:T(4,128)} %param.27) | copy-start | bytes 3076
  126.4 7.0 %copy-start.6 = (s32[64,4]{0,1:T(4,128)S(1)}, s32[64,4]{0,1:T(4,128)}, u32[]{:S(2)}) copy-start(s32[64,4]{0,1:T(4,128)} %param.26) | copy-start | bytes 3076
  126.4 43.2 %all-to-all-start.5 = ((bf16[32,16,1536]{2,1,0:T(8,128)(2,1)}), bf16[32,16,1536]{2,1,0:T(8,128)(2,1)S(1)}, u32[]{:S(2)}, u32[]{:S(2)}) async-start(bf16[32,16,1536]{2,1,0:T(8,128)(2,1)} %bitcast.20), calls=%async_computation.5 | async-start | bytes 3145728 | tf_op jit(solution)/shard_map/all_to_all | solution.py:19
  170.4 16.0 %all-to-all-start.6 = ((bf16[32,12,128]{2,1,0:T(8,128)(2,1)}), bf16[32,12,128]{2,1,0:T(8,128)(2,1)S(1)}, u32[]{:S(2)}, u32[]{:S(2)}) async-start(bf16[32,12,128]{2,1,0:T(8,128)(2,1)} %broadcast_in_dim.151), calls=%async_computation.6 | async-start | bytes 262144 | tf_op jit(solution)/shard_map/all_to_all | solution.py:19
  177.3 10.0 %copy-start.5 = (f32[1536]{0:T(1024)S(1)}, f32[1536]{0:T(1024)}, u32[]{:S(2)}) copy-start(f32[1536]{0:T(1024)} %param.28) | copy-start | bytes 18436
  189.8 9.4 %copy-start.1 = (bf16[63,1536]{1,0:T(8,128)(2,1)S(1)}, bf16[63,1536]{1,0:T(8,128)(2,1)}, u32[]{:S(2)}) copy-start(bf16[63,1536]{1,0:T(8,128)(2,1)} %param.25) | copy-start | bytes 580612
  194.5 14.3 %all-to-all-start.7 = ((bf16[32,12,128]{2,1,0:T(8,128)(2,1)}), bf16[32,12,128]{2,1,0:T(8,128)(2,1)S(1)}, u32[]{:S(2)}, u32[]{:S(2)}) async-start(bf16[32,12,128]{2,1,0:T(8,128)(2,1)} %reshape.245), calls=%async_computation.7 | async-start | bytes 262144 | tf_op jit(solution)/shard_map/all_to_all | solution.py:19
Sparse Core Ops, SparseCore 0:
  13.4 58.0 all-gather.3
